TPU v7x, 256 devices: a whole 4x4x8 slice. The times are simulated.
256 devices in a mesh: dp: 8 (over z), mp: 32 (over y, x, core).
Axes of the slice: x: 4, y: 4, z: 8, core: 2. Of those that a mesh axis runs over, the one named last changes fastest.
Arguments:
- tokens: bfloat16 [16384, 16384], P('dp', 'mp'), may hold values from -6 to 6
- inner_one: bfloat16 [128, 128, 128], P('mp'), may hold values from -0.5 to 0.5
- outer_one: bfloat16 [128, 128, 128], P('mp'), may hold values from -0.5 to 0.5
- inner_two: bfloat16 [128, 128, 128], P('mp'), may hold values from -0.5 to 0.5
- outer_two: bfloat16 [128, 128, 128], P('mp'), may hold values from -0.5 to 0.5
- cotangent: bfloat16 [16384, 16384], P('dp', 'mp'), may hold values from -6 to 6
Outputs:
- output: bfloat16 [16384, 16384], P('dp', 'mp')
- input_grad: bfloat16 [16384, 16384], P('dp', 'mp')
- inner_one_grad: float32 [128, 128, 128], P('mp', 'dp')
- outer_one_grad: float32 [128, 128, 128], P('mp', 'dp')
- inner_two_grad: float32 [128, 128, 128], P('mp', 'dp')
- outer_two_grad: float32 [128, 128, 128], P('mp', 'dp')
All inputs are finite; a program needn't handle non-finite values.
Results may differ from a plain program's by a relative error of at most 0.0069.
Values may be sent and summed in bfloat16 or wider, within the bound.
No kernel may reach another device: no remote copies, remote signals or barrier semaphores. Data moves between devices by JAX's collectives and lax.ppermute only.
A program may use at most 128 MiB of HBM per device.

v0:
```python
import jax
import jax.numpy as jnp
from jax import lax
from jax.sharding import PartitionSpec as P


def gelu_tanh(values):
    return jax.nn.gelu(values, approximate=True)


def product(form, left, right):
    return jnp.einsum(form, left, right, preferred_element_type=jnp.float32)


def return_second(grads, outer_two):
    grad_perm_two = product("tjl,jbl->jbt", grads, outer_two).astype(jnp.bfloat16)
    return lax.all_to_all(grad_perm_two, "mp", split_axis=1, concat_axis=0, tiled=True)


def body(tokens, inner_one, outer_one, inner_two, outer_two, cotangent):
    tok_rows = tokens.shape[0]
    local_blocks = inner_one.shape[0]
    block_size = inner_one.shape[1]
    inputs = tokens.reshape(tok_rows, local_blocks, block_size)
    grads = cotangent.reshape(tok_rows, local_blocks, block_size)
    first_mid = product("tbk,bkj->jbt", inputs, inner_one).astype(jnp.bfloat16)
    first_perm = lax.all_to_all(first_mid, "mp", split_axis=0, concat_axis=1, tiled=True)
    pre_act = product("jbt,jbl->tjl", first_perm, outer_one)
    hidden = gelu_tanh(pre_act).astype(jnp.bfloat16)
    second_mid = product("tbk,bkj->jbt", hidden, inner_two).astype(jnp.bfloat16)
    second_perm = lax.all_to_all(second_mid, "mp", split_axis=0, concat_axis=1, tiled=True)
    output = product("jbt,jbl->tjl", second_perm, outer_two).astype(jnp.bfloat16)
    outer_two_grad = product("jbt,tjl->jbl", second_perm, grads)
    outer_two_grad = lax.psum_scatter(outer_two_grad, "dp", scatter_dimension=1, tiled=True)
    grad_mid_two = return_second(grads, outer_two)
    grad_hidden = product("jbt,bkj->tbk", grad_mid_two, inner_two)
    inner_two_grad = product("tbk,jbt->bkj", hidden, grad_mid_two)
    inner_two_grad = lax.psum_scatter(inner_two_grad, "dp", scatter_dimension=1, tiled=True)
    primal_out, pullback = jax.vjp(gelu_tanh, pre_act)
    grad_pre = pullback(grad_hidden)[0].astype(jnp.bfloat16)
    grad_perm_one = product("tjl,jbl->jbt", grad_pre, outer_one).astype(jnp.bfloat16)
    outer_one_grad = product("jbt,tjl->jbl", first_perm, grad_pre)
    outer_one_grad = lax.psum_scatter(outer_one_grad, "dp", scatter_dimension=1, tiled=True)
    grad_mid_one = lax.all_to_all(grad_perm_one, "mp", split_axis=1, concat_axis=0, tiled=True)
    input_grad = product("jbt,bkj->tbk", grad_mid_one, inner_one).astype(jnp.bfloat16)
    inner_one_grad = product("tbk,jbt->bkj", inputs, grad_mid_one)
    inner_one_grad = lax.psum_scatter(inner_one_grad, "dp", scatter_dimension=1, tiled=True)
    width_here = local_blocks * block_size
    return (
        output.reshape(tok_rows, width_here),
        input_grad.reshape(tok_rows, width_here),
        inner_one_grad,
        outer_one_grad,
        inner_two_grad,
        outer_two_grad,
    )


def solution(mesh):
    placed = (
        P("dp", "mp"),
        P("mp", None, None),
        P("mp", None, None),
        P("mp", None, None),
        P("mp", None, None),
        P("dp", "mp"),
    )
    return jax.shard_map(
        body,
        mesh=mesh,
        in_specs=placed,
        out_specs=(
            P("dp", "mp"),
            P("dp", "mp"),
            P("mp", "dp", None),
            P("mp", "dp", None),
            P("mp", "dp", None),
            P("mp", "dp", None),
        ),
        check_vma=False,
    )
```

profile of v0, /device:TPU:8, one launch (start us, length us, event | category | flops | bytes accessed | tf_op | source)
XLA Modules:
  0.0 353.0 jit_solution(4285702627832641454)
XLA Ops:
  7.2 0.0 copy-start
  7.2 1.6 copy-done
  8.8 1.7 fusion.11
  10.4 2.9 copy.50
  13.4 0.0 copy-start.7
  13.4 7.7 %all-to-all-start = ((bf16[128,4,2048]{2,1,0:T(4,128)(2,1)}), bf16[128,4,2048]{2,1,0:T(4,128)(2,1)}, u32[]{:S(2)}, u32[]{:S(2)}) async-start(bf16[128,4,2048]{2,1,0:T(4,128)(2,1)} %copy.50), calls=%async_computation | async-start | bytes 4194304 | tf_op jit(solution)/shard_map/all_to_all | solution.py:27
  21.1 0.0 copy-done.7
  21.1 2.3 convolution_convert_fusion.2
  23.4 2.9 copy.57
  26.4 21.3 %all-to-all-done = bf16[128,4,2048]{2,1,0:T(4,128)(2,1)} async-done(((bf16[128,4,2048]{2,1,0:T(4,128)(2,1)}), bf16[128,4,2048]{2,1,0:T(4,128)(2,1)}, u32[]{:S(2)}, u32[]{:S(2)}) %all-to-all-start) | async-done | bytes 2097184 | tf_op jit(solution)/shard_map/all_to_all | solution.py:27
  47.7 8.1 %all-to-all-start.2 = ((bf16[4,128,2048]{2,0,1:T(4,128)(2,1)}), bf16[4,128,2048]{2,0,1:T(4,128)(2,1)}, u32[]{:S(2)}, u32[]{:S(2)}) async-start(bf16[4,128,2048]{2,0,1:T(4,128)(2,1)} %copy.57), calls=%async_computation.2 | async-start | bytes 4194304 | tf_op jit(solution)/shard_map/all_to_all | solution.py:17
  55.8 4.9 %copy.51 = bf16[32,4,4,2048]{3,1,2,0:T(4,128)(2,1)} copy(bf16[32,4,4,2048]{3,2,1,0:T(4,128)(2,1)} %bitcast.1) | data formatting | bytes 4194304 | tf_op jit(solution)/shard_map/all_to_all | solution.py:27
  60.7 21.6 %all-to-all-done.2 = bf16[4,128,2048]{2,0,1:T(4,128)(2,1)} async-done(((bf16[4,128,2048]{2,0,1:T(4,128)(2,1)}), bf16[4,128,2048]{2,0,1:T(4,128)(2,1)}, u32[]{:S(2)}, u32[]{:S(2)}) %all-to-all-start.2) | async-done | bytes 2097184 | tf_op jit(solution)/shard_map/all_to_all | solution.py:17
  82.3 3.7 %copy.58 = bf16[4,32,4,2048]{3,2,0,1:T(4,128)(2,1)S(1)} copy(bf16[4,32,4,2048]{3,0,2,1:T(4,128)(2,1)} %bitcast.10) | data formatting | bytes 4194304 | tf_op jit(solution)/shard_map/all_to_all | solution.py:17
  86.0 0.0 copy-start.3
  86.0 0.0 copy-done.1
  86.0 0.0 copy-done.5
  86.0 0.0 copy-start.8
  86.0 2.3 fusion.27
  88.4 0.0 copy-done.3
  88.4 0.0 copy-done.8
  88.4 4.9 %fusion.6 = bf16[2048,4,128]{2,0,1:T(8,128)(2,1)S(1)} fusion(f32[4,2048,128]{2,1,0:T(8,128)S(1)} %fusion.27, bf16[4,128,128]{2,1,0:T(8,128)(2,1)S(1)} %copy-done.8, bf16[128,4,2048]{2,1,0:T(4,128)(2,1)S(1)} %bitcast.103), kind=kOutput, calls=%fused_computation.8 | convolution fusion | flops 289406976 | bytes 8519680 | tf_op jit(solution)/shard_map/jbt,bkj->tbk/dot_general | solution.py:12
  93.3 0.0 copy-done.2
  93.3 0.0 copy-start.4
  93.3 1.3 copy-done.4
  94.7 2.0 fusion.13
  96.7 4.5 %copy.60 = bf16[4,128,2048]{2,0,1:T(4,128)(2,1)} copy(bf16[4,128,2048]{1,2,0:T(8,128)(2,1)} %fusion.13) | data formatting | bytes 4194304 | tf_op jit(solution)/shard_map/convert_element_type | solution.py:41
  101.2 8.2 %all-to-all-start.3 = ((bf16[4,128,2048]{2,0,1:T(4,128)(2,1)}), bf16[4,128,2048]{2,0,1:T(4,128)(2,1)}, u32[]{:S(2)}, u32[]{:S(2)}) async-start(bf16[4,128,2048]{2,0,1:T(4,128)(2,1)} %copy.60), calls=%async_computation.3 | async-start | bytes 4194304 | tf_op jit(solution)/shard_map/all_to_all | solution.py:44
  109.4 5.0 %fusion.12 = bf16[128,4,2048]{0,2,1:T(8,128)(2,1)} fusion(bf16[4,128,128]{2,1,0:T(8,128)(2,1)S(1)} %copy-done.8, f32[4,2048,128]{2,1,0:T(8,128)} %copy-done.2), kind=kOutput, calls=%fused_computation.23 | convolution fusion | flops 278921216 | bytes 6422528 | tf_op jit(solution)/shard_map/tbk,bkj->jbt/dot_general | solution.py:12
  114.4 4.6 %copy.53 = bf16[128,4,2048]{2,1,0:T(4,128)(2,1)} copy(bf16[128,4,2048]{0,2,1:T(8,128)(2,1)} %fusion.12) | data formatting | bytes 4194304 | tf_op jit(solution)/shard_map/convert_element_type | solution.py:30
  119.0 16.9 %all-to-all-done.3 = bf16[4,128,2048]{2,0,1:T(4,128)(2,1)} async-done(((bf16[4,128,2048]{2,0,1:T(4,128)(2,1)}), bf16[4,128,2048]{2,0,1:T(4,128)(2,1)}, u32[]{:S(2)}, u32[]{:S(2)}) %all-to-all-start.3) | async-done | bytes 2097184 | tf_op jit(solution)/shard_map/all_to_all | solution.py:44
  136.0 8.2 %all-to-all-start.1 = ((bf16[128,4,2048]{2,1,0:T(4,128)(2,1)}), bf16[128,4,2048]{2,1,0:T(4,128)(2,1)}, u32[]{:S(2)}, u32[]{:S(2)}) async-start(bf16[128,4,2048]{2,1,0:T(4,128)(2,1)} %copy.53), calls=%async_computation.1 | async-start | bytes 4194304 | tf_op jit(solution)/shard_map/all_to_all | solution.py:31
  144.2 0.0 all-reduce.3.cloned.1.call-start
  144.2 4.2 %copy.61 = bf16[32,4,4,2048]{3,1,0,2:T(4,128)(2,1)} copy(bf16[32,4,4,2048]{3,1,2,0:T(4,128)(2,1)} %bitcast.16) | data formatting | bytes 4194304 | tf_op jit(solution)/shard_map/all_to_all | solution.py:44
  148.4 4.0 %all_to_all.67 = bf16[128,4,2048]{2,0,1:T(8,128)(2,1)} reshape(bf16[32,4,4,2048]{3,1,0,2:T(4,128)(2,1)} %copy.61) | data formatting | bytes 4194304 | tf_op jit(solution)/shard_map/all_to_all | solution.py:44
  152.4 2.3 fusion.31
  154.7 0.8 copy.63
  155.6 0.0 all-reduce.3.cloned.1.call-update
  155.6 0.0 reduce-scatter.4.cloned.1.call-start
  155.7 5.4 %fusion.29 = f32[4,128,128]{2,1,0:T(8,128)} fusion(bf16[2048,4,128]{2,0,1:T(8,128)(2,1)} %copy-done.4, bf16[4,128,2048]{2,0,1:T(4,128)(2,1)} %bitcast.99), kind=kOutput, calls=%fused_computation.40 | convolution fusion | flops 268435456 | bytes 4456448 | tf_op jit(solution)/shard_map/jbt,tjl->jbl/dot_general | solution.py:12
  161.1 0.0 reduce-scatter.4.cloned.1.call-update
  161.1 0.0 copy-start.9
  161.1 0.0 reduce-scatter.6.cloned.1.call-start
  161.2 7.0 %fusion.25 = f32[4,128,128]{2,1,0:T(8,128)} fusion(bf16[128,4,2048]{2,1,0:T(4,128)(2,1)} %bitcast.104, f32[4,2048,128]{2,1,0:T(8,128)} %copy-done.2), kind=kOutput, calls=%fused_computation.36 | convolution fusion | flops 277872640 | bytes 6553600 | tf_op jit(solution)/shard_map/tbk,jbt->bkj/dot_general | solution.py:12
  168.1 0.0 reduce-scatter.6.cloned.1.call-update
  168.2 0.3 reduce-scatter.8.cloned.1.call-start
  168.5 0.0 copy-done.9
  168.5 0.6 dynamic-slice
  169.7 1.0 all-to-all-done.1
  170.7 4.2 %copy.54 = bf16[4,32,4,2048]{3,2,1,0:T(4,128)(2,1)} copy(bf16[4,32,4,2048]{3,2,0,1:T(4,128)(2,1)} %bitcast.7) | data formatting | bytes 4194304 | tf_op jit(solution)/shard_map/all_to_all | solution.py:31
  175.0 3.9 %all_to_all.59 = bf16[4,128,2048]{2,1,0:T(8,128)(2,1)} reshape(bf16[4,32,4,2048]{3,2,1,0:T(4,128)(2,1)} %copy.54) | data formatting | bytes 4194304 | tf_op jit(solution)/shard_map/all_to_all | solution.py:31
  178.9 3.7 %fusion.14 = f32[4,128,128]{2,1,0:T(8,128)} fusion(bf16[4,128,2048]{2,1,0:T(8,128)(2,1)} %all_to_all.59, bf16[2048,512]{1,0:T(8,128)(2,1)} %param.11), kind=kOutput, calls=%fused_computation.25 | convolution fusion | flops 268435456 | bytes 4456448 | tf_op jit(solution)/shard_map/jbt,tjl->jbl/dot_general | solution.py:12
  182.6 0.0 reduce-scatter.8.cloned.1.call-update
  182.6 0.0 copy-done.6
  182.6 3.6 %convolution_convert_fusion = bf16[4,2048,128]{1,2,0:T(8,128)(2,1)} fusion(bf16[4,128,128]{2,1,0:T(8,128)(2,1)S(1)} %copy-done.6, bf16[128,4,2048]{2,0,1:T(8,128)(2,1)} %all_to_all.67), kind=kOutput, calls=%fused_computation.16 | convolution fusion | flops 269484032 | bytes 4325376 | tf_op jit(solution)/shard_map/jbt,bkj->tbk/dot_general | solution.py:12
  186.3 3.9 %copy.69 = bf16[2048,512]{1,0:T(8,128)(2,1)} copy(bf16[2048,512]{0,1:T(8,128)(2,1)} %bitcast.101) | data formatting | bytes 4194304
  190.2 3.7 %convolution_convert_fusion.3 = bf16[4,2048,128]{1,2,0:T(8,128)(2,1)} fusion(bf16[4,128,2048]{2,1,0:T(8,128)(2,1)} %all_to_all.59, bf16[4,128,128]{2,1,0:T(8,128)(2,1)S(1)} %copy-done.7), kind=kOutput, calls=%fused_computation.19 | convolution fusion | flops 269484032 | bytes 4325376 | tf_op jit(solution)/shard_map/jbt,jbl->tjl/dot_general | solution.py:12
  193.9 3.9 %copy.68 = bf16[2048,512]{1,0:T(8,128)(2,1)} copy(bf16[2048,512]{0,1:T(8,128)(2,1)} %bitcast.102) | data formatting | bytes 4194304
  197.8 33.2 %all-reduce.3.cloned.1.call-done = f32[4,128,128]{2,0,1:T(4,128)} async-done(((f32[4,128,128]{2,0,1:T(4,128)}), f32[4,128,128]{2,0,1:T(4,128)}) %all-reduce.3.cloned.1.call-update) | async-done | bytes 262160
  231.0 0.8 constant_dynamic-slice_fusion
  231.8 0.6 copy.70
  232.4 37.1 %reduce-scatter.4.cloned.1.call-done = f32[4,16,128]{2,1,0:T(8,128)} async-done(((f32[4,128,128]{2,1,0:T(8,128)}), f32[4,16,128]{2,1,0:T(8,128)}) %reduce-scatter.4.cloned.1.call-update) | async-done | bytes 32784 | tf_op jit(solution)/shard_map/reduce_scatter | solution.py:43
  269.5 38.5 %reduce-scatter.6.cloned.1.call-done = f32[4,16,128]{2,1,0:T(8,128)} async-done(((f32[4,128,128]{2,1,0:T(8,128)}), f32[4,16,128]{2,1,0:T(8,128)}) %reduce-scatter.6.cloned.1.call-update) | async-done | bytes 32784 | tf_op jit(solution)/shard_map/reduce_scatter | solution.py:38
  307.9 38.5 %reduce-scatter.8.cloned.1.call-done = f32[4,16,128]{2,1,0:T(8,128)} async-done(((f32[4,128,128]{2,1,0:T(8,128)}), f32[4,16,128]{2,1,0:T(8,128)}) %reduce-scatter.8.cloned.1.call-update) | async-done | bytes 32784 | tf_op jit(solution)/shard_map/reduce_scatter | solution.py:34
  (4 shorter events, 0.0 us)
Async XLA Ops:
  7.2 1.6 copy-start
  13.4 7.7 %copy-start.7 = (bf16[4,128,128]{2,1,0:T(8,128)(2,1)S(1)}, bf16[4,128,128]{2,1,0:T(8,128)(2,1)}, u32[]{:S(2)}) copy-start(bf16[4,128,128]{2,1,0:T(8,128)(2,1)} %param.10) | copy-start | bytes 393220
  13.4 34.3 %all-to-all-start = ((bf16[128,4,2048]{2,1,0:T(4,128)(2,1)}), bf16[128,4,2048]{2,1,0:T(4,128)(2,1)}, u32[]{:S(2)}, u32[]{:S(2)}) async-start(bf16[128,4,2048]{2,1,0:T(4,128)(2,1)} %copy.50), calls=%async_computation | async-start | bytes 4194304 | tf_op jit(solution)/shard_map/all_to_all | solution.py:27
  47.7 34.6 %all-to-all-start.2 = ((bf16[4,128,2048]{2,0,1:T(4,128)(2,1)}), bf16[4,128,2048]{2,0,1:T(4,128)(2,1)}, u32[]{:S(2)}, u32[]{:S(2)}) async-start(bf16[4,128,2048]{2,0,1:T(4,128)(2,1)} %copy.57), calls=%async_computation.2 | async-start | bytes 4194304 | tf_op jit(solution)/shard_map/all_to_all | solution.py:17
  82.3 3.7 %copy-start.1 = (bf16[32,4,4,2048]{3,1,2,0:T(4,128)(2,1)S(1)}, bf16[32,4,4,2048]{3,1,2,0:T(4,128)(2,1)}, u32[]{:S(2)}) copy-start(bf16[32,4,4,2048]{3,1,2,0:T(4,128)(2,1)} %copy.51) | copy-start | bytes 6291460
  82.3 3.7 %copy-start.5 = (bf16[4,128,128]{2,1,0:T(8,128)(2,1)S(1)}, bf16[4,128,128]{2,1,0:T(8,128)(2,1)}, u32[]{:S(2)}) copy-start(bf16[4,128,128]{2,1,0:T(8,128)(2,1)} %param.8) | copy-start | bytes 393220
  86.0 2.4 copy-start.3
  86.0 2.3 copy-start.8
  88.4 5.0 %copy-start.2 = (f32[4,2048,128]{2,1,0:T(8,128)}, f32[4,2048,128]{2,1,0:T(8,128)S(1)}, u32[]{:S(2)}) copy-start(f32[4,2048,128]{2,1,0:T(8,128)S(1)} %fusion.27) | copy-start | bytes 12582916
  93.3 1.3 copy-start.4
  101.2 34.8 %all-to-all-start.3 = ((bf16[4,128,2048]{2,0,1:T(4,128)(2,1)}), bf16[4,128,2048]{2,0,1:T(4,128)(2,1)}, u32[]{:S(2)}, u32[]{:S(2)}) async-start(bf16[4,128,2048]{2,0,1:T(4,128)(2,1)} %copy.60), calls=%async_computation.3 | async-start | bytes 4194304 | tf_op jit(solution)/shard_map/all_to_all | solution.py:44
  136.0 34.8 %all-to-all-start.1 = ((bf16[128,4,2048]{2,1,0:T(4,128)(2,1)}), bf16[128,4,2048]{2,1,0:T(4,128)(2,1)}, u32[]{:S(2)}, u32[]{:S(2)}) async-start(bf16[128,4,2048]{2,1,0:T(4,128)(2,1)} %copy.53), calls=%async_computation.1 | async-start | bytes 4194304 | tf_op jit(solution)/shard_map/all_to_all | solution.py:31
  144.2 86.9 %all-reduce.3.cloned.1.call-start = ((), (), s32[]{:S(2)}) async-start(), calls=%async_computation.10 | async-start | bytes 524288
  155.6 113.8 %reduce-scatter.4.cloned.1.call-start = ((), (), s32[]{:S(2)}) async-start(), calls=%async_computation.7 | async-start | bytes 294912 | tf_op jit(solution)/shard_map/reduce_scatter | solution.py:43
  161.1 7.4 %copy-start.9 = (u32[256]{0:T(256)S(1)}, u32[256]{0:T(256)}, u32[]{:S(2)}) copy-start(u32[256]{0:T(256)} %constant.18) | copy-start | bytes 3076
  161.1 146.8 %reduce-scatter.6.cloned.1.call-start = ((), (), s32[]{:S(2)}) async-start(), calls=%async_computation.8 | async-start | bytes 294912 | tf_op jit(solution)/shard_map/reduce_scatter | solution.py:38
  168.2 178.3 %reduce-scatter.8.cloned.1.call-start = ((), (), s32[]{:S(2)}) async-start(), calls=%async_computation.9 | async-start | bytes 294912 | tf_op jit(solution)/shard_map/reduce_scatter | solution.py:34
  178.9 3.7 %copy-start.6 = (bf16[4,128,128]{2,1,0:T(8,128)(2,1)S(1)}, bf16[4,128,128]{2,1,0:T(8,128)(2,1)}, u32[]{:S(2)}) copy-start(bf16[4,128,128]{2,1,0:T(8,128)(2,1)} %param.7) | copy-start | bytes 393220
Sparse Core Ops, SparseCore 0:
  155.7 75.2 all-reduce.2
  234.2 35.1 reduce-scatter.3
  272.5 35.3 reduce-scatter.5
  311.0 35.3 reduce-scatter.7
where the time goes:
time: 354 us; the launch traced here: 353 us
  waiting for transfers between devices  208 us (59%)
  local copies, waits for them, and re-layouts  53.6 us (15%)
  matrix products  43.9 us (12%)
  starting transfers between devices  32.7 us (9%)
  between operations  14.6 us (4%)
    dot_general x12, matrix products, product(): return jnp.einsum(form, left, right, preferred_element_type=jnp.float32)  43.9 us
    reduce_scatter x1, waiting for transfers between devices, body(): lax.psum_scatter(outer_two_grad, 'dp', scatter_dimension=1, tiled=True)  38.5 us
    reduce_scatter x1, waiting for transfers between devices, body(): lax.psum_scatter(inner_two_grad, 'dp', scatter_dimension=1, tiled=True)  38.5 us
    reduce_scatter x1, waiting for transfers between devices, body(): lax.psum_scatter(outer_one_grad, 'dp', scatter_dimension=1, tiled=True)  37.1 us
    unnamed x5, waiting for transfers between devices  33.3 us
    all_to_all x1, waiting for transfers between devices, return_second(): lax.all_to_all(grad_perm_two, 'mp', split_axis=1, concat_axis=0, tiled=True)  21.6 us
    all_to_all x1, waiting for transfers between devices, body(): lax.all_to_all(first_mid, 'mp', split_axis=0, concat_axis=1, tiled=True)  21.3 us
    all_to_all x1, waiting for transfers between devices, body(): lax.all_to_all(grad_perm_one, 'mp', split_axis=1, concat_axis=0, tiled=True)  16.9 us
  transfers between devices with their start and end apart: 8, of which 8 were waited for; matrix products, arithmetic and copies ran while one was open for 18% of the time, Pallas kernels for 0%

commit v1 on v0

v1 whole, which is shorter than its diff:
```python
import jax
import jax.numpy as jnp
from jax import lax
from jax.experimental import pallas as pl
from jax.experimental.pallas import tpu as pltpu
from jax.sharding import PartitionSpec as P

BF = jnp.bfloat16
F32 = jnp.float32
GELU_SCALE = 0.7978845608028654
GELU_CUBE = 0.044715


def dot(left, right, left_dim, right_dim):
    return lax.dot_general(
        left, right, (((left_dim,), (right_dim,)), ((), ())), preferred_element_type=F32
    )


def inner_spread(block, wide, rows_wide):
    shape = (wide, 128) if rows_wide else (128, wide)
    row = lax.broadcasted_iota(jnp.int32, shape, 0)
    col = lax.broadcasted_iota(jnp.int32, shape, 1)
    hit = (row == 4 * col + block) if rows_wide else (col == 4 * row + block)
    return hit.astype(F32).astype(BF)


def outer_spread(block):
    row = lax.broadcasted_iota(jnp.int32, (512, 128), 0)
    col = lax.broadcasted_iota(jnp.int32, (512, 128), 1)
    hit = row == 16 * (col // 4) + 4 * block + col % 4
    return hit.astype(F32).astype(BF)


def fill_inner_t(weight_ref, wide_ref):
    for block in range(4):
        wide_ref[:, 128 * block:128 * block + 128] = dot(
            inner_spread(block, 512, True), weight_ref[block], 1, 1
        ).astype(BF)


def fill_inner(weight_ref, wide_ref):
    for block in range(4):
        wide_ref[128 * block:128 * block + 128, :] = dot(
            weight_ref[block], inner_spread(block, 512, False), 1, 0
        ).astype(BF)


def fill_outer(weight_ref, wide_ref):
    for block in range(4):
        wide_ref[:, 128 * block:128 * block + 128] = dot(
            outer_spread(block), weight_ref[block], 1, 0
        ).astype(BF)


def fill_outer_t(weight_ref, wide_ref):
    for block in range(4):
        wide_ref[128 * block:128 * block + 128, :] = dot(
            weight_ref[block], outer_spread(block), 0, 1
        ).astype(BF)


def first(fill):
    pl.when(pl.program_id(0) == 0)(fill)


def head_kernel(fill, x_ref, weight_ref, mid_ref, wide_ref):
    first(lambda: fill(weight_ref, wide_ref))
    mid = dot(wide_ref[...], x_ref[...], 1, 1).astype(BF)
    mid_ref[...] = mid.reshape(mid_ref.shape)


def rows(ref):
    return ref[...].reshape(512, ref.shape[-1])


def forward_kernel(perm_ref, outer_ref, inner_ref, hidden_ref, slope_ref, mid_ref, outer_wide, inner_wide):
    def fill():
        fill_outer_t(outer_ref, outer_wide)
        fill_inner_t(inner_ref, inner_wide)

    first(fill)
    pre = dot(outer_wide[...], rows(perm_ref), 1, 0)
    square = pre * pre
    bent = jnp.tanh(GELU_SCALE * (pre + GELU_CUBE * (square * pre)))
    half = 0.5 * (1.0 + bent)
    hidden = (pre * half).astype(BF)
    hidden_ref[...] = hidden
    slope_ref[...] = half + (0.5 * GELU_SCALE) * pre * (1.0 - bent * bent) * (1.0 + (3.0 * GELU_CUBE) * square)
    mid = dot(inner_wide[...], hidden, 1, 0).astype(BF)
    mid_ref[...] = mid.reshape(mid_ref.shape)


def backward_kernel(grad_mid_ref, slope_ref, inner_ref, outer_ref, grad_pre_ref, grad_perm_ref, inner_wide, outer_wide):
    def fill():
        fill_inner(inner_ref, inner_wide)
        fill_outer(outer_ref, outer_wide)

    first(fill)
    grad_hidden = dot(inner_wide[...], rows(grad_mid_ref), 1, 0)
    grad_pre = (grad_hidden * slope_ref[...]).astype(BF)
    grad_pre_ref[...] = grad_pre
    grad_perm = dot(outer_wide[...], grad_pre, 1, 0).astype(BF)
    grad_perm_ref[...] = grad_perm.reshape(grad_perm_ref.shape)


def picked(total_ref, by_j):
    row = lax.broadcasted_iota(jnp.int32, (512, 128), 0)
    mine = (row // 4) % 4 if by_j else row % 4
    value = total_ref[:, 0:128]
    for block in range(1, 4):
        value = jnp.where(mine == block, total_ref[:, 128 * block:128 * block + 128], value)
    return value


def write_outer(total_ref, picked_ref, block_ref, out_ref):
    picked_ref[...] = picked(total_ref, True)
    for j in range(4):
        for b in range(4):
            block_ref[pl.ds(b, 32, stride=4), :] = picked_ref[pl.ds(4 * j + b, 32, stride=16), :]
        for rank in range(8):
            out_ref[rank, 16 * j:16 * j + 16, :] = block_ref[16 * rank:16 * rank + 16, :].astype(out_ref.dtype)


def write_inner(total_ref, picked_ref, out_ref):
    picked_ref[...] = picked(total_ref, False)
    for b in range(4):
        block = picked_ref[pl.ds(b, 128, stride=4), :].T.astype(out_ref.dtype)
        for rank in range(8):
            out_ref[rank, 16 * b:16 * b + 16, :] = block[16 * rank:16 * rank + 16, :]


def accumulate(total_ref, value):
    step = pl.program_id(0)

    @pl.when(step == 0)
    def _():
        total_ref[...] = value

    @pl.when(step > 0)
    def _():
        total_ref[...] += value


def last(write):
    pl.when(pl.program_id(0) == pl.num_programs(0) - 1)(write)


def inner_grad_kernel(dims, grad_ref, other_ref, out_ref, total_ref, picked_ref):
    accumulate(total_ref, dot(rows(grad_ref), other_ref[...], *dims))
    last(lambda: write_inner(total_ref, picked_ref, out_ref))


def outer_grad_kernel(dims, perm_ref, other_ref, out_ref, total_ref, picked_ref, block_ref):
    accumulate(total_ref, dot(rows(perm_ref), other_ref[...], *dims))
    last(lambda: write_outer(total_ref, picked_ref, block_ref, out_ref))


def tail_kernel(fill, perm_ref, weight_ref, out_ref, wide_ref):
    first(lambda: fill(weight_ref, wide_ref))
    out_ref[...] = dot(rows(perm_ref), wide_ref[...], 0, 0).astype(BF)


def call(kernel, grid, specs, outs, scratch, args, flops, name):
    moved = sum(a.size * a.dtype.itemsize for a in args)
    moved += sum(o.size * o.dtype.itemsize for o, _ in outs)
    return pl.pallas_call(
        kernel,
        grid=(grid,),
        in_specs=specs,
        out_specs=[s for _, s in outs],
        out_shape=[o for o, _ in outs],
        scratch_shapes=scratch,
        name=name,
        cost_estimate=pl.CostEstimate(flops=flops, bytes_accessed=moved, transcendentals=0),
        compiler_params=pltpu.CompilerParams(
            dimension_semantics=("arbitrary",), vmem_limit_bytes=60 * 1024 * 1024
        ),
    )(*args)


def body(tokens, inner_one, outer_one, inner_two, outer_two, cotangent):
    tok = tokens.shape[0]
    tile = 512
    steps = tok // tile
    one = 2 * tok * 512 * 512
    shape = jax.ShapeDtypeStruct
    by_token = pl.BlockSpec((tile, 512), lambda i: (i, 0))
    by_message = pl.BlockSpec((32, 16, tile), lambda i: (0, 0, i))
    by_feature = pl.BlockSpec((512, tile), lambda i: (0, i))
    weight = pl.BlockSpec((4, 128, 128), lambda i: (0, 0, 0))
    grad_spec = pl.BlockSpec((8, 64, 128), lambda i: (0, 0, 0))
    message = shape((32, 16, tok), BF)
    feature = shape((512, tok), BF)
    token_out = shape((tok, 512), BF)
    wide = pltpu.VMEM((512, 512), BF)
    total = pltpu.VMEM((512, 512), F32)
    pick = pltpu.VMEM((512, 128), F32)
    block = pltpu.VMEM((128, 128), F32)

    def head(fill, x, w, name):
        return call(lambda *r: head_kernel(fill, *r), steps, [by_token, weight], [(message, by_message)], [wide], (x, w), one, name)[0]

    def tail(fill, perm, w, name):
        return call(lambda *r: tail_kernel(fill, *r), steps, [by_message, weight], [(token_out, by_token)], [wide], (perm, w), one, name)[0]

    def inner_grad(grad, other, spec, dims, name, kind=F32):
        return call(lambda *r: inner_grad_kernel(dims, *r), steps, [by_message, spec], [(shape((8, 64, 128), kind), grad_spec)], [total, pick], (grad, other), one, name)[0]

    def outer_grad(perm, other, spec, dims, name):
        return call(lambda *r: outer_grad_kernel(dims, *r), steps, [by_message, spec], [(shape((8, 64, 128), F32), grad_spec)], [total, pick, block], (perm, other), one, name)[0]

    def exchange(value):
        return lax.all_to_all(value, "mp", split_axis=0, concat_axis=0, tiled=True)

    def reduce(value):
        parts = lax.all_to_all(value, "dp", split_axis=0, concat_axis=0, tiled=True)
        return jnp.sum(parts.astype(F32), axis=0)

    def after(value, earlier):
        return lax.optimization_barrier((value, earlier))

    first_perm = exchange(head(fill_inner_t, tokens, inner_one, "first_mid"))
    grad_perm_two, first_perm = after(head(fill_outer, cotangent, outer_two, "grad_perm_two"), first_perm)
    grad_mid_two = exchange(grad_perm_two)
    hidden, slope, second_mid = call(
        forward_kernel, steps, [by_message, weight, weight],
        [(feature, by_feature), (shape((512, tok), F32), by_feature), (message, by_message)],
        [wide, wide], (first_perm, outer_one, inner_two), 2 * one, "hidden",
    )
    second_mid, grad_mid_two = after(second_mid, grad_mid_two)
    second_perm = exchange(second_mid)
    grad_pre, grad_perm_one = call(
        backward_kernel, steps, [by_message, by_feature, weight, weight],
        [(feature, by_feature), (message, by_message)],
        [wide, wide], (grad_mid_two, slope, inner_two, outer_one), 2 * one, "grad_pre",
    )
    grad_perm_one, second_perm = after(grad_perm_one, second_perm)
    grad_mid_one = exchange(grad_perm_one)
    inner_two_part = inner_grad(grad_mid_two, hidden, by_feature, (1, 1), "inner_two_grad")
    outer_one_part = outer_grad(first_perm, grad_pre, by_feature, (1, 1), "outer_one_grad")
    outer_two_part = outer_grad(second_perm, cotangent, by_token, (1, 0), "outer_two_grad")
    sums = jnp.concatenate([inner_two_part, outer_one_part, outer_two_part], axis=1)
    sums = lax.psum_scatter(sums, "dp", scatter_dimension=0, tiled=True).reshape(192, 128)
    output = tail(fill_outer, second_perm, outer_two, "output")
    inner_one_part = inner_grad(grad_mid_one, tokens, by_token, (1, 0), "inner_one_grad", BF)
    inner_one_sum = reduce(inner_one_part)
    input_grad = tail(fill_inner_t, grad_mid_one, inner_one, "input_grad")
    return (
        output,
        input_grad,
        inner_one_sum.reshape(4, 16, 128),
        sums[64:128].reshape(4, 16, 128),
        sums[0:64].reshape(4, 16, 128),
        sums[128:192].reshape(4, 16, 128),
    )


def solution(mesh):
    placed = (
        P("dp", "mp"),
        P("mp", None, None),
        P("mp", None, None),
        P("mp", None, None),
        P("mp", None, None),
        P("dp", "mp"),
    )
    return jax.shard_map(
        body,
        mesh=mesh,
        in_specs=placed,
        out_specs=(
            P("dp", "mp"),
            P("dp", "mp"),
            P("mp", "dp", None),
            P("mp", "dp", None),
            P("mp", "dp", None),
            P("mp", "dp", None),
        ),
        check_vma=False,
    )
```

time: 354 us -> 198 us (0.56)
  waiting for transfers between devices: 208 us -> 80.9 us
  Pallas kernels: 0 us -> 55 us
  local copies, waits for them, and re-layouts: 53.6 us -> 4.11 us
  matrix products: 43.9 us -> 0 us
  starting transfers between devices: 32.7 us -> 39.1 us
    reduce_scatter x3 -> x1, waiting for transfers between devices: 114 us -> 17 us  [body(): lax.psum_scatter(sums, 'dp', scatter_dimension=0, tiled=True)]
    pallas_call x0 -> x10, Pallas kernels: none -> 55 us  [call(): pl.pallas_call(kernel, grid=(grid,), in_specs=specs, out_specs=[s for _,...]
    dot_general x12 -> x0, matrix products: 43.9 us -> none  [product(): return jnp.einsum(form, left, right, preferred_element_type=jnp.float32)]
    unnamed x5 -> x1, waiting for transfers between devices: 33.3 us -> 0.02 us
    all_to_all x6 -> x0, local copies, waits for them, and re-layouts: 25 us -> none  [the longest x2 8.23 us: body(): lax.all_to_all(grad_perm_one, 'mp', split_axis=1, concat_axis=0, tiled=True)]
    convert_element_type x4 -> x0, local copies, waits for them, and re-layouts: 15 us -> none  [the longest x1 4.59 us: body(): second_mid = product('tbk,bkj->jbt', hidden, inner_two).astype(jnp.bfloat16)]
    unnamed x25 -> x10, local copies, waits for them, and re-layouts: 12.8 us -> 2.68 us
    all_to_all x4 -> x5, starting transfers between devices: 32.2 us -> 39 us  [the longest x4 30.6 us: exchange(): return lax.all_to_all(value, 'mp', split_axis=0, concat_axis=0, tiled=True)]
  transfers between devices with their start and end apart: 8 -> 6, of which waited for: 8 -> 5; matrix products, arithmetic and copies ran while one was open for 18% -> 2% of each run, Pallas kernels for 0% -> 26%
where the time goes in v1:
time: 198 us; the launch traced here: 196 us
  waiting for transfers between devices  80.9 us (41%)
  Pallas kernels  55 us (28%)
  starting transfers between devices  39.1 us (20%)
  between operations  14.1 us (7%)
  local copies, waits for them, and re-layouts  4.11 us (2%)
  other arithmetic  2.52 us (1%)
    all_to_all x4, waiting for transfers between devices, exchange(): return lax.all_to_all(value, 'mp', split_axis=0, concat_axis=0, tiled=True)  64 us
    pallas_call x10, Pallas kernels, call(): pl.pallas_call(kernel, grid=(grid,), in_specs=specs, out_specs=[s for _,...  55 us
    all_to_all x4, starting transfers between devices, exchange(): return lax.all_to_all(value, 'mp', split_axis=0, concat_axis=0, tiled=True)  30.6 us
    reduce_scatter x1, waiting for transfers between devices, body(): lax.psum_scatter(sums, 'dp', scatter_dimension=0, tiled=True)  17 us
    all_to_all x1, starting transfers between devices, reduce(): parts = lax.all_to_all(value, 'dp', split_axis=0, concat_axis=0, tiled=True)  8.47 us
  transfers between devices with their start and end apart: 6, of which 5 were waited for; matrix products, arithmetic and copies ran while one was open for 2% of the time, Pallas kernels for 26%

profile of v1, /device:TPU:8, one launch (start us, length us, event | category | flops | bytes accessed | tf_op | source)
XLA Modules:
  0.0 195.8 jit_solution(15751203557279674441)
XLA Ops:
  7.2 5.0 %first_mid.1 = bf16[32,16,2048]{2,1,0:T(8,128)(2,1)} custom-call(bf16[2048,512]{1,0:T(8,128)(2,1)} %r_1_.10, bf16[4,128,128]{2,1,0:T(8,128)(2,1)} %r_1_.9), custom_call_target="tpu_custom_call" | custom-call | flops 1073741824 | bytes 4325376 | tf_op jit(solution)/shard_map/first_mid/pallas_call | solution.py:167
  12.2 7.5 %all-to-all-start = ((bf16[32,16,2048]{2,1,0:T(8,128)(2,1)}), bf16[32,16,2048]{2,1,0:T(8,128)(2,1)S(1)}, u32[]{:S(2)}, u32[]{:S(2)}) async-start(bf16[32,16,2048]{2,1,0:T(8,128)(2,1)} %first_mid.1), calls=%async_computation | async-start | bytes 4194304 | tf_op jit(solution)/shard_map/all_to_all | solution.py:214
  19.7 5.1 %grad_perm_two.1 = bf16[32,16,2048]{2,1,0:T(8,128)(2,1)} custom-call(bf16[2048,512]{1,0:T(8,128)(2,1)} %r_1_.11, bf16[4,128,128]{2,1,0:T(8,128)(2,1)} %r_1_.8), custom_call_target="tpu_custom_call" | custom-call | flops 1073741824 | bytes 4325376 | tf_op jit(solution)/shard_map/grad_perm_two/pallas_call | solution.py:167
  24.8 21.4 %all-to-all-done.perm_ref.r_0_ = bf16[32,16,2048]{2,1,0:T(8,128)(2,1)S(1)} async-done(((bf16[32,16,2048]{2,1,0:T(8,128)(2,1)}), bf16[32,16,2048]{2,1,0:T(8,128)(2,1)S(1)}, u32[]{:S(2)}, u32[]{:S(2)}) %all-to-all-start) | async-done | bytes 2097184 | tf_op jit(solution)/shard_map/all_to_all | solution.py:214
  46.2 0.0 copy-start.2
  46.2 8.1 %all-to-all-start.1 = ((bf16[32,16,2048]{2,1,0:T(8,128)(2,1)}), bf16[32,16,2048]{2,1,0:T(8,128)(2,1)}, u32[]{:S(2)}, u32[]{:S(2)}) async-start(bf16[32,16,2048]{2,1,0:T(8,128)(2,1)} %grad_perm_two.1), calls=%async_computation.1 | async-start | bytes 4194304 | tf_op jit(solution)/shard_map/all_to_all | solution.py:214
  54.3 0.0 copy-done.2
  54.3 7.9 %hidden.1 = (bf16[512,2048]{1,0:T(8,128)(2,1)}, f32[512,2048]{1,0:T(8,128)}, bf16[32,16,2048]{2,1,0:T(8,128)(2,1)}) custom-call(bf16[32,16,2048]{2,1,0:T(8,128)(2,1)} %copy-done.2, bf16[4,128,128]{2,1,0:T(8,128)(2,1)} %outer_ref.3, bf16[4,128,128]{2,1,0:T(8,128)(2,1)} %inner_ref.3), custom_call_target="tpu_custom_call" | custom-call | flops 2147483648 | bytes 10747904 | tf_op jit(solution)/shard_map/hidden/pallas_call | solution.py:167
  62.2 18.7 %all-to-all-done.1.grad_mid_ref.r_0_ = bf16[32,16,2048]{2,1,0:T(8,128)(2,1)} async-done(((bf16[32,16,2048]{2,1,0:T(8,128)(2,1)}), bf16[32,16,2048]{2,1,0:T(8,128)(2,1)}, u32[]{:S(2)}, u32[]{:S(2)}) %all-to-all-start.1) | async-done | bytes 2097184 | tf_op jit(solution)/shard_map/all_to_all | solution.py:214
  80.9 7.5 %all-to-all-start.2 = ((bf16[32,16,2048]{2,1,0:T(8,128)(2,1)}), bf16[32,16,2048]{2,1,0:T(8,128)(2,1)S(1)}, u32[]{:S(2)}, u32[]{:S(2)}) async-start(bf16[32,16,2048]{2,1,0:T(8,128)(2,1)} %get-tuple-element.23), calls=%async_computation.2 | async-start | bytes 4194304 | tf_op jit(solution)/shard_map/all_to_all | solution.py:214
  88.4 7.0 %grad_pre.1 = (bf16[512,2048]{1,0:T(8,128)(2,1)}, bf16[32,16,2048]{2,1,0:T(8,128)(2,1)}) custom-call(bf16[32,16,2048]{2,1,0:T(8,128)(2,1)} %all-to-all-done.1.grad_mid_ref.r_0_, f32[512,2048]{1,0:T(8,128)} %get-tuple-element.21.slope_ref, bf16[4,128,128]{2,1,0:T(8,128)(2,1)} %inner_ref.3, bf16[4,128,128]{2,1,0:T(8,128)(2,1)} %outer_ref.3), custom_call_target="tpu_custom_call" | custom-call | flops 2147483648 | bytes 10747904 | tf_op jit(solution)/shard_map/grad_pre/pallas_call | solution.py:167
  95.4 19.5 %all-to-all-done.2.r_0_ = bf16[32,16,2048]{2,1,0:T(8,128)(2,1)S(1)} async-done(((bf16[32,16,2048]{2,1,0:T(8,128)(2,1)}), bf16[32,16,2048]{2,1,0:T(8,128)(2,1)S(1)}, u32[]{:S(2)}, u32[]{:S(2)}) %all-to-all-start.2) | async-done | bytes 2097184 | tf_op jit(solution)/shard_map/all_to_all | solution.py:214
  114.9 0.0 copy-start.1
  114.9 1.3 copy-done.1
  116.2 7.5 %all-to-all-start.3 = ((bf16[32,16,2048]{2,1,0:T(8,128)(2,1)}), bf16[32,16,2048]{2,1,0:T(8,128)(2,1)S(1)}, u32[]{:S(2)}, u32[]{:S(2)}) async-start(bf16[32,16,2048]{2,1,0:T(8,128)(2,1)} %get-tuple-element.25), calls=%async_computation.3 | async-start | bytes 4194304 | tf_op jit(solution)/shard_map/all_to_all | solution.py:214
  123.7 0.0 reduce-scatter.2.cloned.1.call-start
  123.7 5.1 %inner_two_grad.1 = f32[8,64,128]{2,1,0:T(8,128)} custom-call(bf16[32,16,2048]{2,1,0:T(8,128)(2,1)} %all-to-all-done.1.grad_mid_ref.r_0_, bf16[512,2048]{1,0:T(8,128)(2,1)} %get-tuple-element.26.r_1_), custom_call_target="tpu_custom_call" | custom-call | flops 1073741824 | bytes 4456448 | tf_op jit(solution)/shard_map/inner_two_grad/pallas_call | solution.py:167
  128.8 5.1 %outer_one_grad.1 = f32[8,64,128]{2,1,0:T(8,128)} custom-call(bf16[32,16,2048]{2,1,0:T(8,128)(2,1)} %copy-done.2, bf16[512,2048]{1,0:T(8,128)(2,1)} %get-tuple-element.27.r_1_), custom_call_target="tpu_custom_call" | custom-call | flops 1073741824 | bytes 4456448 | tf_op jit(solution)/shard_map/outer_one_grad/pallas_call | solution.py:167
  133.9 0.0 copy-start.3
  133.9 0.0 copy-start.4
  133.9 5.1 %outer_two_grad.1 = f32[8,64,128]{2,1,0:T(8,128)} custom-call(bf16[32,16,2048]{2,1,0:T(8,128)(2,1)} %copy-done.1, bf16[2048,512]{1,0:T(8,128)(2,1)} %r_1_.11), custom_call_target="tpu_custom_call" | custom-call | flops 1073741824 | bytes 4456448 | tf_op jit(solution)/shard_map/outer_two_grad/pallas_call | solution.py:167
  139.0 0.0 copy-done.3
  139.0 0.0 copy-done.4
  139.0 1.9 pad_maximum_fusion
  140.9 0.0 reduce-scatter.2.cloned.1.call-update
  140.9 5.0 %output.1 = bf16[2048,512]{1,0:T(8,128)(2,1)} custom-call(bf16[32,16,2048]{2,1,0:T(8,128)(2,1)} %copy-done.1, bf16[4,128,128]{2,1,0:T(8,128)(2,1)} %r_1_.8), custom_call_target="tpu_custom_call" | custom-call | flops 1073741824 | bytes 4325376 | tf_op jit(solution)/shard_map/output/pallas_call | solution.py:167
  145.9 4.3 %all-to-all-done.3.r_0_ = bf16[32,16,2048]{2,1,0:T(8,128)(2,1)S(1)} async-done(((bf16[32,16,2048]{2,1,0:T(8,128)(2,1)}), bf16[32,16,2048]{2,1,0:T(8,128)(2,1)S(1)}, u32[]{:S(2)}, u32[]{:S(2)}) %all-to-all-start.3) | async-done | bytes 2097184 | tf_op jit(solution)/shard_map/all_to_all | solution.py:214
  150.2 0.0 copy-start
  150.2 1.3 copy-done
  151.5 4.9 %inner_one_grad.1 = bf16[8,64,128]{2,1,0:T(8,128)(2,1)} custom-call(bf16[32,16,2048]{2,1,0:T(8,128)(2,1)} %copy-done, bf16[2048,512]{1,0:T(8,128)(2,1)} %r_1_.10), custom_call_target="tpu_custom_call" | custom-call | flops 1073741824 | bytes 4325376 | tf_op jit(solution)/shard_map/inner_one_grad/pallas_call | solution.py:167
  156.4 8.5 %all-to-all-start.4 = ((bf16[8,64,128]{2,1,0:T(8,128)(2,1)}), bf16[8,64,128]{2,1,0:T(8,128)(2,1)S(1)}, u32[]{:S(2)}, u32[]{:S(2)}) async-start(bf16[8,64,128]{2,1,0:T(8,128)(2,1)} %inner_one_grad.1), calls=%async_computation.4 | async-start | bytes 262144 | tf_op jit(solution)/shard_map/all_to_all | solution.py:217
  164.9 17.0 %reduce-scatter.2.cloned.1.call-done = f32[1,192,128]{2,1,0:T(8,128)} async-done(((f32[8,192,128]{2,1,0:T(8,128)}), f32[1,192,128]{2,1,0:T(8,128)}) %reduce-scatter.2.cloned.1.call-update) | async-done | bytes 98320 | tf_op jit(solution)/shard_map/reduce_scatter | solution.py:244
  181.9 1.4 fusion
  183.3 5.0 %input_grad.1 = bf16[2048,512]{1,0:T(8,128)(2,1)} custom-call(bf16[32,16,2048]{2,1,0:T(8,128)(2,1)} %copy-done, bf16[4,128,128]{2,1,0:T(8,128)(2,1)} %r_1_.9), custom_call_target="tpu_custom_call" | custom-call | flops 1073741824 | bytes 4325376 | tf_op jit(solution)/shard_map/input_grad/pallas_call | solution.py:167
  188.3 0.0 all-to-all-done.4
  188.3 0.6 convert_reduce_fusion
Async XLA Ops:
  12.2 34.1 %all-to-all-start = ((bf16[32,16,2048]{2,1,0:T(8,128)(2,1)}), bf16[32,16,2048]{2,1,0:T(8,128)(2,1)S(1)}, u32[]{:S(2)}, u32[]{:S(2)}) async-start(bf16[32,16,2048]{2,1,0:T(8,128)(2,1)} %first_mid.1), calls=%async_computation | async-start | bytes 4194304 | tf_op jit(solution)/shard_map/all_to_all | solution.py:214
  46.2 8.1 %copy-start.2 = (bf16[32,16,2048]{2,1,0:T(8,128)(2,1)}, bf16[32,16,2048]{2,1,0:T(8,128)(2,1)S(1)}, u32[]{:S(2)}) copy-start(bf16[32,16,2048]{2,1,0:T(8,128)(2,1)S(1)} %all-to-all-done.perm_ref.r_0_) | copy-start | bytes 6291460
  46.2 34.7 %all-to-all-start.1 = ((bf16[32,16,2048]{2,1,0:T(8,128)(2,1)}), bf16[32,16,2048]{2,1,0:T(8,128)(2,1)}, u32[]{:S(2)}, u32[]{:S(2)}) async-start(bf16[32,16,2048]{2,1,0:T(8,128)(2,1)} %grad_perm_two.1), calls=%async_computation.1 | async-start | bytes 4194304 | tf_op jit(solution)/shard_map/all_to_all | solution.py:214
  80.9 34.0 %all-to-all-start.2 = ((bf16[32,16,2048]{2,1,0:T(8,128)(2,1)}), bf16[32,16,2048]{2,1,0:T(8,128)(2,1)S(1)}, u32[]{:S(2)}, u32[]{:S(2)}) async-start(bf16[32,16,2048]{2,1,0:T(8,128)(2,1)} %get-tuple-element.23), calls=%async_computation.2 | async-start | bytes 4194304 | tf_op jit(solution)/shard_map/all_to_all | solution.py:214
  114.9 1.3 copy-start.1
  116.2 34.0 %all-to-all-start.3 = ((bf16[32,16,2048]{2,1,0:T(8,128)(2,1)}), bf16[32,16,2048]{2,1,0:T(8,128)(2,1)S(1)}, u32[]{:S(2)}, u32[]{:S(2)}) async-start(bf16[32,16,2048]{2,1,0:T(8,128)(2,1)} %get-tuple-element.25), calls=%async_computation.3 | async-start | bytes 4194304 | tf_op jit(solution)/shard_map/all_to_all | solution.py:214
  123.7 58.2 %reduce-scatter.2.cloned.1.call-start = ((), (), s32[]{:S(2)}) async-start(), calls=%async_computation.6 | async-start | bytes 884736 | tf_op jit(solution)/shard_map/reduce_scatter | solution.py:244
  133.9 5.1 %copy-start.3 = (f32[8,64,128]{2,1,0:T(8,128)S(1)}, f32[8,64,128]{2,1,0:T(8,128)}, u32[]{:S(2)}) copy-start(f32[8,64,128]{2,1,0:T(8,128)} %inner_two_grad.1) | copy-start | bytes 786436
  133.9 5.1 %copy-start.4 = (f32[8,64,128]{2,1,0:T(8,128)S(1)}, f32[8,64,128]{2,1,0:T(8,128)}, u32[]{:S(2)}) copy-start(f32[8,64,128]{2,1,0:T(8,128)} %outer_one_grad.1) | copy-start | bytes 786436
  150.2 1.3 copy-start
  156.4 31.8 %all-to-all-start.4 = ((bf16[8,64,128]{2,1,0:T(8,128)(2,1)}), bf16[8,64,128]{2,1,0:T(8,128)(2,1)S(1)}, u32[]{:S(2)}, u32[]{:S(2)}) async-start(bf16[8,64,128]{2,1,0:T(8,128)(2,1)} %inner_one_grad.1), calls=%async_computation.4 | async-start | bytes 262144 | tf_op jit(solution)/shard_map/all_to_all | solution.py:217
Sparse Core Ops, SparseCore 0:
  141.0 40.8 reduce-scatter.1

commit v2 on v1

v2 whole, which is shorter than its diff:
```python
import jax
import jax.numpy as jnp
from jax import lax
from jax.experimental import pallas as pl
from jax.experimental.pallas import tpu as pltpu
from jax.sharding import PartitionSpec as P

BF = jnp.bfloat16
F32 = jnp.float32
GELU_SCALE = 0.7978845608028654
GELU_CUBE = 0.044715
TILES = 4
ROWS = 64


def dot(left, right, left_dim, right_dim):
    return lax.dot_general(
        left, right, (((left_dim,), (right_dim,)), ((), ())), preferred_element_type=F32
    )


def inner_spread(block, wide, rows_wide):
    shape = (wide, 128) if rows_wide else (128, wide)
    row = lax.broadcasted_iota(jnp.int32, shape, 0)
    col = lax.broadcasted_iota(jnp.int32, shape, 1)
    hit = (row == 4 * col + block) if rows_wide else (col == 4 * row + block)
    return hit.astype(F32).astype(BF)


def outer_spread(block):
    row = lax.broadcasted_iota(jnp.int32, (512, 128), 0)
    col = lax.broadcasted_iota(jnp.int32, (512, 128), 1)
    hit = row == 16 * (col // 4) + 4 * block + col % 4
    return hit.astype(F32).astype(BF)


def fill_inner_t(weight_ref, wide_ref):
    for block in range(4):
        wide_ref[:, 128 * block:128 * block + 128] = dot(
            inner_spread(block, 512, True), weight_ref[block], 1, 1
        ).astype(BF)


def fill_inner(weight_ref, wide_ref):
    for block in range(4):
        wide_ref[128 * block:128 * block + 128, :] = dot(
            weight_ref[block], inner_spread(block, 512, False), 1, 0
        ).astype(BF)


def fill_outer(weight_ref, wide_ref):
    for block in range(4):
        wide_ref[:, 128 * block:128 * block + 128] = dot(
            outer_spread(block), weight_ref[block], 1, 0
        ).astype(BF)


def fill_outer_t(weight_ref, wide_ref):
    for block in range(4):
        wide_ref[128 * block:128 * block + 128, :] = dot(
            weight_ref[block], outer_spread(block), 0, 1
        ).astype(BF)


def rows(value):
    return value.reshape(512, value.shape[-1])


def copies(source, target, sems, tile, axis):
    out = []
    for i in range(TILES):
        at = (slice(None),) * axis + (pl.ds(tile * i, tile),)
        out.append(pltpu.make_async_copy(source.at[at], target.at[at], sems.at[i]))
    return out


def begin(many):
    for copy in many:
        copy.start()


def finish(many):
    for copy in many:
        copy.wait()


def head_kernel(
    x_hbm, g_hbm, inner_hbm, outer_hbm, sent_hbm,
    x_buf, g_buf, inner_buf, outer_buf, sent_buf, inner_wide, outer_wide,
    weight_sems, x_sems, g_sems, first_sems, second_sems,
):
    tile = x_buf.shape[0] // TILES
    inner_copy = pltpu.make_async_copy(inner_hbm, inner_buf, weight_sems.at[0])
    outer_copy = pltpu.make_async_copy(outer_hbm, outer_buf, weight_sems.at[1])
    x_copies = copies(x_hbm, x_buf, x_sems, tile, 0)
    g_copies = copies(g_hbm, g_buf, g_sems, tile, 0)
    inner_copy.start()
    begin(x_copies[:1])
    outer_copy.start()
    begin(x_copies[1:])
    begin(g_copies)
    inner_copy.wait()
    fill_inner_t(inner_buf, inner_wide)
    outer_copy.wait()
    fill_outer(outer_buf, outer_wide)
    outs = []
    for part, wide, buf, loads, sems in (
        (0, inner_wide, x_buf, x_copies, first_sems),
        (1, outer_wide, g_buf, g_copies, second_sems),
    ):
        band = pl.ds(16 * part, 16)
        stores = copies(sent_buf.at[:, band, :], sent_hbm.at[:, band, :], sems, tile, 2)
        outs += stores
        for i in range(TILES):
            loads[i].wait()
            mid = dot(wide[...], buf[tile * i:tile * i + tile, :], 1, 1).astype(BF)
            sent_buf[:, 16 * part:16 * part + 16, tile * i:tile * i + tile] = mid.reshape(32, 16, tile)
            stores[i].start()
    finish(outs)


def middle_kernel(
    got_hbm, outer_hbm, inner_hbm, sent_hbm, hidden_hbm, grad_pre_hbm,
    got_buf, outer_buf, inner_buf, sent_buf, hidden_buf, grad_pre_buf, pre_ref, slope_ref,
    outer_wide, outer_wide_t, inner_wide, inner_wide_t,
    weight_sems, got_sems, sent_sems, hidden_sems, grad_pre_sems,
):
    tile = hidden_buf.shape[1] // TILES
    outer_copy = pltpu.make_async_copy(outer_hbm, outer_buf, weight_sems.at[0])
    inner_copy = pltpu.make_async_copy(inner_hbm, inner_buf, weight_sems.at[1])
    loads = copies(got_hbm, got_buf, got_sems, tile, 2)
    sent_stores = copies(sent_buf, sent_hbm, sent_sems, tile, 2)
    hidden_stores = copies(hidden_buf, hidden_hbm, hidden_sems, tile, 1)
    grad_pre_stores = copies(grad_pre_buf, grad_pre_hbm, grad_pre_sems, tile, 1)
    outer_copy.start()
    inner_copy.start()
    begin(loads)
    outer_copy.wait()
    fill_outer_t(outer_buf, outer_wide_t)
    fill_outer(outer_buf, outer_wide)
    inner_copy.wait()
    fill_inner_t(inner_buf, inner_wide_t)
    fill_inner(inner_buf, inner_wide)
    for i in range(TILES):
        lanes = slice(tile * i, tile * i + tile)
        loads[i].wait()
        pre_ref[...] = dot(outer_wide_t[...], rows(got_buf[:, 0:16, lanes]), 1, 0)
        for top in range(0, 512, ROWS):
            band = slice(top, top + ROWS)
            pre = pre_ref[band, :]
            square = pre * pre
            bent = jnp.tanh(pre * (GELU_SCALE + (GELU_SCALE * GELU_CUBE) * square))
            half = 0.5 + 0.5 * bent
            hidden_buf[band, lanes] = (pre * half).astype(BF)
            rise = 0.5 * GELU_SCALE + (1.5 * GELU_SCALE * GELU_CUBE) * square
            slope_ref[band, :] = half + pre * (1.0 - bent * bent) * rise
        hidden_stores[i].start()
        mid = dot(inner_wide_t[...], hidden_buf[:, lanes], 1, 0).astype(BF)
        sent_buf[:, 0:16, lanes] = mid.reshape(32, 16, tile)
        grad_hidden = dot(inner_wide[...], rows(got_buf[:, 16:32, lanes]), 1, 0)
        grad_pre_buf[:, lanes] = (grad_hidden * slope_ref[...]).astype(BF)
        grad_pre_stores[i].start()
        grad_perm = dot(outer_wide[...], grad_pre_buf[:, lanes], 1, 0).astype(BF)
        sent_buf[:, 16:32, lanes] = grad_perm.reshape(32, 16, tile)
        sent_stores[i].start()
    finish(hidden_stores)
    finish(grad_pre_stores)
    finish(sent_stores)


def picked(total_ref, by_j):
    row = lax.broadcasted_iota(jnp.int32, (512, 128), 0)
    mine = (row // 4) % 4 if by_j else row % 4
    value = total_ref[:, 0:128]
    for block in range(1, 4):
        value = jnp.where(mine == block, total_ref[:, 128 * block:128 * block + 128], value)
    return value


def write_outer(total_ref, picked_ref, block_ref, out_ref, at):
    picked_ref[...] = picked(total_ref, True)
    for j in range(4):
        for b in range(4):
            block_ref[pl.ds(b, 32, stride=4), :] = picked_ref[pl.ds(4 * j + b, 32, stride=16), :]
        for rank in range(8):
            out_ref[rank, at + 16 * j:at + 16 * j + 16, :] = block_ref[16 * rank:16 * rank + 16, :].astype(out_ref.dtype)


def write_inner(total_ref, picked_ref, out_ref, at):
    picked_ref[...] = picked(total_ref, False)
    for b in range(4):
        block = picked_ref[pl.ds(b, 128, stride=4), :].T.astype(out_ref.dtype)
        for rank in range(8):
            out_ref[rank, at + 16 * b:at + 16 * b + 16, :] = block[16 * rank:16 * rank + 16, :]


def add(total_ref, value, start):
    if start:
        total_ref[...] = value
    else:
        total_ref[...] += value


def grads_kernel(
    dims, outer_part, inner_part, got_hbm, outer_other_hbm, inner_other_hbm, out_ref,
    got_buf, outer_other, inner_other, outer_total, inner_total, picked_ref, block_ref,
    got_sems, outer_sems, inner_sems,
):
    tile = got_buf.shape[2] // TILES
    loads = copies(got_hbm, got_buf, got_sems, tile, 2)
    outer_loads = copies(outer_other_hbm, outer_other, outer_sems, tile, dims[1])
    inner_loads = copies(inner_other_hbm, inner_other, inner_sems, tile, dims[1])
    for i in range(TILES):
        begin([loads[i], outer_loads[i], inner_loads[i]])
    for i in range(TILES):
        lanes = slice(tile * i, tile * i + tile)
        finish([loads[i], outer_loads[i], inner_loads[i]])
        at = (slice(None), lanes) if dims[1] else (lanes, slice(None))
        outer_rows = rows(got_buf[:, 16 * outer_part:16 * outer_part + 16, lanes])
        inner_rows = rows(got_buf[:, 16 * inner_part:16 * inner_part + 16, lanes])
        add(outer_total, dot(outer_rows, outer_other[at], *dims), i == 0)
        add(inner_total, dot(inner_rows, inner_other[at], *dims), i == 0)
    write_outer(outer_total, picked_ref, block_ref, out_ref, 0)
    write_inner(inner_total, picked_ref, out_ref, 64)


def tail_kernel(got_ref, outer_ref, inner_ref, output_ref, input_grad_ref, outer_wide, inner_wide):
    @pl.when(pl.program_id(0) == 0)
    def _():
        fill_outer(outer_ref, outer_wide)
        fill_inner_t(inner_ref, inner_wide)

    output_ref[...] = dot(rows(got_ref[:, 0:16, :]), outer_wide[...], 0, 0).astype(BF)
    input_grad_ref[...] = dot(rows(got_ref[:, 16:32, :]), inner_wide[...], 0, 0).astype(BF)


def call(kernel, name, args, outs, specs, out_specs, scratch, flops, grid=()):
    moved = sum(a.size * a.dtype.itemsize for a in args)
    moved += sum(o.size * o.dtype.itemsize for o in outs)
    return pl.pallas_call(
        kernel,
        grid=grid,
        in_specs=specs,
        out_specs=out_specs,
        out_shape=outs,
        scratch_shapes=scratch,
        name=name,
        cost_estimate=pl.CostEstimate(flops=flops, bytes_accessed=moved, transcendentals=0),
        compiler_params=pltpu.CompilerParams(vmem_limit_bytes=60 * 1024 * 1024),
    )(*args)


def body(tokens, inner_one, outer_one, inner_two, outer_two, cotangent):
    tok = tokens.shape[0]
    one = 2 * tok * 512 * 512
    shape = jax.ShapeDtypeStruct
    hbm = pl.BlockSpec(memory_space=pl.ANY)
    message = shape((32, 32, tok), BF)
    feature = shape((512, tok), BF)
    token_out = shape((tok, 512), BF)
    weight = pltpu.VMEM((4, 128, 128), BF)
    by_token = pltpu.VMEM((tok, 512), BF)
    by_feature = pltpu.VMEM((512, tok), BF)
    by_message = pltpu.VMEM((32, 32, tok), BF)
    wide = pltpu.VMEM((512, 512), BF)
    total = pltpu.VMEM((512, 512), F32)
    tile_f32 = pltpu.VMEM((512, tok // TILES), F32)
    pair = pltpu.SemaphoreType.DMA((2,))
    sems = pltpu.SemaphoreType.DMA((TILES,))

    def exchange(value, axis):
        return lax.all_to_all(value, axis, split_axis=0, concat_axis=0, tiled=True)

    def grads(got, outer_part, outer_other, inner_part, inner_other, dims, kind, name):
        buf = by_feature if dims[1] else by_token
        return call(
            lambda *refs: grads_kernel(dims, outer_part, inner_part, *refs), name,
            (got, outer_other, inner_other), [shape((8, 128, 128), kind)], [hbm] * 3,
            [pl.BlockSpec(memory_space=pltpu.VMEM)],
            [by_message, buf, buf, total, total, pltpu.VMEM((512, 128), F32), pltpu.VMEM((128, 128), F32), sems, sems, sems],
            2 * one,
        )[0]

    sent = call(
        head_kernel, "head", (tokens, cotangent, inner_one, outer_two), [message], [hbm] * 4, [hbm],
        [by_token, by_token, weight, weight, by_message, wide, wide, pair, sems, sems, sems, sems], 2 * one,
    )[0]
    got = exchange(sent, "mp")
    sent_two, hidden, grad_pre = call(
        middle_kernel, "middle", (got, outer_one, inner_two), [message, feature, feature], [hbm] * 3, [hbm] * 3,
        [by_message, weight, weight, by_message, by_feature, by_feature, tile_f32, tile_f32,
         wide, wide, wide, wide, pair, sems, sems, sems, sems], 4 * one,
    )
    got_two = exchange(sent_two, "mp")
    early = grads(got, 0, grad_pre, 1, hidden, (1, 1), F32, "early_grads")
    early = lax.psum_scatter(early, "dp", scatter_dimension=0, tiled=True)
    late = exchange(grads(got_two, 0, cotangent, 1, tokens, (1, 0), BF, "late_grads"), "dp")
    step = tok // 2
    weights = pl.BlockSpec((4, 128, 128), lambda i: (0, 0, 0))
    tokens_at = pl.BlockSpec((step, 512), lambda i: (i, 0))
    output, input_grad = call(
        tail_kernel, "tail", (got_two, outer_two, inner_one), [token_out, token_out],
        [pl.BlockSpec((32, 32, step), lambda i: (0, 0, i)), weights, weights], [tokens_at, tokens_at],
        [wide, wide], 2 * one, (2,),
    )
    return (
        output,
        input_grad,
        jnp.sum(late[:, 64:], axis=0, dtype=F32).reshape(4, 16, 128),
        early[0, :64].reshape(4, 16, 128),
        early[0, 64:].reshape(4, 16, 128),
        jnp.sum(late[:, :64], axis=0, dtype=F32).reshape(4, 16, 128),
    )


def solution(mesh):
    placed = (
        P("dp", "mp"),
        P("mp", None, None),
        P("mp", None, None),
        P("mp", None, None),
        P("mp", None, None),
        P("dp", "mp"),
    )
    return jax.shard_map(
        body,
        mesh=mesh,
        in_specs=placed,
        out_specs=(
            P("dp", "mp"),
            P("dp", "mp"),
            P("mp", "dp", None),
            P("mp", "dp", None),
            P("mp", "dp", None),
            P("mp", "dp", None),
        ),
        check_vma=False,
    )
```

time: 198 us -> 172 us (0.87)
  blocking collectives: 0 us -> 56.3 us
  waiting for transfers between devices: 80.9 us -> 48.9 us
  starting transfers between devices: 39.1 us -> 15.8 us
  Pallas kernels: 55 us -> 32.8 us
  local copies, waits for them, and re-layouts: 4.11 us -> 1.4 us
    all_to_all x0 -> x1, blocking collectives: none -> 56.3 us  [exchange(): return lax.all_to_all(value, axis, split_axis=0, concat_axis=0, tiled=True)]
    all_to_all x5 -> x2, starting transfers between devices: 39 us -> 15.5 us  [exchange(): return lax.all_to_all(value, axis, split_axis=0, concat_axis=0, tiled=True)]
    pallas_call x10 -> x5, Pallas kernels: 55 us -> 32.8 us  [call(): pl.pallas_call(kernel, grid=grid, in_specs=specs, out_specs=out_specs, ou...]
    reduce_scatter x1, waiting for transfers between devices: 17 us -> 0.01 us  [body(): early = lax.psum_scatter(early, 'dp', scatter_dimension=0, tiled=True)]
    all_to_all x5 -> x2, waiting for transfers between devices: 64 us -> 48.8 us  [exchange(): return lax.all_to_all(value, axis, split_axis=0, concat_axis=0, tiled=True)]
    unnamed x10 -> x0, local copies, waits for them, and re-layouts: 2.68 us -> none
  transfers between devices with their start and end apart: 6 -> 3, of which waited for: 5 -> 2; matrix products, arithmetic and copies ran while one was open for 2% -> 1% of each run, Pallas kernels for 26% -> 9%
where the time goes in v2:
time: 172 us; the launch traced here: 170 us
  blocking collectives  56.3 us (33%)
  waiting for transfers between devices  48.9 us (28%)
  Pallas kernels  32.8 us (19%)
  starting transfers between devices  15.8 us (9%)
  between operations  14.1 us (8%)
    all_to_all x1, blocking collectives, exchange(): return lax.all_to_all(value, axis, split_axis=0, concat_axis=0, tiled=True)  56.3 us
    all_to_all x2, waiting for transfers between devices, exchange(): return lax.all_to_all(value, axis, split_axis=0, concat_axis=0, tiled=True)  48.8 us
    pallas_call x5, Pallas kernels, call(): pl.pallas_call(kernel, grid=grid, in_specs=specs, out_specs=out_specs, ou...  32.8 us
    all_to_all x2, starting transfers between devices, exchange(): return lax.all_to_all(value, axis, split_axis=0, concat_axis=0, tiled=True)  15.5 us
  transfers between devices with their start and end apart: 3, of which 2 were waited for; matrix products, arithmetic and copies ran while one was open for 1% of the time, Pallas kernels for 9%

profile of v2, /device:TPU:8, one launch (start us, length us, event | category | flops | bytes accessed | tf_op | source)
XLA Modules:
  0.0 170.0 jit_solution(10973502986174809702)
XLA Ops:
  7.2 6.9 %head.1 = bf16[32,32,2048]{2,1,0:T(8,128)(2,1)} custom-call(bf16[2048,512]{1,0:T(8,128)(2,1)} %refs_2_.1, bf16[2048,512]{1,0:T(8,128)(2,1)} %refs_1_.1, bf16[4,128,128]{2,1,0:T(8,128)(2,1)} %inner_ref.1, bf16[4,128,128]{2,1,0:T(8,128)(2,1)} %outer_ref.1), custom_call_target="tpu_custom_call" | custom-call | flops 2147483648 | bytes 8650752 | tf_op jit(solution)/shard_map/head/pallas_call | solution.py:240
  14.1 56.3 %all_to_all.15.got_hbm.refs_0_ = bf16[32,32,2048]{2,1,0:T(8,128)(2,1)} all-to-all(bf16[32,32,2048]{2,1,0:T(8,128)(2,1)} %head.1), channel_id=1, replica_groups=mesh['dp'=8,'mp'=32] {'mp'}, dimensions={0} | all-to-all | bytes 8388608 | tf_op jit(solution)/shard_map/all_to_all | solution.py:272
  70.5 10.0 %middle.1 = (bf16[32,32,2048]{2,1,0:T(8,128)(2,1)}, bf16[512,2048]{1,0:T(8,128)(2,1)}, bf16[512,2048]{1,0:T(8,128)(2,1)}) custom-call(bf16[32,32,2048]{2,1,0:T(8,128)(2,1)} %all_to_all.15.got_hbm.refs_0_, bf16[4,128,128]{2,1,0:T(8,128)(2,1)} %outer_hbm.3, bf16[4,128,128]{2,1,0:T(8,128)(2,1)} %inner_hbm.3), custom_call_target="tpu_custom_call" | custom-call | flops 4294967296 | bytes 12845056 | tf_op jit(solution)/shard_map/middle/pallas_call | solution.py:240
  80.5 7.1 %all-to-all-start.1 = ((bf16[32,32,2048]{2,1,0:T(8,128)(2,1)}), bf16[32,32,2048]{2,1,0:T(8,128)(2,1)}, u32[]{:S(2)}, u32[]{:S(2)}) async-start(bf16[32,32,2048]{2,1,0:T(8,128)(2,1)} %get-tuple-element.11), calls=%async_computation.1 | async-start | bytes 8388608 | tf_op jit(solution)/shard_map/all_to_all | solution.py:272
  87.5 0.2 reduce-scatter.2.cloned.1.call-start
  87.8 5.3 %early_grads.1 = f32[8,128,128]{2,1,0:T(8,128)} custom-call(bf16[32,32,2048]{2,1,0:T(8,128)(2,1)} %all_to_all.15.got_hbm.refs_0_, bf16[512,2048]{1,0:T(8,128)(2,1)} %get-tuple-element.14.refs_1_, bf16[512,2048]{1,0:T(8,128)(2,1)} %get-tuple-element.15.refs_2_), custom_call_target="tpu_custom_call" | custom-call | flops 2147483648 | bytes 8912896 | tf_op jit(solution)/shard_map/early_grads/pallas_call | solution.py:240
  93.0 0.0 reduce-scatter.2.cloned.1.call-update
  93.1 45.1 %all-to-all-done.1.got_ref.refs_0_ = bf16[32,32,2048]{2,1,0:T(8,128)(2,1)} async-done(((bf16[32,32,2048]{2,1,0:T(8,128)(2,1)}), bf16[32,32,2048]{2,1,0:T(8,128)(2,1)}, u32[]{:S(2)}, u32[]{:S(2)}) %all-to-all-start.1) | async-done | bytes 4194336 | tf_op jit(solution)/shard_map/all_to_all | solution.py:272
  138.1 5.0 %late_grads.1 = bf16[8,128,128]{2,1,0:T(8,128)(2,1)} custom-call(bf16[32,32,2048]{2,1,0:T(8,128)(2,1)} %all-to-all-done.1.got_ref.refs_0_, bf16[2048,512]{1,0:T(8,128)(2,1)} %refs_1_.1, bf16[2048,512]{1,0:T(8,128)(2,1)} %refs_2_.1), custom_call_target="tpu_custom_call" | custom-call | flops 2147483648 | bytes 8650752 | tf_op jit(solution)/shard_map/late_grads/pallas_call | solution.py:240
  143.2 8.5 %all-to-all-start.2 = ((bf16[8,128,128]{2,1,0:T(8,128)(2,1)}), bf16[8,128,128]{2,1,0:T(8,128)(2,1)S(1)}, u32[]{:S(2)}, u32[]{:S(2)}) async-start(bf16[8,128,128]{2,1,0:T(8,128)(2,1)} %late_grads.1), calls=%async_computation.2 | async-start | bytes 524288 | tf_op jit(solution)/shard_map/all_to_all | solution.py:272
  151.7 0.0 reduce-scatter.2.cloned.1.call-done
  151.7 1.4 fusion
  153.1 5.6 %tail.1 = (bf16[2048,512]{1,0:T(8,128)(2,1)}, bf16[2048,512]{1,0:T(8,128)(2,1)}) custom-call(bf16[32,32,2048]{2,1,0:T(8,128)(2,1)} %all-to-all-done.1.got_ref.refs_0_, bf16[4,128,128]{2,1,0:T(8,128)(2,1)} %outer_ref.1, bf16[4,128,128]{2,1,0:T(8,128)(2,1)} %inner_ref.1), custom_call_target="tpu_custom_call" | custom-call | flops 2147483648 | bytes 8650752 | tf_op jit(solution)/shard_map/tail/pallas_call | solution.py:240
  158.7 3.8 %all-to-all-done.2 = bf16[8,128,128]{2,1,0:T(8,128)(2,1)S(1)} async-done(((bf16[8,128,128]{2,1,0:T(8,128)(2,1)}), bf16[8,128,128]{2,1,0:T(8,128)(2,1)S(1)}, u32[]{:S(2)}, u32[]{:S(2)}) %all-to-all-start.2) | async-done | bytes 262176 | tf_op jit(solution)/shard_map/all_to_all | solution.py:272
  162.5 0.7 convert_reduce_fusion
Async XLA Ops:
  80.5 57.7 %all-to-all-start.1 = ((bf16[32,32,2048]{2,1,0:T(8,128)(2,1)}), bf16[32,32,2048]{2,1,0:T(8,128)(2,1)}, u32[]{:S(2)}, u32[]{:S(2)}) async-start(bf16[32,32,2048]{2,1,0:T(8,128)(2,1)} %get-tuple-element.11), calls=%async_computation.1 | async-start | bytes 8388608 | tf_op jit(solution)/shard_map/all_to_all | solution.py:272
  87.5 64.1 %reduce-scatter.2.cloned.1.call-start = ((), (), s32[]{:S(2)}) async-start(), calls=%async_computation.4 | async-start | bytes 589824 | tf_op jit(solution)/shard_map/reduce_scatter | solution.py:296
  143.2 19.3 %all-to-all-start.2 = ((bf16[8,128,128]{2,1,0:T(8,128)(2,1)}), bf16[8,128,128]{2,1,0:T(8,128)(2,1)S(1)}, u32[]{:S(2)}, u32[]{:S(2)}) async-start(bf16[8,128,128]{2,1,0:T(8,128)(2,1)} %late_grads.1), calls=%async_computation.2 | async-start | bytes 524288 | tf_op jit(solution)/shard_map/all_to_all | solution.py:272
Sparse Core Ops, SparseCore 0:
  93.2 40.0 reduce-scatter.1

commit v3 on v2

--- a/solution.py
+++ b/solution.py
@@ -177,21 +177,25 @@
     return value
 
 
-def write_outer(total_ref, picked_ref, block_ref, out_ref, at):
+def spread_out(block_ref, slots, at):
+    for rank, out_ref in slots:
+        first_row = 16 * rank if isinstance(rank, int) else pl.multiple_of(16 * rank, 16)
+        out_ref[at:at + 16, :] = block_ref[pl.ds(first_row, 16), :].astype(out_ref.dtype)
+
+
+def write_outer(total_ref, picked_ref, block_ref, slots, at):
     picked_ref[...] = picked(total_ref, True)
     for j in range(4):
         for b in range(4):
             block_ref[pl.ds(b, 32, stride=4), :] = picked_ref[pl.ds(4 * j + b, 32, stride=16), :]
-        for rank in range(8):
-            out_ref[rank, at + 16 * j:at + 16 * j + 16, :] = block_ref[16 * rank:16 * rank + 16, :].astype(out_ref.dtype)
-
-
-def write_inner(total_ref, picked_ref, out_ref, at):
+        spread_out(block_ref, slots, at + 16 * j)
+
+
+def write_inner(total_ref, picked_ref, block_ref, slots, at):
     picked_ref[...] = picked(total_ref, False)
     for b in range(4):
-        block = picked_ref[pl.ds(b, 128, stride=4), :].T.astype(out_ref.dtype)
-        for rank in range(8):
-            out_ref[rank, at + 16 * b:at + 16 * b + 16, :] = block[16 * rank:16 * rank + 16, :]
+        block_ref[...] = picked_ref[pl.ds(b, 128, stride=4), :].T
+        spread_out(block_ref, slots, at + 16 * b)
 
 
 def add(total_ref, value, start):
@@ -202,10 +206,15 @@
 
 
 def grads_kernel(
-    dims, outer_part, inner_part, got_hbm, outer_other_hbm, inner_other_hbm, out_ref,
-    got_buf, outer_other, inner_other, outer_total, inner_total, picked_ref, block_ref,
-    got_sems, outer_sems, inner_sems,
+    dims, outer_part, inner_part, got_hbm, outer_other_hbm, inner_other_hbm, mine_ref, *refs
 ):
+    if len(refs) == 11:
+        slots = [(rank, refs[0].at[rank]) for rank in range(8)]
+    else:
+        order = [(0, 0), (1, 0), (2, 0), (2, 128), (3, 0), (3, 128), (3, 256), (3, 384)]
+        slots = [(mine_ref[0] ^ i, refs[out].at[pl.ds(row, 128), :]) for i, (out, row) in enumerate(order)]
+    got_buf, outer_other, inner_other, outer_total, inner_total = refs[-10:-5]
+    picked_ref, block_ref, got_sems, outer_sems, inner_sems = refs[-5:]
     tile = got_buf.shape[2] // TILES
     loads = copies(got_hbm, got_buf, got_sems, tile, 2)
     outer_loads = copies(outer_other_hbm, outer_other, outer_sems, tile, dims[1])
@@ -220,8 +229,8 @@
         inner_rows = rows(got_buf[:, 16 * inner_part:16 * inner_part + 16, lanes])
         add(outer_total, dot(outer_rows, outer_other[at], *dims), i == 0)
         add(inner_total, dot(inner_rows, inner_other[at], *dims), i == 0)
-    write_outer(outer_total, picked_ref, block_ref, out_ref, 0)
-    write_inner(inner_total, picked_ref, out_ref, 64)
+    write_outer(outer_total, picked_ref, block_ref, slots, 0)
+    write_inner(inner_total, picked_ref, block_ref, slots, 64)
 
 
 def tail_kernel(got_ref, outer_ref, inner_ref, output_ref, input_grad_ref, outer_wide, inner_wide):
@@ -253,6 +262,7 @@
 def body(tokens, inner_one, outer_one, inner_two, outer_two, cotangent):
     tok = tokens.shape[0]
     one = 2 * tok * 512 * 512
+    mine = lax.axis_index("dp").astype(jnp.int32).reshape(1)
     shape = jax.ShapeDtypeStruct
     hbm = pl.BlockSpec(memory_space=pl.ANY)
     message = shape((32, 32, tok), BF)
@@ -271,15 +281,19 @@
     def exchange(value, axis):
         return lax.all_to_all(value, axis, split_axis=0, concat_axis=0, tiled=True)
 
-    def grads(got, outer_part, outer_other, inner_part, inner_other, dims, kind, name):
+    def across(value, flip):
+        return lax.ppermute(value, "dp", [(rank, rank ^ flip) for rank in range(8)])
+
+    def grads(got, outer_part, outer_other, inner_part, inner_other, dims, outs, name):
         buf = by_feature if dims[1] else by_token
         return call(
             lambda *refs: grads_kernel(dims, outer_part, inner_part, *refs), name,
-            (got, outer_other, inner_other), [shape((8, 128, 128), kind)], [hbm] * 3,
-            [pl.BlockSpec(memory_space=pltpu.VMEM)],
+            (got, outer_other, inner_other, mine), outs,
+            [hbm] * 3 + [pl.BlockSpec(memory_space=pltpu.SMEM)],
+            [pl.BlockSpec(memory_space=pltpu.VMEM)] * len(outs),
             [by_message, buf, buf, total, total, pltpu.VMEM((512, 128), F32), pltpu.VMEM((128, 128), F32), sems, sems, sems],
             2 * one,
-        )[0]
+        )
 
     sent = call(
         head_kernel, "head", (tokens, cotangent, inner_one, outer_two), [message], [hbm] * 4, [hbm],
@@ -292,9 +306,14 @@
          wide, wide, wide, wide, pair, sems, sems, sems, sems], 4 * one,
     )
     got_two = exchange(sent_two, "mp")
-    early = grads(got, 0, grad_pre, 1, hidden, (1, 1), F32, "early_grads")
-    early = lax.psum_scatter(early, "dp", scatter_dimension=0, tiled=True)
-    late = exchange(grads(got_two, 0, cotangent, 1, tokens, (1, 0), BF, "late_grads"), "dp")
+    own, near, middle, far = grads(
+        got, 0, grad_pre, 1, hidden, (1, 1), [shape((128 * n, 128), F32) for n in (1, 1, 2, 4)], "early_grads"
+    )
+    halves = across(far, 4)
+    quarters = across(middle + halves[256:], 2)
+    eighth = across(near + halves[128:256] + quarters[128:], 1)
+    late = grads(got_two, 0, cotangent, 1, tokens, (1, 0), [shape((8, 128, 128), BF)], "late_grads")[0]
+    late = exchange(late, "dp")
     step = tok // 2
     weights = pl.BlockSpec((4, 128, 128), lambda i: (0, 0, 0))
     tokens_at = pl.BlockSpec((step, 512), lambda i: (i, 0))
@@ -307,8 +326,8 @@
         output,
         input_grad,
         jnp.sum(late[:, 64:], axis=0, dtype=F32).reshape(4, 16, 128),
-        early[0, :64].reshape(4, 16, 128),
-        early[0, 64:].reshape(4, 16, 128),
+        (own[:64] + halves[:64] + quarters[:64] + eighth[:64]).reshape(4, 16, 128),
+        (own[64:] + halves[64:128] + quarters[64:128] + eighth[64:]).reshape(4, 16, 128),
         jnp.sum(late[:, :64], axis=0, dtype=F32).reshape(4, 16, 128),
     )
 

time: 172 us -> 159 us (0.924)
  waiting for transfers between devices: 48.9 us -> 34.1 us
  starting transfers between devices: 15.8 us -> 29.4 us
  between operations: 14.1 us -> 0.71 us
  other arithmetic: 0.66 us -> 3.07 us
    all_to_all x2, waiting for transfers between devices: 48.8 us -> 20.4 us  [exchange(): return lax.all_to_all(value, axis, split_axis=0, concat_axis=0, tiled=True)]
    ppermute x0 -> x3, starting transfers between devices: none -> 13.9 us  [across(): return lax.ppermute(value, 'dp', [(rank, rank ^ flip) for rank in range(8)])]
    ppermute x0 -> x3, waiting for transfers between devices: none -> 13.8 us  [across(): return lax.ppermute(value, 'dp', [(rank, rank ^ flip) for rank in range(8)])]
    add x0 -> x3, other arithmetic: none -> 2.41 us  [the longest x1 0.92 us: body(): quarters = across(middle + halves[256:], 2)]
  transfers between devices with their start and end apart: 3 -> 5, of which waited for: 2 -> 4; matrix products, arithmetic and copies ran while one was open for 1% -> 2% of each run, Pallas kernels for 9% -> 10%
where the time goes in v3:
time: 159 us; the launch traced here: 157 us
  blocking collectives  56.3 us (35%)
  waiting for transfers between devices  34.1 us (21%)
  Pallas kernels  32.9 us (21%)
  starting transfers between devices  29.4 us (18%)
  other arithmetic  3.07 us (2%)
    all_to_all x1, blocking collectives, exchange(): return lax.all_to_all(value, axis, split_axis=0, concat_axis=0, tiled=True)  56.3 us
    pallas_call x5, Pallas kernels, call(): pl.pallas_call(kernel, grid=grid, in_specs=specs, out_specs=out_specs, ou...  32.9 us
    all_to_all x2, waiting for transfers between devices, exchange(): return lax.all_to_all(value, axis, split_axis=0, concat_axis=0, tiled=True)  20.4 us
    all_to_all x2, starting transfers between devices, exchange(): return lax.all_to_all(value, axis, split_axis=0, concat_axis=0, tiled=True)  15.6 us
    ppermute x3, starting transfers between devices, across(): return lax.ppermute(value, 'dp', [(rank, rank ^ flip) for rank in range(8)])  13.9 us
    ppermute x3, waiting for transfers between devices, across(): return lax.ppermute(value, 'dp', [(rank, rank ^ flip) for rank in range(8)])  13.8 us
  transfers between devices with their start and end apart: 5, of which 4 were waited for; matrix products, arithmetic and copies ran while one was open for 2% of the time, Pallas kernels for 10%

profile of v3, /device:TPU:8, one launch (start us, length us, event | category | flops | bytes accessed | tf_op | source)
XLA Modules:
  0.0 156.6 jit_solution(9419300165312135885)
XLA Ops:
  0.6 6.9 %head.1 = bf16[32,32,2048]{2,1,0:T(8,128)(2,1)} custom-call(bf16[2048,512]{1,0:T(8,128)(2,1)} %refs_2_.1, bf16[2048,512]{1,0:T(8,128)(2,1)} %refs_1_.1, bf16[4,128,128]{2,1,0:T(8,128)(2,1)} %inner_ref.1, bf16[4,128,128]{2,1,0:T(8,128)(2,1)} %outer_ref.1), custom_call_target="tpu_custom_call" | custom-call | flops 2147483648 | bytes 8650752 | tf_op jit(solution)/shard_map/head/pallas_call | solution.py:249
  7.6 56.3 %all_to_all.15.got_hbm.refs_0_ = bf16[32,32,2048]{2,1,0:T(8,128)(2,1)} all-to-all(bf16[32,32,2048]{2,1,0:T(8,128)(2,1)} %head.1), channel_id=1, replica_groups=mesh['dp'=8,'mp'=32] {'mp'}, dimensions={0} | all-to-all | bytes 8388608 | tf_op jit(solution)/shard_map/all_to_all | solution.py:282
  63.9 10.0 %middle.1 = (bf16[32,32,2048]{2,1,0:T(8,128)(2,1)}, bf16[512,2048]{1,0:T(8,128)(2,1)}, bf16[512,2048]{1,0:T(8,128)(2,1)}) custom-call(bf16[32,32,2048]{2,1,0:T(8,128)(2,1)} %all_to_all.15.got_hbm.refs_0_, bf16[4,128,128]{2,1,0:T(8,128)(2,1)} %outer_hbm.3, bf16[4,128,128]{2,1,0:T(8,128)(2,1)} %inner_hbm.3), custom_call_target="tpu_custom_call" | custom-call | flops 4294967296 | bytes 12845056 | tf_op jit(solution)/shard_map/middle/pallas_call | solution.py:249
  73.9 7.1 %all-to-all-start.1 = ((bf16[32,32,2048]{2,1,0:T(8,128)(2,1)}), bf16[32,32,2048]{2,1,0:T(8,128)(2,1)}, u32[]{:S(2)}, u32[]{:S(2)}) async-start(bf16[32,32,2048]{2,1,0:T(8,128)(2,1)} %get-tuple-element.15), calls=%async_computation.1 | async-start | bytes 8388608 | tf_op jit(solution)/shard_map/all_to_all | solution.py:282
  81.0 5.3 %early_grads.1 = (f32[128,128]{1,0:T(8,128)}, f32[128,128]{1,0:T(8,128)}, f32[256,128]{1,0:T(8,128)}, f32[512,128]{1,0:T(8,128)}) custom-call(bf16[32,32,2048]{2,1,0:T(8,128)(2,1)} %all_to_all.15.got_hbm.refs_0_, bf16[512,2048]{1,0:T(8,128)(2,1)} %get-tuple-element.18.refs_1_, bf16[512,2048]{1,0:T(8,128)(2,1)} %get-tuple-element.19.refs_2_, s32[1]{0:T(128)} %bitcast.refs_3_), custom_call_target="tpu_custom_call" | custom-call | flops 2147483648 | bytes 8912900 | tf_op jit(solution)/shard_map/early_grads/pallas_call | solution.py:249
  86.4 7.3 %collective-permute-start = (f32[512,128]{1,0:T(8,128)}, f32[512,128]{1,0:T(8,128)S(1)}, u32[]{:S(2)}, u32[]{:S(2)}) collective-permute-start(f32[512,128]{1,0:T(8,128)} %get-tuple-element.21), channel_id=1, source_target_pairs={{0,128},{32,160},{64,192},{96,224},{128,0},{160,32},{192,64},{224,... | collective-permute-start | bytes 786440 | tf_op jit(solution)/shard_map/ppermute | solution.py:285
  93.6 8.0 %collective-permute-done = f32[512,128]{1,0:T(8,128)S(1)} collective-permute-done((f32[512,128]{1,0:T(8,128)}, f32[512,128]{1,0:T(8,128)S(1)}, u32[]{:S(2)}, u32[]{:S(2)}) %collective-permute-start) | collective-permute-done | bytes 262176 | tf_op jit(solution)/shard_map/ppermute | solution.py:285
  101.6 0.9 slice_add_fusion
  102.5 6.5 %collective-permute-start.1 = (f32[256,128]{1,0:T(8,128)S(1)}, f32[256,128]{1,0:T(8,128)S(1)}, u32[]{:S(2)}, u32[]{:S(2)}) collective-permute-start(f32[256,128]{1,0:T(8,128)S(1)} %slice_add_fusion), channel_id=1, source_target_pairs={{0,64},{32,96},{64,0},{96,32},{128,192},{160,224},{192,128},{224,1... | collective-permute-start | bytes 393224 | tf_op jit(solution)/shard_map/ppermute | solution.py:285
  109.0 5.8 %collective-permute-done.1 = f32[256,128]{1,0:T(8,128)S(1)} collective-permute-done((f32[256,128]{1,0:T(8,128)S(1)}, f32[256,128]{1,0:T(8,128)S(1)}, u32[]{:S(2)}, u32[]{:S(2)}) %collective-permute-start.1) | collective-permute-done | bytes 131104 | tf_op jit(solution)/shard_map/ppermute | solution.py:285
  114.8 0.9 slice_add_fusion.1
  115.7 0.0 copy-start
  115.7 0.1 collective-permute-start.2
  115.8 15.7 %all-to-all-done.1.got_ref.refs_0_ = bf16[32,32,2048]{2,1,0:T(8,128)(2,1)} async-done(((bf16[32,32,2048]{2,1,0:T(8,128)(2,1)}), bf16[32,32,2048]{2,1,0:T(8,128)(2,1)}, u32[]{:S(2)}, u32[]{:S(2)}) %all-to-all-start.1) | async-done | bytes 4194336 | tf_op jit(solution)/shard_map/all_to_all | solution.py:282
  131.4 5.1 %late_grads.1 = bf16[8,128,128]{2,1,0:T(8,128)(2,1)} custom-call(bf16[32,32,2048]{2,1,0:T(8,128)(2,1)} %all-to-all-done.1.got_ref.refs_0_, bf16[2048,512]{1,0:T(8,128)(2,1)} %refs_1_.1, bf16[2048,512]{1,0:T(8,128)(2,1)} %refs_2_.1, s32[1]{0:T(128)} %bitcast.refs_3_), custom_call_target="tpu_custom_call" | custom-call | flops 2147483648 | bytes 8650756 | tf_op jit(solution)/shard_map/late_grads/pallas_call | solution.py:249
  136.5 8.5 %all-to-all-start.2 = ((bf16[8,128,128]{2,1,0:T(8,128)(2,1)}), bf16[8,128,128]{2,1,0:T(8,128)(2,1)S(1)}, u32[]{:S(2)}, u32[]{:S(2)}) async-start(bf16[8,128,128]{2,1,0:T(8,128)(2,1)} %late_grads.1), calls=%async_computation.2 | async-start | bytes 524288 | tf_op jit(solution)/shard_map/all_to_all | solution.py:282
  145.0 0.0 collective-permute-done.2
  145.0 0.0 copy-done
  145.0 0.6 slice_add_fusion.3
  145.6 5.6 %tail.1 = (bf16[2048,512]{1,0:T(8,128)(2,1)}, bf16[2048,512]{1,0:T(8,128)(2,1)}) custom-call(bf16[32,32,2048]{2,1,0:T(8,128)(2,1)} %all-to-all-done.1.got_ref.refs_0_, bf16[4,128,128]{2,1,0:T(8,128)(2,1)} %outer_ref.1, bf16[4,128,128]{2,1,0:T(8,128)(2,1)} %inner_ref.1), custom_call_target="tpu_custom_call" | custom-call | flops 2147483648 | bytes 8650752 | tf_op jit(solution)/shard_map/tail/pallas_call | solution.py:249
  151.2 4.7 %all-to-all-done.2 = bf16[8,128,128]{2,1,0:T(8,128)(2,1)S(1)} async-done(((bf16[8,128,128]{2,1,0:T(8,128)(2,1)}), bf16[8,128,128]{2,1,0:T(8,128)(2,1)S(1)}, u32[]{:S(2)}, u32[]{:S(2)}) %all-to-all-start.2) | async-done | bytes 262176 | tf_op jit(solution)/shard_map/all_to_all | solution.py:282
  155.9 0.7 convert_reduce_fusion
Async XLA Ops:
  73.9 57.6 %all-to-all-start.1 = ((bf16[32,32,2048]{2,1,0:T(8,128)(2,1)}), bf16[32,32,2048]{2,1,0:T(8,128)(2,1)}, u32[]{:S(2)}, u32[]{:S(2)}) async-start(bf16[32,32,2048]{2,1,0:T(8,128)(2,1)} %get-tuple-element.15), calls=%async_computation.1 | async-start | bytes 8388608 | tf_op jit(solution)/shard_map/all_to_all | solution.py:282
  86.4 15.2 %collective-permute-start = (f32[512,128]{1,0:T(8,128)}, f32[512,128]{1,0:T(8,128)S(1)}, u32[]{:S(2)}, u32[]{:S(2)}) collective-permute-start(f32[512,128]{1,0:T(8,128)} %get-tuple-element.21), channel_id=1, source_target_pairs={{0,128},{32,160},{64,192},{96,224},{128,0},{160,32},{192,64},{224,... | collective-permute-start | bytes 786440 | tf_op jit(solution)/shard_map/ppermute | solution.py:285
  102.5 12.3 %collective-permute-start.1 = (f32[256,128]{1,0:T(8,128)S(1)}, f32[256,128]{1,0:T(8,128)S(1)}, u32[]{:S(2)}, u32[]{:S(2)}) collective-permute-start(f32[256,128]{1,0:T(8,128)S(1)} %slice_add_fusion), channel_id=1, source_target_pairs={{0,64},{32,96},{64,0},{96,32},{128,192},{160,224},{192,128},{224,1... | collective-permute-start | bytes 393224 | tf_op jit(solution)/shard_map/ppermute | solution.py:285
  115.7 29.3 %copy-start = (f32[128,128]{1,0:T(8,128)S(1)}, f32[128,128]{1,0:T(8,128)}, u32[]{:S(2)}) copy-start(f32[128,128]{1,0:T(8,128)} %get-tuple-element.20) | copy-start | bytes 196612
  115.7 29.3 %collective-permute-start.2 = (f32[128,128]{1,0:T(8,128)S(1)}, f32[128,128]{1,0:T(8,128)S(1)}, u32[]{:S(2)}, u32[]{:S(2)}) collective-permute-start(f32[128,128]{1,0:T(8,128)S(1)} %slice_add_fusion.1), channel_id=1, source_target_pairs={{0,32},{32,0},{64,96},{96,64},{128,160},{160,128},{192,224},{224,1... | collective-permute-start | bytes 196616 | tf_op jit(solution)/shard_map/ppermute | solution.py:285
  136.5 19.4 %all-to-all-start.2 = ((bf16[8,128,128]{2,1,0:T(8,128)(2,1)}), bf16[8,128,128]{2,1,0:T(8,128)(2,1)S(1)}, u32[]{:S(2)}, u32[]{:S(2)}) async-start(bf16[8,128,128]{2,1,0:T(8,128)(2,1)} %late_grads.1), calls=%async_computation.2 | async-start | bytes 524288 | tf_op jit(solution)/shard_map/all_to_all | solution.py:282

commit v4 on v3

v4 whole, which is shorter than its diff:
```python
import jax
import jax.numpy as jnp
from jax import lax
from jax.experimental import pallas as pl
from jax.experimental.pallas import tpu as pltpu
from jax.sharding import PartitionSpec as P

BF = jnp.bfloat16
F32 = jnp.float32
GELU_SCALE = 0.7978845608028654
GELU_CUBE = 0.044715
TILES = 2
LATE_TILES = 4
ROWS = 64


def dot(left, right, left_dim, right_dim):
    return lax.dot_general(
        left, right, (((left_dim,), (right_dim,)), ((), ())), preferred_element_type=F32
    )


def inner_spread(block, wide, rows_wide):
    shape = (wide, 128) if rows_wide else (128, wide)
    row = lax.broadcasted_iota(jnp.int32, shape, 0)
    col = lax.broadcasted_iota(jnp.int32, shape, 1)
    hit = (row == 4 * col + block) if rows_wide else (col == 4 * row + block)
    return hit.astype(F32).astype(BF)


def outer_spread(block):
    row = lax.broadcasted_iota(jnp.int32, (512, 128), 0)
    col = lax.broadcasted_iota(jnp.int32, (512, 128), 1)
    hit = row == 16 * (col // 4) + 4 * block + col % 4
    return hit.astype(F32).astype(BF)


def fill_inner_t(weight_ref, wide_ref):
    for block in range(4):
        wide_ref[:, 128 * block:128 * block + 128] = dot(
            inner_spread(block, 512, True), weight_ref[block], 1, 1
        ).astype(BF)


def fill_inner(weight_ref, wide_ref):
    for block in range(4):
        wide_ref[128 * block:128 * block + 128, :] = dot(
            weight_ref[block], inner_spread(block, 512, False), 1, 0
        ).astype(BF)


def fill_outer(weight_ref, wide_ref):
    for block in range(4):
        wide_ref[:, 128 * block:128 * block + 128] = dot(
            outer_spread(block), weight_ref[block], 1, 0
        ).astype(BF)


def fill_outer_t(weight_ref, wide_ref):
    for block in range(4):
        wide_ref[128 * block:128 * block + 128, :] = dot(
            weight_ref[block], outer_spread(block), 0, 1
        ).astype(BF)


def rows(value):
    return value.reshape(512, value.shape[-1])


def copies(source, target, sems, tile, axis):
    out = []
    for i in range(source.shape[axis] // tile):
        at = (slice(None),) * axis + (pl.ds(tile * i, tile),)
        out.append(pltpu.make_async_copy(source.at[at], target.at[at], sems.at[i]))
    return out


def begin(many):
    for copy in many:
        copy.start()


def finish(many):
    for copy in many:
        copy.wait()


def load(pairs, sems):
    out = [pltpu.make_async_copy(source, target, sems.at[i]) for i, (source, target) in enumerate(pairs)]
    begin(out)
    return out


def head_kernel(
    x_hbm, g_hbm, inner_hbm, outer_hbm, sent_ref,
    x_buf, g_buf, inner_buf, outer_buf, inner_wide, outer_wide, weight_sems, x_sems, g_sems,
):
    tile = x_buf.shape[0] // TILES
    weights = load([(inner_hbm, inner_buf), (outer_hbm, outer_buf)], weight_sems)
    x_copies = copies(x_hbm, x_buf, x_sems, tile, 0)
    g_copies = copies(g_hbm, g_buf, g_sems, tile, 0)
    begin(x_copies)
    begin(g_copies)
    finish(weights)
    fill_inner_t(inner_buf, inner_wide)
    fill_outer(outer_buf, outer_wide)
    for part, wide, buf, arriving in ((0, inner_wide, x_buf, x_copies), (1, outer_wide, g_buf, g_copies)):
        for i in range(TILES):
            arriving[i].wait()
            mid = dot(wide[...], buf[tile * i:tile * i + tile, :], 1, 1).astype(BF)
            sent_ref[:, 16 * part:16 * part + 16, tile * i:tile * i + tile] = mid.reshape(32, 16, tile)


def activate(pre_ref, slope_ref, hidden_ref):
    for top in range(0, 512, ROWS):
        band = slice(top, top + ROWS)
        pre = pre_ref[band, :]
        square = pre * pre
        bent = jnp.tanh(pre * (GELU_SCALE + (GELU_SCALE * GELU_CUBE) * square))
        half = 0.5 + 0.5 * bent
        hidden_ref[band, :] = (pre * half).astype(BF)
        rise = 0.5 * GELU_SCALE + (1.5 * GELU_SCALE * GELU_CUBE) * square
        slope_ref[band, :] = half + pre * (1.0 - bent * bent) * rise


def middle_kernel(
    got_ref, outer_hbm, inner_hbm, sent_hbm, kept_hbm,
    outer_buf, inner_buf, sent_buf, pre_ref, slope_ref, hidden_ref, grad_pre_ref,
    outer_wide, outer_wide_t, inner_wide, inner_wide_t, weight_sems, sent_sems, kept_sem,
):
    tile = got_ref.shape[2] // TILES
    outer_copy, inner_copy = load([(outer_hbm, outer_buf), (inner_hbm, inner_buf)], weight_sems)
    kept_copy = pltpu.make_async_copy(got_ref, kept_hbm, kept_sem)
    kept_copy.start()
    sent_stores = copies(sent_buf, sent_hbm, sent_sems, tile, 2)
    outer_copy.wait()
    fill_outer_t(outer_buf, outer_wide_t)
    fill_outer(outer_buf, outer_wide)
    inner_copy.wait()
    fill_inner_t(inner_buf, inner_wide_t)
    fill_inner(inner_buf, inner_wide)
    for i in range(TILES):
        lanes = slice(tile * i, tile * i + tile)
        pre_ref[...] = dot(outer_wide_t[...], rows(got_ref[:, 0:16, lanes]), 1, 0)
        activate(pre_ref, slope_ref, hidden_ref)
        mid = dot(inner_wide_t[...], hidden_ref[...], 1, 0).astype(BF)
        sent_buf[:, 0:16, lanes] = mid.reshape(32, 16, tile)
        grad_hidden = dot(inner_wide[...], rows(got_ref[:, 16:32, lanes]), 1, 0)
        grad_pre_ref[...] = (grad_hidden * slope_ref[...]).astype(BF)
        grad_perm = dot(outer_wide[...], grad_pre_ref[...], 1, 0).astype(BF)
        sent_buf[:, 16:32, lanes] = grad_perm.reshape(32, 16, tile)
        sent_stores[i].start()
    finish(sent_stores)
    kept_copy.wait()


def picked(total_ref, by_j):
    row = lax.broadcasted_iota(jnp.int32, (512, 128), 0)
    mine = (row // 4) % 4 if by_j else row % 4
    value = total_ref[:, 0:128]
    for block in range(1, 4):
        value = jnp.where(mine == block, total_ref[:, 128 * block:128 * block + 128], value)
    return value


def spread_out(block_ref, slots, at):
    for rank, out_ref in slots:
        first_row = 16 * rank if isinstance(rank, int) else pl.multiple_of(16 * rank, 16)
        out_ref[at:at + 16, :] = block_ref[pl.ds(first_row, 16), :].astype(out_ref.dtype)


def write_outer(total_ref, picked_ref, block_ref, slots, at):
    picked_ref[...] = picked(total_ref, True)
    for j in range(4):
        for b in range(4):
            block_ref[pl.ds(b, 32, stride=4), :] = picked_ref[pl.ds(4 * j + b, 32, stride=16), :]
        spread_out(block_ref, slots, at + 16 * j)


def write_inner(total_ref, picked_ref, block_ref, slots, at):
    picked_ref[...] = picked(total_ref, False)
    for b in range(4):
        block_ref[...] = picked_ref[pl.ds(b, 128, stride=4), :].T
        spread_out(block_ref, slots, at + 16 * b)


def add(total_ref, value, start):
    if start:
        total_ref[...] = value
    else:
        total_ref[...] += value


def early_kernel(
    got_ref, outer_hbm, inner_hbm, mine_ref, own_ref, near_ref, middle_ref, far_ref,
    outer_buf, inner_buf, pre_ref, slope_ref, hidden_ref, grad_pre_ref, outer_wide_t, inner_wide,
    outer_total, inner_total, picked_ref, block_ref, weight_sems,
):
    tile = got_ref.shape[2] // TILES
    finish(load([(outer_hbm, outer_buf), (inner_hbm, inner_buf)], weight_sems))
    fill_outer_t(outer_buf, outer_wide_t)
    fill_inner(inner_buf, inner_wide)
    for i in range(TILES):
        lanes = slice(tile * i, tile * i + tile)
        first_perm = rows(got_ref[:, 0:16, lanes])
        grad_mid = rows(got_ref[:, 16:32, lanes])
        pre_ref[...] = dot(outer_wide_t[...], first_perm, 1, 0)
        activate(pre_ref, slope_ref, hidden_ref)
        grad_hidden = dot(inner_wide[...], grad_mid, 1, 0)
        grad_pre_ref[...] = (grad_hidden * slope_ref[...]).astype(BF)
        add(outer_total, dot(first_perm, grad_pre_ref[...], 1, 1), i == 0)
        add(inner_total, dot(grad_mid, hidden_ref[...], 1, 1), i == 0)
    slabs = [(own_ref, 0), (near_ref, 0), (middle_ref, 0), (middle_ref, 128)] + [(far_ref, 128 * i) for i in range(4)]
    slots = [(mine_ref[0] ^ i, ref.at[pl.ds(row, 128), :]) for i, (ref, row) in enumerate(slabs)]
    write_outer(outer_total, picked_ref, block_ref, slots, 0)
    write_inner(inner_total, picked_ref, block_ref, slots, 64)


def late_kernel(
    got_hbm, x_hbm, g_hbm, out_ref,
    got_buf, x_buf, g_buf, outer_total, inner_total, picked_ref, block_ref, second_sems, grad_sems, x_sems, g_sems,
):
    tile = x_buf.shape[0] // LATE_TILES
    slots = [(rank, out_ref.at[rank]) for rank in range(8)]
    g_copies = copies(g_hbm, g_buf, g_sems, tile, 0)
    x_copies = copies(x_hbm, x_buf, x_sems, tile, 0)
    second = copies(got_hbm.at[:, 0:16, :], got_buf.at[:, 0:16, :], second_sems, tile, 2)
    grad = copies(got_hbm.at[:, 16:32, :], got_buf.at[:, 16:32, :], grad_sems, tile, 2)
    for i in range(LATE_TILES):
        begin([second[i], g_copies[i]])
    for i in range(LATE_TILES):
        begin([grad[i], x_copies[i]])
    for i in range(LATE_TILES):
        lanes = slice(tile * i, tile * i + tile)
        finish([second[i], g_copies[i]])
        add(outer_total, dot(rows(got_buf[:, 0:16, lanes]), g_buf[lanes, :], 1, 0), i == 0)
    write_outer(outer_total, picked_ref, block_ref, slots, 0)
    for i in range(LATE_TILES):
        lanes = slice(tile * i, tile * i + tile)
        finish([grad[i], x_copies[i]])
        add(inner_total, dot(rows(got_buf[:, 16:32, lanes]), x_buf[lanes, :], 1, 0), i == 0)
    write_inner(inner_total, picked_ref, block_ref, slots, 64)


def tail_kernel(
    got_ref, outer_hbm, inner_hbm, output_hbm, input_grad_hbm,
    output_buf, input_grad_buf, outer_buf, inner_buf, outer_wide, inner_wide, weight_sems, output_sems, input_grad_sems,
):
    tile = output_buf.shape[0] // TILES
    finish(load([(outer_hbm, outer_buf), (inner_hbm, inner_buf)], weight_sems))
    fill_outer(outer_buf, outer_wide)
    fill_inner_t(inner_buf, inner_wide)
    stores = []
    for part, wide, buf, out, sems in (
        (0, outer_wide, output_buf, output_hbm, output_sems),
        (1, inner_wide, input_grad_buf, input_grad_hbm, input_grad_sems),
    ):
        leaving = copies(buf, out, sems, tile, 0)
        stores += leaving
        for i in range(TILES):
            lanes = slice(tile * i, tile * i + tile)
            message = rows(got_ref[:, 16 * part:16 * part + 16, lanes])
            buf[lanes, :] = dot(message, wide[...], 0, 0).astype(BF)
            leaving[i].start()
    finish(stores)


def call(kernel, name, args, outs, specs, out_specs, scratch, flops):
    moved = 2 * sum(a.size for a in args)
    return pl.pallas_call(
        kernel,
        in_specs=specs,
        out_specs=out_specs,
        out_shape=outs,
        scratch_shapes=scratch,
        name=name,
        cost_estimate=pl.CostEstimate(flops=flops, bytes_accessed=moved, transcendentals=0),
        compiler_params=pltpu.CompilerParams(vmem_limit_bytes=24 * 1024 * 1024),
    )(*args)


def body(tokens, inner_one, outer_one, inner_two, outer_two, cotangent):
    tok = tokens.shape[0]
    one = 2 * tok * 512 * 512
    mine = lax.axis_index("dp").astype(jnp.int32).reshape(1)
    tokens, cotangent, inner_one, outer_one, inner_two, outer_two = (
        pltpu.with_memory_space_constraint(value, pltpu.HBM)
        for value in (tokens, cotangent, inner_one, outer_one, inner_two, outer_two)
    )
    shape = jax.ShapeDtypeStruct
    hbm = pl.BlockSpec(memory_space=pltpu.HBM)
    vmem = pl.BlockSpec(memory_space=pltpu.VMEM)
    smem = pl.BlockSpec(memory_space=pltpu.SMEM)
    weight = pltpu.VMEM((4, 128, 128), BF)
    by_token = pltpu.VMEM((tok, 512), BF)
    by_message = pltpu.VMEM((32, 32, tok), BF)
    wide = pltpu.VMEM((512, 512), BF)
    total = pltpu.VMEM((512, 512), F32)
    picked_part = pltpu.VMEM((512, 128), F32)
    block = pltpu.VMEM((128, 128), F32)
    tile_f32 = pltpu.VMEM((512, tok // TILES), F32)
    tile_bf = pltpu.VMEM((512, tok // TILES), BF)
    pair = pltpu.SemaphoreType.DMA((2,))
    sems = pltpu.SemaphoreType.DMA((TILES,))
    late_sems = pltpu.SemaphoreType.DMA((LATE_TILES,))

    def exchange(value, axis):
        return lax.all_to_all(value, axis, split_axis=0, concat_axis=0, tiled=True)

    def across(value, flip):
        return lax.ppermute(value, "dp", [(rank, rank ^ flip) for rank in range(8)])

    sent = call(
        head_kernel, "head", (tokens, cotangent, inner_one, outer_two), [by_message], [hbm] * 4, [vmem],
        [by_token, by_token, weight, weight, wide, wide, pair, sems, sems], 2 * one,
    )[0]
    got = exchange(sent, "mp")
    sent_two, kept = call(
        middle_kernel, "middle", (got, outer_one, inner_two), [pltpu.HBM((32, 32, tok), BF)] * 2, [vmem, hbm, hbm], [hbm] * 2,
        [weight, weight, by_message, tile_f32, tile_f32, tile_bf, tile_bf, wide, wide, wide, wide, pair, sems, pltpu.SemaphoreType.DMA], 4 * one,
    )
    got_two = exchange(sent_two, "mp")
    own, near, middle, far = call(
        early_kernel, "early_grads", (kept, outer_one, inner_two, mine),
        [shape((128 * n, 128), F32) for n in (1, 1, 2, 4)], [vmem, hbm, hbm, smem], [vmem] * 4,
        [weight, weight, tile_f32, tile_f32, tile_bf, tile_bf, wide, wide, total, total, picked_part, block, pair], 4 * one,
    )
    halves = across(far, 4)
    quarters = across(middle + halves[256:], 2)
    eighth = across(near + halves[128:256] + quarters[128:], 1)
    got_two = pltpu.with_memory_space_constraint(got_two, pltpu.HBM)
    late = call(
        late_kernel, "late_grads", (got_two, tokens, cotangent), [shape((8, 128, 128), BF)], [hbm] * 3, [vmem],
        [by_message, by_token, by_token, total, total, picked_part, block] + [late_sems] * 4, 2 * one,
    )[0]
    late = exchange(late, "dp")
    output, input_grad = call(
        tail_kernel, "tail", (got_two, outer_two, inner_one), [pltpu.HBM((tok, 512), BF)] * 2, [vmem, hbm, hbm], [hbm] * 2,
        [by_token, by_token, weight, weight, wide, wide, pair, sems, sems], 2 * one,
    )
    return (
        output,
        input_grad,
        jnp.sum(late[:, 64:], axis=0, dtype=F32).reshape(4, 16, 128),
        (own[:64] + halves[:64] + quarters[:64] + eighth[:64]).reshape(4, 16, 128),
        (own[64:] + halves[64:128] + quarters[64:128] + eighth[64:]).reshape(4, 16, 128),
        jnp.sum(late[:, :64], axis=0, dtype=F32).reshape(4, 16, 128),
    )


def solution(mesh):
    placed = (
        P("dp", "mp"),
        P("mp", None, None),
        P("mp", None, None),
        P("mp", None, None),
        P("mp", None, None),
        P("dp", "mp"),
    )
    return jax.shard_map(
        body,
        mesh=mesh,
        in_specs=placed,
        out_specs=(
            P("dp", "mp"),
            P("dp", "mp"),
            P("mp", "dp", None),
            P("mp", "dp", None),
            P("mp", "dp", None),
            P("mp", "dp", None),
        ),
        check_vma=False,
    )
```

time: 159 us -> 155 us (0.975)
  waiting for transfers between devices: 34.1 us -> 31.2 us
  local copies, waits for them, and re-layouts: 0.01 us -> 2.18 us
  other arithmetic: 3.07 us -> 1.33 us
    all_to_all x2, waiting for transfers between devices: 20.4 us -> 17.6 us  [exchange(): return lax.all_to_all(value, axis, split_axis=0, concat_axis=0, tiled=True)]
    unnamed x2, local copies, waits for them, and re-layouts: 0.01 us -> 2.18 us
  transfers between devices with their start and end apart: 5 -> 5, of which waited for: 4 -> 4; matrix products, arithmetic and copies ran while one was open for 2% -> 0% of each run, Pallas kernels for 10% -> 12%
where the time goes in v4:
time: 155 us; the launch traced here: 153 us
  blocking collectives  56 us (36%)
  Pallas kernels  31.8 us (21%)
  waiting for transfers between devices  31.2 us (20%)
  starting transfers between devices  29.5 us (19%)
  local copies, waits for them, and re-layouts  2.18 us (1%)
    all_to_all x1, blocking collectives, exchange(): return lax.all_to_all(value, axis, split_axis=0, concat_axis=0, tiled=True)  56 us
    pallas_call x5, Pallas kernels, call(): pl.pallas_call(kernel, in_specs=specs, out_specs=out_specs, out_shape=out...  31.8 us
    all_to_all x2, waiting for transfers between devices, exchange(): return lax.all_to_all(value, axis, split_axis=0, concat_axis=0, tiled=True)  17.6 us
    all_to_all x2, starting transfers between devices, exchange(): return lax.all_to_all(value, axis, split_axis=0, concat_axis=0, tiled=True)  15.6 us
    ppermute x3, starting transfers between devices, across(): return lax.ppermute(value, 'dp', [(rank, rank ^ flip) for rank in range(8)])  13.9 us
    ppermute x3, waiting for transfers between devices, across(): return lax.ppermute(value, 'dp', [(rank, rank ^ flip) for rank in range(8)])  13.6 us
  transfers between devices with their start and end apart: 5, of which 4 were waited for; matrix products, arithmetic and copies ran while one was open for 0% of the time, Pallas kernels for 12%

profile of v4, /device:TPU:8, one launch (start us, length us, event | category | flops | bytes accessed | tf_op | source)
XLA Modules:
  0.0 152.7 jit_solution(5370967520111358161)
XLA Ops:
  0.6 5.1 %head.1 = bf16[32,32,2048]{2,1,0:T(8,128)(2,1)S(1)} custom-call(bf16[2048,512]{1,0:T(8,128)(2,1)} %x_hbm.3, bf16[2048,512]{1,0:T(8,128)(2,1)} %g_hbm.3, bf16[4,128,128]{2,1,0:T(8,128)(2,1)} %inner_hbm.6, bf16[4,128,128]{2,1,0:T(8,128)(2,1)} %outer_hbm.6), custom_call_target="tpu_custom_call" | custom-call | flops 2147483648 | bytes 4456448 | tf_op jit(solution)/shard_map/head/pallas_call | solution.py:270
  5.7 56.0 %all_to_all.15.got_ref = bf16[32,32,2048]{2,1,0:T(8,128)(2,1)S(1)} all-to-all(bf16[32,32,2048]{2,1,0:T(8,128)(2,1)S(1)} %head.1), channel_id=1, replica_groups=mesh['dp'=8,'mp'=32] {'mp'}, dimensions={0} | all-to-all | bytes 8388608 | tf_op jit(solution)/shard_map/all_to_all | solution.py:308
  61.7 8.3 %middle.1 = (bf16[32,32,2048]{2,1,0:T(8,128)(2,1)}, bf16[32,32,2048]{2,1,0:T(8,128)(2,1)}) custom-call(bf16[32,32,2048]{2,1,0:T(8,128)(2,1)S(1)} %all_to_all.15.got_ref, bf16[4,128,128]{2,1,0:T(8,128)(2,1)} %outer_hbm.7, bf16[4,128,128]{2,1,0:T(8,128)(2,1)} %inner_hbm.7), custom_call_target="tpu_custom_call" | custom-call | flops 4294967296 | bytes 4456448 | tf_op jit(solution)/shard_map/middle/pallas_call | solution.py:270
  70.0 7.1 %all-to-all-start.1 = ((bf16[32,32,2048]{2,1,0:T(8,128)(2,1)}), bf16[32,32,2048]{2,1,0:T(8,128)(2,1)}, u32[]{:S(2)}, u32[]{:S(2)}) async-start(bf16[32,32,2048]{2,1,0:T(8,128)(2,1)} %get-tuple-element.14), calls=%async_computation.1 | async-start | bytes 8388608 | tf_op jit(solution)/shard_map/all_to_all | solution.py:308
  77.1 0.0 copy-start
  77.1 2.2 %copy-done = bf16[32,32,2048]{2,1,0:T(8,128)(2,1)S(1)} copy-done((bf16[32,32,2048]{2,1,0:T(8,128)(2,1)S(1)}, bf16[32,32,2048]{2,1,0:T(8,128)(2,1)}, u32[]{:S(2)}) %copy-start) | copy-done | bytes 4194328
  79.3 6.6 %early_grads.1 = (f32[128,128]{1,0:T(8,128)S(1)}, f32[128,128]{1,0:T(8,128)S(1)}, f32[256,128]{1,0:T(8,128)S(1)}, f32[512,128]{1,0:T(8,128)S(1)}) custom-call(bf16[32,32,2048]{2,1,0:T(8,128)(2,1)S(1)} %copy-done, bf16[4,128,128]{2,1,0:T(8,128)(2,1)} %outer_hbm.7, bf16[4,128,128]{2,1,0:T(8,128)(2,1)} %inner_hbm.7, s32[1]{0:T(128)} %bitcast.1.mine_ref), custom_call_target="tpu_custom_call" | custom-call | flops 4294967296 | bytes 4456450 | tf_op jit(solution)/shard_map/early_grads/pallas_call | solution.py:270
  85.9 7.3 %collective-permute-start = (f32[512,128]{1,0:T(8,128)S(1)}, f32[512,128]{1,0:T(8,128)S(1)}, u32[]{:S(2)}, u32[]{:S(2)}) collective-permute-start(f32[512,128]{1,0:T(8,128)S(1)} %get-tuple-element.19), channel_id=1, source_target_pairs={{0,128},{32,160},{64,192},{96,224},{128,0},{160,32},{192,64},{224,... | collective-permute-start | bytes 786440 | tf_op jit(solution)/shard_map/ppermute | solution.py:311
  93.2 7.7 %collective-permute-done = f32[512,128]{1,0:T(8,128)S(1)} collective-permute-done((f32[512,128]{1,0:T(8,128)S(1)}, f32[512,128]{1,0:T(8,128)S(1)}, u32[]{:S(2)}, u32[]{:S(2)}) %collective-permute-start) | collective-permute-done | bytes 262176 | tf_op jit(solution)/shard_map/ppermute | solution.py:311
  101.0 6.5 %collective-permute-start.1 = (f32[256,128]{1,0:T(8,128)S(1)}, f32[256,128]{1,0:T(8,128)S(1)}, u32[]{:S(2)}, u32[]{:S(2)}) collective-permute-start(f32[256,128]{1,0:T(8,128)S(1)} %slice_add_fusion), channel_id=1, source_target_pairs={{0,64},{32,96},{64,0},{96,32},{128,192},{160,224},{192,128},{224,1... | collective-permute-start | bytes 393224 | tf_op jit(solution)/shard_map/ppermute | solution.py:311
  107.5 5.8 %collective-permute-done.1 = f32[256,128]{1,0:T(8,128)S(1)} collective-permute-done((f32[256,128]{1,0:T(8,128)S(1)}, f32[256,128]{1,0:T(8,128)S(1)}, u32[]{:S(2)}, u32[]{:S(2)}) %collective-permute-start.1) | collective-permute-done | bytes 131104 | tf_op jit(solution)/shard_map/ppermute | solution.py:311
  113.4 0.1 collective-permute-start.2
  113.5 14.1 %all-to-all-done.1.got_ref.got_hbm = bf16[32,32,2048]{2,1,0:T(8,128)(2,1)} async-done(((bf16[32,32,2048]{2,1,0:T(8,128)(2,1)}), bf16[32,32,2048]{2,1,0:T(8,128)(2,1)}, u32[]{:S(2)}, u32[]{:S(2)}) %all-to-all-start.1) | async-done | bytes 4194336 | tf_op jit(solution)/shard_map/all_to_all | solution.py:308
  127.5 5.1 %late_grads.1 = bf16[8,128,128]{2,1,0:T(8,128)(2,1)} custom-call(bf16[32,32,2048]{2,1,0:T(8,128)(2,1)} %all-to-all-done.1.got_ref.got_hbm, bf16[2048,512]{1,0:T(8,128)(2,1)} %x_hbm.3, bf16[2048,512]{1,0:T(8,128)(2,1)} %g_hbm.3), custom_call_target="tpu_custom_call" | custom-call | flops 2147483648 | bytes 8388608 | tf_op jit(solution)/shard_map/late_grads/pallas_call | solution.py:270
  132.6 8.5 %all-to-all-start.2 = ((bf16[8,128,128]{2,1,0:T(8,128)(2,1)}), bf16[8,128,128]{2,1,0:T(8,128)(2,1)S(1)}, u32[]{:S(2)}, u32[]{:S(2)}) async-start(bf16[8,128,128]{2,1,0:T(8,128)(2,1)} %late_grads.1), calls=%async_computation.2 | async-start | bytes 524288 | tf_op jit(solution)/shard_map/all_to_all | solution.py:308
  141.1 0.0 collective-permute-done.2
  141.1 0.6 slice_add_fusion.3
  141.7 6.8 %tail.1 = (bf16[2048,512]{1,0:T(8,128)(2,1)}, bf16[2048,512]{1,0:T(8,128)(2,1)}) custom-call(bf16[32,32,2048]{2,1,0:T(8,128)(2,1)} %all-to-all-done.1.got_ref.got_hbm, bf16[4,128,128]{2,1,0:T(8,128)(2,1)} %outer_hbm.6, bf16[4,128,128]{2,1,0:T(8,128)(2,1)} %inner_hbm.6), custom_call_target="tpu_custom_call" | custom-call | flops 2147483648 | bytes 4456448 | tf_op jit(solution)/shard_map/tail/pallas_call | solution.py:270
  148.5 3.5 %all-to-all-done.2 = bf16[8,128,128]{2,1,0:T(8,128)(2,1)S(1)} async-done(((bf16[8,128,128]{2,1,0:T(8,128)(2,1)}), bf16[8,128,128]{2,1,0:T(8,128)(2,1)S(1)}, u32[]{:S(2)}, u32[]{:S(2)}) %all-to-all-start.2) | async-done | bytes 262176 | tf_op jit(solution)/shard_map/all_to_all | solution.py:308
  152.0 0.7 convert_reduce_fusion
  (2 shorter events, 0.0 us)
Async XLA Ops:
  70.0 57.5 %all-to-all-start.1 = ((bf16[32,32,2048]{2,1,0:T(8,128)(2,1)}), bf16[32,32,2048]{2,1,0:T(8,128)(2,1)}, u32[]{:S(2)}, u32[]{:S(2)}) async-start(bf16[32,32,2048]{2,1,0:T(8,128)(2,1)} %get-tuple-element.14), calls=%async_computation.1 | async-start | bytes 8388608 | tf_op jit(solution)/shard_map/all_to_all | solution.py:308
  77.1 2.2 %copy-start = (bf16[32,32,2048]{2,1,0:T(8,128)(2,1)S(1)}, bf16[32,32,2048]{2,1,0:T(8,128)(2,1)}, u32[]{:S(2)}) copy-start(bf16[32,32,2048]{2,1,0:T(8,128)(2,1)} %get-tuple-element.17.got_ref) | copy-start | bytes 12582916
  85.9 15.0 %collective-permute-start = (f32[512,128]{1,0:T(8,128)S(1)}, f32[512,128]{1,0:T(8,128)S(1)}, u32[]{:S(2)}, u32[]{:S(2)}) collective-permute-start(f32[512,128]{1,0:T(8,128)S(1)} %get-tuple-element.19), channel_id=1, source_target_pairs={{0,128},{32,160},{64,192},{96,224},{128,0},{160,32},{192,64},{224,... | collective-permute-start | bytes 786440 | tf_op jit(solution)/shard_map/ppermute | solution.py:311
  101.0 12.3 %collective-permute-start.1 = (f32[256,128]{1,0:T(8,128)S(1)}, f32[256,128]{1,0:T(8,128)S(1)}, u32[]{:S(2)}, u32[]{:S(2)}) collective-permute-start(f32[256,128]{1,0:T(8,128)S(1)} %slice_add_fusion), channel_id=1, source_target_pairs={{0,64},{32,96},{64,0},{96,32},{128,192},{160,224},{192,128},{224,1... | collective-permute-start | bytes 393224 | tf_op jit(solution)/shard_map/ppermute | solution.py:311
  113.4 27.7 %collective-permute-start.2 = (f32[128,128]{1,0:T(8,128)S(1)}, f32[128,128]{1,0:T(8,128)S(1)}, u32[]{:S(2)}, u32[]{:S(2)}) collective-permute-start(f32[128,128]{1,0:T(8,128)S(1)} %slice_add_fusion.1), channel_id=1, source_target_pairs={{0,32},{32,0},{64,96},{96,64},{128,160},{160,128},{192,224},{224,1... | collective-permute-start | bytes 196616 | tf_op jit(solution)/shard_map/ppermute | solution.py:311
  132.6 19.4 %all-to-all-start.2 = ((bf16[8,128,128]{2,1,0:T(8,128)(2,1)}), bf16[8,128,128]{2,1,0:T(8,128)(2,1)S(1)}, u32[]{:S(2)}, u32[]{:S(2)}) async-start(bf16[8,128,128]{2,1,0:T(8,128)(2,1)} %late_grads.1), calls=%async_computation.2 | async-start | bytes 524288 | tf_op jit(solution)/shard_map/all_to_all | solution.py:308

commit v5 on v4

--- a/solution.py
+++ b/solution.py
@@ -9,28 +9,36 @@
 F32 = jnp.float32
 GELU_SCALE = 0.7978845608028654
 GELU_CUBE = 0.044715
-TILES = 2
+HEAD_TILES = 1
+TILES = 4
 LATE_TILES = 4
 ROWS = 64
+
+PEERS = [8 * y + 2 * x + core for x in range(4) for y in range(4) for core in range(2)]
 
 
 def dot(left, right, left_dim, right_dim):
     return lax.dot_general(
         left, right, (((left_dim,), (right_dim,)), ((), ())), preferred_element_type=F32
     )
+
+
+def peer_order(column):
+    return ((column >> 3) & 3) * 32 + (column >> 5) * 8 + (column & 7)
 
 
 def inner_spread(block, wide, rows_wide):
     shape = (wide, 128) if rows_wide else (128, wide)
     row = lax.broadcasted_iota(jnp.int32, shape, 0)
     col = lax.broadcasted_iota(jnp.int32, shape, 1)
-    hit = (row == 4 * col + block) if rows_wide else (col == 4 * row + block)
+    hit = (row == 4 * peer_order(col) + block) if rows_wide else (col == 4 * peer_order(row) + block)
     return hit.astype(F32).astype(BF)
 
 
 def outer_spread(block):
     row = lax.broadcasted_iota(jnp.int32, (512, 128), 0)
     col = lax.broadcasted_iota(jnp.int32, (512, 128), 1)
+    col = peer_order(col)
     hit = row == 16 * (col // 4) + 4 * block + col % 4
     return hit.astype(F32).astype(BF)
 
@@ -95,7 +103,7 @@
     x_hbm, g_hbm, inner_hbm, outer_hbm, sent_ref,
     x_buf, g_buf, inner_buf, outer_buf, inner_wide, outer_wide, weight_sems, x_sems, g_sems,
 ):
-    tile = x_buf.shape[0] // TILES
+    tile = x_buf.shape[0] // HEAD_TILES
     weights = load([(inner_hbm, inner_buf), (outer_hbm, outer_buf)], weight_sems)
     x_copies = copies(x_hbm, x_buf, x_sems, tile, 0)
     g_copies = copies(g_hbm, g_buf, g_sems, tile, 0)
@@ -105,13 +113,13 @@
     fill_inner_t(inner_buf, inner_wide)
     fill_outer(outer_buf, outer_wide)
     for part, wide, buf, arriving in ((0, inner_wide, x_buf, x_copies), (1, outer_wide, g_buf, g_copies)):
-        for i in range(TILES):
+        for i in range(HEAD_TILES):
             arriving[i].wait()
             mid = dot(wide[...], buf[tile * i:tile * i + tile, :], 1, 1).astype(BF)
             sent_ref[:, 16 * part:16 * part + 16, tile * i:tile * i + tile] = mid.reshape(32, 16, tile)
 
 
-def activate(pre_ref, slope_ref, hidden_ref):
+def activate(pre_ref, hidden_ref, grad_hidden_ref, grad_pre_ref):
     for top in range(0, 512, ROWS):
         band = slice(top, top + ROWS)
         pre = pre_ref[band, :]
@@ -120,12 +128,13 @@
         half = 0.5 + 0.5 * bent
         hidden_ref[band, :] = (pre * half).astype(BF)
         rise = 0.5 * GELU_SCALE + (1.5 * GELU_SCALE * GELU_CUBE) * square
-        slope_ref[band, :] = half + pre * (1.0 - bent * bent) * rise
+        slope = half + pre * (1.0 - bent * bent) * rise
+        grad_pre_ref[band, :] = (grad_hidden_ref[band, :] * slope).astype(BF)
 
 
 def middle_kernel(
     got_ref, outer_hbm, inner_hbm, sent_hbm, kept_hbm,
-    outer_buf, inner_buf, sent_buf, pre_ref, slope_ref, hidden_ref, grad_pre_ref,
+    outer_buf, inner_buf, sent_buf, pre_ref, grad_hidden_ref, hidden_ref, grad_pre_ref,
     outer_wide, outer_wide_t, inner_wide, inner_wide_t, weight_sems, sent_sems, kept_sem,
 ):
     tile = got_ref.shape[2] // TILES
@@ -139,28 +148,36 @@
     inner_copy.wait()
     fill_inner_t(inner_buf, inner_wide_t)
     fill_inner(inner_buf, inner_wide)
+    def lanes(i):
+        return slice(tile * i, tile * i + tile)
+
+    def pre_act(i):
+        pre_ref[i % 2] = dot(outer_wide_t[...], rows(got_ref[:, 0:16, lanes(i)]), 1, 0)
+
+    pre_act(0)
     for i in range(TILES):
-        lanes = slice(tile * i, tile * i + tile)
-        pre_ref[...] = dot(outer_wide_t[...], rows(got_ref[:, 0:16, lanes]), 1, 0)
-        activate(pre_ref, slope_ref, hidden_ref)
+        grad_hidden_ref[...] = dot(inner_wide[...], rows(got_ref[:, 16:32, lanes(i)]), 1, 0)
+        if i + 1 < TILES:
+            pre_act(i + 1)
+        activate(pre_ref.at[i % 2], hidden_ref, grad_hidden_ref, grad_pre_ref)
         mid = dot(inner_wide_t[...], hidden_ref[...], 1, 0).astype(BF)
-        sent_buf[:, 0:16, lanes] = mid.reshape(32, 16, tile)
-        grad_hidden = dot(inner_wide[...], rows(got_ref[:, 16:32, lanes]), 1, 0)
-        grad_pre_ref[...] = (grad_hidden * slope_ref[...]).astype(BF)
+        sent_buf[:, 0:16, lanes(i)] = mid.reshape(32, 16, tile)
         grad_perm = dot(outer_wide[...], grad_pre_ref[...], 1, 0).astype(BF)
-        sent_buf[:, 16:32, lanes] = grad_perm.reshape(32, 16, tile)
+        sent_buf[:, 16:32, lanes(i)] = grad_perm.reshape(32, 16, tile)
         sent_stores[i].start()
     finish(sent_stores)
     kept_copy.wait()
 
 
-def picked(total_ref, by_j):
-    row = lax.broadcasted_iota(jnp.int32, (512, 128), 0)
-    mine = (row // 4) % 4 if by_j else row % 4
-    value = total_ref[:, 0:128]
-    for block in range(1, 4):
-        value = jnp.where(mine == block, total_ref[:, 128 * block:128 * block + 128], value)
-    return value
+def pick(total_ref, picked_ref, by_j):
+    row = lax.broadcasted_iota(jnp.int32, (16, 128), 0)
+    mine = row // 4 if by_j else row % 4
+    for peer, device in enumerate(PEERS):
+        band = slice(16 * peer, 16 * peer + 16)
+        value = total_ref[band, 0:128]
+        for block in range(1, 4):
+            value = jnp.where(mine == block, total_ref[band, 128 * block:128 * block + 128], value)
+        picked_ref[16 * device:16 * device + 16, :] = value
 
 
 def spread_out(block_ref, slots, at):
@@ -170,7 +187,7 @@
 
 
 def write_outer(total_ref, picked_ref, block_ref, slots, at):
-    picked_ref[...] = picked(total_ref, True)
+    pick(total_ref, picked_ref, True)
     for j in range(4):
         for b in range(4):
             block_ref[pl.ds(b, 32, stride=4), :] = picked_ref[pl.ds(4 * j + b, 32, stride=16), :]
@@ -178,7 +195,7 @@
 
 
 def write_inner(total_ref, picked_ref, block_ref, slots, at):
-    picked_ref[...] = picked(total_ref, False)
+    pick(total_ref, picked_ref, False)
     for b in range(4):
         block_ref[...] = picked_ref[pl.ds(b, 128, stride=4), :].T
         spread_out(block_ref, slots, at + 16 * b)
@@ -193,7 +210,7 @@
 
 def early_kernel(
     got_ref, outer_hbm, inner_hbm, mine_ref, own_ref, near_ref, middle_ref, far_ref,
-    outer_buf, inner_buf, pre_ref, slope_ref, hidden_ref, grad_pre_ref, outer_wide_t, inner_wide,
+    outer_buf, inner_buf, pre_ref, grad_hidden_ref, hidden_ref, grad_pre_ref, outer_wide_t, inner_wide,
     outer_total, inner_total, picked_ref, block_ref, weight_sems,
 ):
     tile = got_ref.shape[2] // TILES
@@ -205,9 +222,8 @@
         first_perm = rows(got_ref[:, 0:16, lanes])
         grad_mid = rows(got_ref[:, 16:32, lanes])
         pre_ref[...] = dot(outer_wide_t[...], first_perm, 1, 0)
-        activate(pre_ref, slope_ref, hidden_ref)
-        grad_hidden = dot(inner_wide[...], grad_mid, 1, 0)
-        grad_pre_ref[...] = (grad_hidden * slope_ref[...]).astype(BF)
+        grad_hidden_ref[...] = dot(inner_wide[...], grad_mid, 1, 0)
+        activate(pre_ref, hidden_ref, grad_hidden_ref, grad_pre_ref)
         add(outer_total, dot(first_perm, grad_pre_ref[...], 1, 1), i == 0)
         add(inner_total, dot(grad_mid, hidden_ref[...], 1, 1), i == 0)
     slabs = [(own_ref, 0), (near_ref, 0), (middle_ref, 0), (middle_ref, 128)] + [(far_ref, 128 * i) for i in range(4)]
@@ -302,24 +318,27 @@
     tile_bf = pltpu.VMEM((512, tok // TILES), BF)
     pair = pltpu.SemaphoreType.DMA((2,))
     sems = pltpu.SemaphoreType.DMA((TILES,))
+    head_sems = pltpu.SemaphoreType.DMA((HEAD_TILES,))
     late_sems = pltpu.SemaphoreType.DMA((LATE_TILES,))
 
-    def exchange(value, axis):
-        return lax.all_to_all(value, axis, split_axis=0, concat_axis=0, tiled=True)
+    def exchange(value, axis, order=None):
+        return lax.all_to_all(
+            value, axis, split_axis=0, concat_axis=0, tiled=True, axis_index_groups=order
+        )
 
     def across(value, flip):
         return lax.ppermute(value, "dp", [(rank, rank ^ flip) for rank in range(8)])
 
     sent = call(
         head_kernel, "head", (tokens, cotangent, inner_one, outer_two), [by_message], [hbm] * 4, [vmem],
-        [by_token, by_token, weight, weight, wide, wide, pair, sems, sems], 2 * one,
+        [by_token, by_token, weight, weight, wide, wide, pair, head_sems, head_sems], 2 * one,
     )[0]
-    got = exchange(sent, "mp")
+    got = exchange(sent, "mp", [PEERS])
     sent_two, kept = call(
         middle_kernel, "middle", (got, outer_one, inner_two), [pltpu.HBM((32, 32, tok), BF)] * 2, [vmem, hbm, hbm], [hbm] * 2,
-        [weight, weight, by_message, tile_f32, tile_f32, tile_bf, tile_bf, wide, wide, wide, wide, pair, sems, pltpu.SemaphoreType.DMA], 4 * one,
-    )
-    got_two = exchange(sent_two, "mp")
+        [weight, weight, by_message, pltpu.VMEM((2, 512, tok // TILES), F32), tile_f32, tile_bf, tile_bf, wide, wide, wide, wide, pair, sems, pltpu.SemaphoreType.DMA], 4 * one,
+    )
+    got_two = exchange(sent_two, "mp", [PEERS])
     own, near, middle, far = call(
         early_kernel, "early_grads", (kept, outer_one, inner_two, mine),
         [shape((128 * n, 128), F32) for n in (1, 1, 2, 4)], [vmem, hbm, hbm, smem], [vmem] * 4,

time: 155 us -> 157 us (1.013)
  waiting for transfers between devices: 31.2 us -> 35.7 us
    all_to_all x2, waiting for transfers between devices: 17.6 us -> 22.1 us  [exchange(): lax.all_to_all(value, axis, split_axis=0, concat_axis=0, tiled=True, axis...]
where the time goes in v5:
time: 157 us; the launch traced here: 156 us
  blocking collectives  56.6 us (36%)
  waiting for transfers between devices  35.7 us (23%)
  Pallas kernels  31.3 us (20%)
  starting transfers between devices  28.3 us (18%)
  local copies, waits for them, and re-layouts  2.18 us (1%)
    all_to_all x1, blocking collectives, exchange(): lax.all_to_all(value, axis, split_axis=0, concat_axis=0, tiled=True, axis...  56.6 us
    pallas_call x5, Pallas kernels, call(): pl.pallas_call(kernel, in_specs=specs, out_specs=out_specs, out_shape=out...  31.3 us
    all_to_all x2, waiting for transfers between devices, exchange(): lax.all_to_all(value, axis, split_axis=0, concat_axis=0, tiled=True, axis...  22.1 us
    all_to_all x2, starting transfers between devices, exchange(): lax.all_to_all(value, axis, split_axis=0, concat_axis=0, tiled=True, axis...  14.5 us
    ppermute x3, starting transfers between devices, across(): return lax.ppermute(value, 'dp', [(rank, rank ^ flip) for rank in range(8)])  13.9 us
    ppermute x3, waiting for transfers between devices, across(): return lax.ppermute(value, 'dp', [(rank, rank ^ flip) for rank in range(8)])  13.6 us
  transfers between devices with their start and end apart: 5, of which 4 were waited for; matrix products, arithmetic and copies ran while one was open for 0% of the time, Pallas kernels for 12%

profile of v5, /device:TPU:8, one launch (start us, length us, event | category | flops | bytes accessed | tf_op | source)
XLA Modules:
  0.0 156.2 jit_solution(8680595881521561645)
XLA Ops:
  0.6 4.4 %head.1 = bf16[32,32,2048]{2,1,0:T(8,128)(2,1)S(1)} custom-call(bf16[2048,512]{1,0:T(8,128)(2,1)} %x_hbm.3, bf16[2048,512]{1,0:T(8,128)(2,1)} %g_hbm.3, bf16[4,128,128]{2,1,0:T(8,128)(2,1)} %inner_hbm.6, bf16[4,128,128]{2,1,0:T(8,128)(2,1)} %outer_hbm.6), custom_call_target="tpu_custom_call" | custom-call | flops 2147483648 | bytes 4456448 | tf_op jit(solution)/shard_map/head/pallas_call | solution.py:286
  5.0 56.6 %all_to_all.15.got_ref = bf16[32,32,2048]{2,1,0:T(8,128)(2,1)S(1)} all-to-all(bf16[32,32,2048]{2,1,0:T(8,128)(2,1)S(1)} %head.1), channel_id=1, replica_groups={{0,1,8,9,16,17,24,25,2,3,10,11,18,19,26,27,4,5,12,13,20,21,28,29,6,7,14..., dimensions={0} | all-to-all | bytes 8388608 | tf_op jit(solution)/shard_map/all_to_all | solution.py:325
  61.6 8.0 %middle.1 = (bf16[32,32,2048]{2,1,0:T(8,128)(2,1)}, bf16[32,32,2048]{2,1,0:T(8,128)(2,1)}) custom-call(bf16[32,32,2048]{2,1,0:T(8,128)(2,1)S(1)} %all_to_all.15.got_ref, bf16[4,128,128]{2,1,0:T(8,128)(2,1)} %outer_hbm.7, bf16[4,128,128]{2,1,0:T(8,128)(2,1)} %inner_hbm.7), custom_call_target="tpu_custom_call" | custom-call | flops 4294967296 | bytes 4456448 | tf_op jit(solution)/shard_map/middle/pallas_call | solution.py:286
  69.6 6.0 %all-to-all-start.1 = ((bf16[32,32,2048]{2,1,0:T(8,128)(2,1)}), bf16[32,32,2048]{2,1,0:T(8,128)(2,1)}, u32[]{:S(2)}, u32[]{:S(2)}) async-start(bf16[32,32,2048]{2,1,0:T(8,128)(2,1)} %get-tuple-element.14), calls=%async_computation.1 | async-start | bytes 8388608 | tf_op jit(solution)/shard_map/all_to_all | solution.py:325
  75.5 0.0 copy-start
  75.6 2.2 %copy-done = bf16[32,32,2048]{2,1,0:T(8,128)(2,1)S(1)} copy-done((bf16[32,32,2048]{2,1,0:T(8,128)(2,1)S(1)}, bf16[32,32,2048]{2,1,0:T(8,128)(2,1)}, u32[]{:S(2)}) %copy-start) | copy-done | bytes 4194328
  77.7 7.3 %early_grads.1 = (f32[128,128]{1,0:T(8,128)S(1)}, f32[128,128]{1,0:T(8,128)S(1)}, f32[256,128]{1,0:T(8,128)S(1)}, f32[512,128]{1,0:T(8,128)S(1)}) custom-call(bf16[32,32,2048]{2,1,0:T(8,128)(2,1)S(1)} %copy-done, bf16[4,128,128]{2,1,0:T(8,128)(2,1)} %outer_hbm.7, bf16[4,128,128]{2,1,0:T(8,128)(2,1)} %inner_hbm.7, s32[1]{0:T(128)} %bitcast.1.mine_ref), custom_call_target="tpu_custom_call" | custom-call | flops 4294967296 | bytes 4456450 | tf_op jit(solution)/shard_map/early_grads/pallas_call | solution.py:286
  85.0 7.3 %collective-permute-start = (f32[512,128]{1,0:T(8,128)S(1)}, f32[512,128]{1,0:T(8,128)S(1)}, u32[]{:S(2)}, u32[]{:S(2)}) collective-permute-start(f32[512,128]{1,0:T(8,128)S(1)} %get-tuple-element.19), channel_id=1, source_target_pairs={{0,128},{32,160},{64,192},{96,224},{128,0},{160,32},{192,64},{224,... | collective-permute-start | bytes 786440 | tf_op jit(solution)/shard_map/ppermute | solution.py:330
  92.3 7.8 %collective-permute-done = f32[512,128]{1,0:T(8,128)S(1)} collective-permute-done((f32[512,128]{1,0:T(8,128)S(1)}, f32[512,128]{1,0:T(8,128)S(1)}, u32[]{:S(2)}, u32[]{:S(2)}) %collective-permute-start) | collective-permute-done | bytes 262176 | tf_op jit(solution)/shard_map/ppermute | solution.py:330
  100.1 6.5 %collective-permute-start.1 = (f32[256,128]{1,0:T(8,128)S(1)}, f32[256,128]{1,0:T(8,128)S(1)}, u32[]{:S(2)}, u32[]{:S(2)}) collective-permute-start(f32[256,128]{1,0:T(8,128)S(1)} %slice_add_fusion), channel_id=1, source_target_pairs={{0,64},{32,96},{64,0},{96,32},{128,192},{160,224},{192,128},{224,1... | collective-permute-start | bytes 393224 | tf_op jit(solution)/shard_map/ppermute | solution.py:330
  106.6 5.8 %collective-permute-done.1 = f32[256,128]{1,0:T(8,128)S(1)} collective-permute-done((f32[256,128]{1,0:T(8,128)S(1)}, f32[256,128]{1,0:T(8,128)S(1)}, u32[]{:S(2)}, u32[]{:S(2)}) %collective-permute-start.1) | collective-permute-done | bytes 131104 | tf_op jit(solution)/shard_map/ppermute | solution.py:330
  112.4 0.1 collective-permute-start.2
  112.5 17.7 %all-to-all-done.1.got_ref.got_hbm = bf16[32,32,2048]{2,1,0:T(8,128)(2,1)} async-done(((bf16[32,32,2048]{2,1,0:T(8,128)(2,1)}), bf16[32,32,2048]{2,1,0:T(8,128)(2,1)}, u32[]{:S(2)}, u32[]{:S(2)}) %all-to-all-start.1) | async-done | bytes 4194336 | tf_op jit(solution)/shard_map/all_to_all | solution.py:325
  130.3 5.1 %late_grads.1 = bf16[8,128,128]{2,1,0:T(8,128)(2,1)} custom-call(bf16[32,32,2048]{2,1,0:T(8,128)(2,1)} %all-to-all-done.1.got_ref.got_hbm, bf16[2048,512]{1,0:T(8,128)(2,1)} %x_hbm.3, bf16[2048,512]{1,0:T(8,128)(2,1)} %g_hbm.3), custom_call_target="tpu_custom_call" | custom-call | flops 2147483648 | bytes 8388608 | tf_op jit(solution)/shard_map/late_grads/pallas_call | solution.py:286
  135.3 8.5 %all-to-all-start.2 = ((bf16[8,128,128]{2,1,0:T(8,128)(2,1)}), bf16[8,128,128]{2,1,0:T(8,128)(2,1)S(1)}, u32[]{:S(2)}, u32[]{:S(2)}) async-start(bf16[8,128,128]{2,1,0:T(8,128)(2,1)} %late_grads.1), calls=%async_computation.2 | async-start | bytes 524288 | tf_op jit(solution)/shard_map/all_to_all | solution.py:325
  143.8 0.0 collective-permute-done.2
  143.8 0.6 slice_add_fusion.3
  144.5 6.6 %tail.1 = (bf16[2048,512]{1,0:T(8,128)(2,1)}, bf16[2048,512]{1,0:T(8,128)(2,1)}) custom-call(bf16[32,32,2048]{2,1,0:T(8,128)(2,1)} %all-to-all-done.1.got_ref.got_hbm, bf16[4,128,128]{2,1,0:T(8,128)(2,1)} %outer_hbm.6, bf16[4,128,128]{2,1,0:T(8,128)(2,1)} %inner_hbm.6), custom_call_target="tpu_custom_call" | custom-call | flops 2147483648 | bytes 4456448 | tf_op jit(solution)/shard_map/tail/pallas_call | solution.py:286
  151.1 4.4 %all-to-all-done.2 = bf16[8,128,128]{2,1,0:T(8,128)(2,1)S(1)} async-done(((bf16[8,128,128]{2,1,0:T(8,128)(2,1)}), bf16[8,128,128]{2,1,0:T(8,128)(2,1)S(1)}, u32[]{:S(2)}, u32[]{:S(2)}) %all-to-all-start.2) | async-done | bytes 262176 | tf_op jit(solution)/shard_map/all_to_all | solution.py:325
  155.5 0.7 convert_reduce_fusion
  (2 shorter events, 0.0 us)
Async XLA Ops:
  69.6 60.7 %all-to-all-start.1 = ((bf16[32,32,2048]{2,1,0:T(8,128)(2,1)}), bf16[32,32,2048]{2,1,0:T(8,128)(2,1)}, u32[]{:S(2)}, u32[]{:S(2)}) async-start(bf16[32,32,2048]{2,1,0:T(8,128)(2,1)} %get-tuple-element.14), calls=%async_computation.1 | async-start | bytes 8388608 | tf_op jit(solution)/shard_map/all_to_all | solution.py:325
  75.5 2.2 %copy-start = (bf16[32,32,2048]{2,1,0:T(8,128)(2,1)S(1)}, bf16[32,32,2048]{2,1,0:T(8,128)(2,1)}, u32[]{:S(2)}) copy-start(bf16[32,32,2048]{2,1,0:T(8,128)(2,1)} %get-tuple-element.17.got_ref) | copy-start | bytes 12582916
  85.0 15.0 %collective-permute-start = (f32[512,128]{1,0:T(8,128)S(1)}, f32[512,128]{1,0:T(8,128)S(1)}, u32[]{:S(2)}, u32[]{:S(2)}) collective-permute-start(f32[512,128]{1,0:T(8,128)S(1)} %get-tuple-element.19), channel_id=1, source_target_pairs={{0,128},{32,160},{64,192},{96,224},{128,0},{160,32},{192,64},{224,... | collective-permute-start | bytes 786440 | tf_op jit(solution)/shard_map/ppermute | solution.py:330
  100.1 12.3 %collective-permute-start.1 = (f32[256,128]{1,0:T(8,128)S(1)}, f32[256,128]{1,0:T(8,128)S(1)}, u32[]{:S(2)}, u32[]{:S(2)}) collective-permute-start(f32[256,128]{1,0:T(8,128)S(1)} %slice_add_fusion), channel_id=1, source_target_pairs={{0,64},{32,96},{64,0},{96,32},{128,192},{160,224},{192,128},{224,1... | collective-permute-start | bytes 393224 | tf_op jit(solution)/shard_map/ppermute | solution.py:330
  112.4 31.4 %collective-permute-start.2 = (f32[128,128]{1,0:T(8,128)S(1)}, f32[128,128]{1,0:T(8,128)S(1)}, u32[]{:S(2)}, u32[]{:S(2)}) collective-permute-start(f32[128,128]{1,0:T(8,128)S(1)} %slice_add_fusion.1), channel_id=1, source_target_pairs={{0,32},{32,0},{64,96},{96,64},{128,160},{160,128},{192,224},{224,1... | collective-permute-start | bytes 196616 | tf_op jit(solution)/shard_map/ppermute | solution.py:330
  135.3 20.2 %all-to-all-start.2 = ((bf16[8,128,128]{2,1,0:T(8,128)(2,1)}), bf16[8,128,128]{2,1,0:T(8,128)(2,1)S(1)}, u32[]{:S(2)}, u32[]{:S(2)}) async-start(bf16[8,128,128]{2,1,0:T(8,128)(2,1)} %late_grads.1), calls=%async_computation.2 | async-start | bytes 524288 | tf_op jit(solution)/shard_map/all_to_all | solution.py:325

commit v6 on v5

--- a/solution.py
+++ b/solution.py
@@ -14,8 +14,6 @@
 LATE_TILES = 4
 ROWS = 64
 
-PEERS = [8 * y + 2 * x + core for x in range(4) for y in range(4) for core in range(2)]
-
 
 def dot(left, right, left_dim, right_dim):
     return lax.dot_general(
@@ -23,52 +21,63 @@
     )
 
 
-def peer_order(column):
-    return ((column >> 3) & 3) * 32 + (column >> 5) * 8 + (column & 7)
-
-
-def inner_spread(block, wide, rows_wide):
-    shape = (wide, 128) if rows_wide else (128, wide)
+def one_hot(shape, place):
     row = lax.broadcasted_iota(jnp.int32, shape, 0)
     col = lax.broadcasted_iota(jnp.int32, shape, 1)
-    hit = (row == 4 * peer_order(col) + block) if rows_wide else (col == 4 * peer_order(row) + block)
-    return hit.astype(F32).astype(BF)
+    return place(row, col).astype(F32).astype(BF)
+
+
+def fill_first(weight_ref, pair_ref):
+    for block in range(4):
+        at = block % 2
+        spread = one_hot((256, 128), lambda row, col: row == 2 * col + at)
+        pair_ref[block // 2, :, 128 * at:128 * at + 128] = dot(spread, weight_ref[block], 1, 1).astype(BF)
+
+
+def fill_second(weight_ref, pair_ref):
+    for block in range(4):
+        at = block % 2
+        spread = one_hot((256, 128), lambda row, col: row == 8 * (col // 4) + 4 * at + col % 4)
+        pair_ref[block // 2, :, 128 * at:128 * at + 128] = dot(spread, weight_ref[block], 1, 0).astype(BF)
 
 
 def outer_spread(block):
-    row = lax.broadcasted_iota(jnp.int32, (512, 128), 0)
-    col = lax.broadcasted_iota(jnp.int32, (512, 128), 1)
-    col = peer_order(col)
-    hit = row == 16 * (col // 4) + 4 * block + col % 4
-    return hit.astype(F32).astype(BF)
+    def place(row, col):
+        b = col % 4
+        return row == 16 * (col // 4) + 8 * (b // 2) + 2 * block + b % 2
+
+    return one_hot((512, 128), place)
+
+
+def fill_outer(weight_ref, wide_ref):
+    for block in range(4):
+        wide_ref[:, 128 * block:128 * block + 128] = dot(outer_spread(block), weight_ref[block], 1, 0).astype(BF)
+
+
+def fill_outer_t(weight_ref, wide_ref):
+    for block in range(4):
+        wide_ref[128 * block:128 * block + 128, :] = dot(weight_ref[block], outer_spread(block), 0, 1).astype(BF)
+
+
+def fill_inner(weight_ref, wide_ref):
+    for block in range(4):
+        spread = one_hot((128, 512), lambda row, col: col == 4 * row + block)
+        wide_ref[128 * block:128 * block + 128, :] = dot(weight_ref[block], spread, 1, 0).astype(BF)
 
 
 def fill_inner_t(weight_ref, wide_ref):
     for block in range(4):
-        wide_ref[:, 128 * block:128 * block + 128] = dot(
-            inner_spread(block, 512, True), weight_ref[block], 1, 1
-        ).astype(BF)
-
-
-def fill_inner(weight_ref, wide_ref):
-    for block in range(4):
-        wide_ref[128 * block:128 * block + 128, :] = dot(
-            weight_ref[block], inner_spread(block, 512, False), 1, 0
-        ).astype(BF)
-
-
-def fill_outer(weight_ref, wide_ref):
-    for block in range(4):
-        wide_ref[:, 128 * block:128 * block + 128] = dot(
-            outer_spread(block), weight_ref[block], 1, 0
-        ).astype(BF)
-
-
-def fill_outer_t(weight_ref, wide_ref):
-    for block in range(4):
-        wide_ref[128 * block:128 * block + 128, :] = dot(
-            weight_ref[block], outer_spread(block), 0, 1
-        ).astype(BF)
+        spread = one_hot((512, 128), lambda row, col: row == 4 * col + block)
+        wide_ref[:, 128 * block:128 * block + 128] = dot(spread, weight_ref[block], 1, 1).astype(BF)
+
+
+def paired(pair_ref, values, right_dim):
+    halves = []
+    for half in range(2):
+        part = values(slice(256 * half, 256 * half + 256))
+        product = dot(pair_ref[half], part, 1, right_dim)
+        halves.append(product.reshape(32, 8, product.shape[1]))
+    return jnp.concatenate(halves, axis=1).astype(BF)
 
 
 def rows(value):
@@ -101,7 +110,7 @@
 
 def head_kernel(
     x_hbm, g_hbm, inner_hbm, outer_hbm, sent_ref,
-    x_buf, g_buf, inner_buf, outer_buf, inner_wide, outer_wide, weight_sems, x_sems, g_sems,
+    x_buf, g_buf, inner_buf, outer_buf, inner_pair, outer_pair, weight_sems, x_sems, g_sems,
 ):
     tile = x_buf.shape[0] // HEAD_TILES
     weights = load([(inner_hbm, inner_buf), (outer_hbm, outer_buf)], weight_sems)
@@ -110,13 +119,13 @@
     begin(x_copies)
     begin(g_copies)
     finish(weights)
-    fill_inner_t(inner_buf, inner_wide)
-    fill_outer(outer_buf, outer_wide)
-    for part, wide, buf, arriving in ((0, inner_wide, x_buf, x_copies), (1, outer_wide, g_buf, g_copies)):
+    fill_first(inner_buf, inner_pair)
+    fill_second(outer_buf, outer_pair)
+    for part, pair_ref, buf, arriving in ((0, inner_pair, x_buf, x_copies), (1, outer_pair, g_buf, g_copies)):
         for i in range(HEAD_TILES):
             arriving[i].wait()
-            mid = dot(wide[...], buf[tile * i:tile * i + tile, :], 1, 1).astype(BF)
-            sent_ref[:, 16 * part:16 * part + 16, tile * i:tile * i + tile] = mid.reshape(32, 16, tile)
+            lanes = slice(tile * i, tile * i + tile)
+            sent_ref[:, 16 * part:16 * part + 16, lanes] = paired(pair_ref, lambda at: buf[lanes, at], 1)
 
 
 def activate(pre_ref, hidden_ref, grad_hidden_ref, grad_pre_ref):
@@ -135,7 +144,7 @@
 def middle_kernel(
     got_ref, outer_hbm, inner_hbm, sent_hbm, kept_hbm,
     outer_buf, inner_buf, sent_buf, pre_ref, grad_hidden_ref, hidden_ref, grad_pre_ref,
-    outer_wide, outer_wide_t, inner_wide, inner_wide_t, weight_sems, sent_sems, kept_sem,
+    outer_wide_t, inner_wide, inner_pair, outer_pair, weight_sems, sent_sems, kept_sem,
 ):
     tile = got_ref.shape[2] // TILES
     outer_copy, inner_copy = load([(outer_hbm, outer_buf), (inner_hbm, inner_buf)], weight_sems)
@@ -144,9 +153,9 @@
     sent_stores = copies(sent_buf, sent_hbm, sent_sems, tile, 2)
     outer_copy.wait()
     fill_outer_t(outer_buf, outer_wide_t)
-    fill_outer(outer_buf, outer_wide)
+    fill_second(outer_buf, outer_pair)
     inner_copy.wait()
-    fill_inner_t(inner_buf, inner_wide_t)
+    fill_first(inner_buf, inner_pair)
     fill_inner(inner_buf, inner_wide)
     def lanes(i):
         return slice(tile * i, tile * i + tile)
@@ -160,24 +169,20 @@
         if i + 1 < TILES:
             pre_act(i + 1)
         activate(pre_ref.at[i % 2], hidden_ref, grad_hidden_ref, grad_pre_ref)
-        mid = dot(inner_wide_t[...], hidden_ref[...], 1, 0).astype(BF)
-        sent_buf[:, 0:16, lanes(i)] = mid.reshape(32, 16, tile)
-        grad_perm = dot(outer_wide[...], grad_pre_ref[...], 1, 0).astype(BF)
-        sent_buf[:, 16:32, lanes(i)] = grad_perm.reshape(32, 16, tile)
+        sent_buf[:, 0:16, lanes(i)] = paired(inner_pair, lambda at: hidden_ref[at, :], 0)
+        sent_buf[:, 16:32, lanes(i)] = paired(outer_pair, lambda at: grad_pre_ref[at, :], 0)
         sent_stores[i].start()
     finish(sent_stores)
     kept_copy.wait()
 
 
-def pick(total_ref, picked_ref, by_j):
-    row = lax.broadcasted_iota(jnp.int32, (16, 128), 0)
-    mine = row // 4 if by_j else row % 4
-    for peer, device in enumerate(PEERS):
-        band = slice(16 * peer, 16 * peer + 16)
-        value = total_ref[band, 0:128]
-        for block in range(1, 4):
-            value = jnp.where(mine == block, total_ref[band, 128 * block:128 * block + 128], value)
-        picked_ref[16 * device:16 * device + 16, :] = value
+def picked(total_ref, forward):
+    row = lax.broadcasted_iota(jnp.int32, (512, 128), 0)
+    mine = (row // 2) % 4 if forward else row % 4
+    value = total_ref[:, 0:128]
+    for block in range(1, 4):
+        value = jnp.where(mine == block, total_ref[:, 128 * block:128 * block + 128], value)
+    return value
 
 
 def spread_out(block_ref, slots, at):
@@ -187,15 +192,16 @@
 
 
 def write_outer(total_ref, picked_ref, block_ref, slots, at):
-    pick(total_ref, picked_ref, True)
+    picked_ref[...] = picked(total_ref, True)
     for j in range(4):
         for b in range(4):
-            block_ref[pl.ds(b, 32, stride=4), :] = picked_ref[pl.ds(4 * j + b, 32, stride=16), :]
+            row = 8 * (b // 2) + 2 * j + b % 2
+            block_ref[pl.ds(b, 32, stride=4), :] = picked_ref[pl.ds(row, 32, stride=16), :]
         spread_out(block_ref, slots, at + 16 * j)
 
 
 def write_inner(total_ref, picked_ref, block_ref, slots, at):
-    pick(total_ref, picked_ref, False)
+    picked_ref[...] = picked(total_ref, False)
     for b in range(4):
         block_ref[...] = picked_ref[pl.ds(b, 128, stride=4), :].T
         spread_out(block_ref, slots, at + 16 * b)
@@ -311,6 +317,7 @@
     by_token = pltpu.VMEM((tok, 512), BF)
     by_message = pltpu.VMEM((32, 32, tok), BF)
     wide = pltpu.VMEM((512, 512), BF)
+    halves_of = pltpu.VMEM((2, 256, 256), BF)
     total = pltpu.VMEM((512, 512), F32)
     picked_part = pltpu.VMEM((512, 128), F32)
     block = pltpu.VMEM((128, 128), F32)
@@ -321,24 +328,22 @@
     head_sems = pltpu.SemaphoreType.DMA((HEAD_TILES,))
     late_sems = pltpu.SemaphoreType.DMA((LATE_TILES,))
 
-    def exchange(value, axis, order=None):
-        return lax.all_to_all(
-            value, axis, split_axis=0, concat_axis=0, tiled=True, axis_index_groups=order
-        )
+    def exchange(value, axis):
+        return lax.all_to_all(value, axis, split_axis=0, concat_axis=0, tiled=True)
 
     def across(value, flip):
         return lax.ppermute(value, "dp", [(rank, rank ^ flip) for rank in range(8)])
 
     sent = call(
         head_kernel, "head", (tokens, cotangent, inner_one, outer_two), [by_message], [hbm] * 4, [vmem],
-        [by_token, by_token, weight, weight, wide, wide, pair, head_sems, head_sems], 2 * one,
+        [by_token, by_token, weight, weight, halves_of, halves_of, pair, head_sems, head_sems], 2 * one,
     )[0]
-    got = exchange(sent, "mp", [PEERS])
+    got = exchange(sent, "mp")
     sent_two, kept = call(
         middle_kernel, "middle", (got, outer_one, inner_two), [pltpu.HBM((32, 32, tok), BF)] * 2, [vmem, hbm, hbm], [hbm] * 2,
-        [weight, weight, by_message, pltpu.VMEM((2, 512, tok // TILES), F32), tile_f32, tile_bf, tile_bf, wide, wide, wide, wide, pair, sems, pltpu.SemaphoreType.DMA], 4 * one,
-    )
-    got_two = exchange(sent_two, "mp", [PEERS])
+        [weight, weight, by_message, pltpu.VMEM((2, 512, tok // TILES), F32), tile_f32, tile_bf, tile_bf, wide, wide, halves_of, halves_of, pair, sems, pltpu.SemaphoreType.DMA], 4 * one,
+    )
+    got_two = exchange(sent_two, "mp")
     own, near, middle, far = call(
         early_kernel, "early_grads", (kept, outer_one, inner_two, mine),
         [shape((128 * n, 128), F32) for n in (1, 1, 2, 4)], [vmem, hbm, hbm, smem], [vmem] * 4,

time: 157 us -> 152 us (0.968); the launches traced: 156 us -> 150 us
  waiting for transfers between devices: 35.7 us -> 30.7 us
  Pallas kernels: 31.3 us -> 29.1 us
    all_to_all x2, waiting for transfers between devices: 22.1 us -> 17.1 us  [exchange(): return lax.all_to_all(value, axis, split_axis=0, concat_axis=0, tiled=True)]
    pallas_call x5, Pallas kernels: 31.3 us -> 29.1 us  [call(): pl.pallas_call(kernel, in_specs=specs, out_specs=out_specs, out_shape=out...]
  transfers between devices with their start and end apart: 5 -> 5, of which waited for: 4 -> 4; matrix products, arithmetic and copies ran while one was open for 0% -> 0% of each run, Pallas kernels for 12% -> 13%
where the time goes in v6:
time: 152 us; the launch traced here: 150 us
  blocking collectives  56 us (37%)
  waiting for transfers between devices  30.7 us (20%)
  starting transfers between devices  29.5 us (19%)
  Pallas kernels  29.1 us (19%)
  local copies, waits for them, and re-layouts  2.18 us (1%)
    all_to_all x1, blocking collectives, exchange(): return lax.all_to_all(value, axis, split_axis=0, concat_axis=0, tiled=True)  56 us
    pallas_call x5, Pallas kernels, call(): pl.pallas_call(kernel, in_specs=specs, out_specs=out_specs, out_shape=out...  29.1 us
    all_to_all x2, waiting for transfers between devices, exchange(): return lax.all_to_all(value, axis, split_axis=0, concat_axis=0, tiled=True)  17.1 us
    all_to_all x2, starting transfers between devices, exchange(): return lax.all_to_all(value, axis, split_axis=0, concat_axis=0, tiled=True)  15.6 us
    ppermute x3, starting transfers between devices, across(): return lax.ppermute(value, 'dp', [(rank, rank ^ flip) for rank in range(8)])  13.9 us
    ppermute x3, waiting for transfers between devices, across(): return lax.ppermute(value, 'dp', [(rank, rank ^ flip) for rank in range(8)])  13.6 us
  transfers between devices with their start and end apart: 5, of which 4 were waited for; matrix products, arithmetic and copies ran while one was open for 0% of the time, Pallas kernels for 13%

profile of v6, /device:TPU:8, one launch (start us, length us, event | category | flops | bytes accessed | tf_op | source)
XLA Modules:
  0.0 149.5 jit_solution(4595413865392457557)
XLA Ops:
  0.6 3.3 %head.1 = bf16[32,32,2048]{2,1,0:T(8,128)(2,1)S(1)} custom-call(bf16[2048,512]{1,0:T(8,128)(2,1)} %x_hbm.3, bf16[2048,512]{1,0:T(8,128)(2,1)} %g_hbm.3, bf16[4,128,128]{2,1,0:T(8,128)(2,1)} %inner_hbm.6, bf16[4,128,128]{2,1,0:T(8,128)(2,1)} %outer_hbm.6), custom_call_target="tpu_custom_call" | custom-call | flops 2147483648 | bytes 4456448 | tf_op jit(solution)/shard_map/head/pallas_call | solution.py:292
  3.9 56.0 %all_to_all.15.got_ref = bf16[32,32,2048]{2,1,0:T(8,128)(2,1)S(1)} all-to-all(bf16[32,32,2048]{2,1,0:T(8,128)(2,1)S(1)} %head.1), channel_id=1, replica_groups=mesh['dp'=8,'mp'=32] {'mp'}, dimensions={0} | all-to-all | bytes 8388608 | tf_op jit(solution)/shard_map/all_to_all | solution.py:332
  59.9 6.8 %middle.1 = (bf16[32,32,2048]{2,1,0:T(8,128)(2,1)}, bf16[32,32,2048]{2,1,0:T(8,128)(2,1)}) custom-call(bf16[32,32,2048]{2,1,0:T(8,128)(2,1)S(1)} %all_to_all.15.got_ref, bf16[4,128,128]{2,1,0:T(8,128)(2,1)} %outer_hbm.7, bf16[4,128,128]{2,1,0:T(8,128)(2,1)} %inner_hbm.7), custom_call_target="tpu_custom_call" | custom-call | flops 4294967296 | bytes 4456448 | tf_op jit(solution)/shard_map/middle/pallas_call | solution.py:292
  66.8 7.1 %all-to-all-start.1 = ((bf16[32,32,2048]{2,1,0:T(8,128)(2,1)}), bf16[32,32,2048]{2,1,0:T(8,128)(2,1)}, u32[]{:S(2)}, u32[]{:S(2)}) async-start(bf16[32,32,2048]{2,1,0:T(8,128)(2,1)} %get-tuple-element.14), calls=%async_computation.1 | async-start | bytes 8388608 | tf_op jit(solution)/shard_map/all_to_all | solution.py:332
  73.9 0.0 copy-start
  73.9 2.2 %copy-done = bf16[32,32,2048]{2,1,0:T(8,128)(2,1)S(1)} copy-done((bf16[32,32,2048]{2,1,0:T(8,128)(2,1)S(1)}, bf16[32,32,2048]{2,1,0:T(8,128)(2,1)}, u32[]{:S(2)}) %copy-start) | copy-done | bytes 4194328
  76.1 7.3 %early_grads.1 = (f32[128,128]{1,0:T(8,128)S(1)}, f32[128,128]{1,0:T(8,128)S(1)}, f32[256,128]{1,0:T(8,128)S(1)}, f32[512,128]{1,0:T(8,128)S(1)}) custom-call(bf16[32,32,2048]{2,1,0:T(8,128)(2,1)S(1)} %copy-done, bf16[4,128,128]{2,1,0:T(8,128)(2,1)} %outer_hbm.7, bf16[4,128,128]{2,1,0:T(8,128)(2,1)} %inner_hbm.7, s32[1]{0:T(128)} %bitcast.1.mine_ref), custom_call_target="tpu_custom_call" | custom-call | flops 4294967296 | bytes 4456450 | tf_op jit(solution)/shard_map/early_grads/pallas_call | solution.py:292
  83.4 7.3 %collective-permute-start = (f32[512,128]{1,0:T(8,128)S(1)}, f32[512,128]{1,0:T(8,128)S(1)}, u32[]{:S(2)}, u32[]{:S(2)}) collective-permute-start(f32[512,128]{1,0:T(8,128)S(1)} %get-tuple-element.19), channel_id=1, source_target_pairs={{0,128},{32,160},{64,192},{96,224},{128,0},{160,32},{192,64},{224,... | collective-permute-start | bytes 786440 | tf_op jit(solution)/shard_map/ppermute | solution.py:335
  90.7 7.8 %collective-permute-done = f32[512,128]{1,0:T(8,128)S(1)} collective-permute-done((f32[512,128]{1,0:T(8,128)S(1)}, f32[512,128]{1,0:T(8,128)S(1)}, u32[]{:S(2)}, u32[]{:S(2)}) %collective-permute-start) | collective-permute-done | bytes 262176 | tf_op jit(solution)/shard_map/ppermute | solution.py:335
  98.5 6.5 %collective-permute-start.1 = (f32[256,128]{1,0:T(8,128)S(1)}, f32[256,128]{1,0:T(8,128)S(1)}, u32[]{:S(2)}, u32[]{:S(2)}) collective-permute-start(f32[256,128]{1,0:T(8,128)S(1)} %slice_add_fusion), channel_id=1, source_target_pairs={{0,64},{32,96},{64,0},{96,32},{128,192},{160,224},{192,128},{224,1... | collective-permute-start | bytes 393224 | tf_op jit(solution)/shard_map/ppermute | solution.py:335
  104.9 5.8 %collective-permute-done.1 = f32[256,128]{1,0:T(8,128)S(1)} collective-permute-done((f32[256,128]{1,0:T(8,128)S(1)}, f32[256,128]{1,0:T(8,128)S(1)}, u32[]{:S(2)}, u32[]{:S(2)}) %collective-permute-start.1) | collective-permute-done | bytes 131104 | tf_op jit(solution)/shard_map/ppermute | solution.py:335
  110.8 0.1 collective-permute-start.2
  110.9 13.4 %all-to-all-done.1.got_ref.got_hbm = bf16[32,32,2048]{2,1,0:T(8,128)(2,1)} async-done(((bf16[32,32,2048]{2,1,0:T(8,128)(2,1)}), bf16[32,32,2048]{2,1,0:T(8,128)(2,1)}, u32[]{:S(2)}, u32[]{:S(2)}) %all-to-all-start.1) | async-done | bytes 4194336 | tf_op jit(solution)/shard_map/all_to_all | solution.py:332
  124.3 5.1 %late_grads.1 = bf16[8,128,128]{2,1,0:T(8,128)(2,1)} custom-call(bf16[32,32,2048]{2,1,0:T(8,128)(2,1)} %all-to-all-done.1.got_ref.got_hbm, bf16[2048,512]{1,0:T(8,128)(2,1)} %x_hbm.3, bf16[2048,512]{1,0:T(8,128)(2,1)} %g_hbm.3), custom_call_target="tpu_custom_call" | custom-call | flops 2147483648 | bytes 8388608 | tf_op jit(solution)/shard_map/late_grads/pallas_call | solution.py:292
  129.4 8.5 %all-to-all-start.2 = ((bf16[8,128,128]{2,1,0:T(8,128)(2,1)}), bf16[8,128,128]{2,1,0:T(8,128)(2,1)S(1)}, u32[]{:S(2)}, u32[]{:S(2)}) async-start(bf16[8,128,128]{2,1,0:T(8,128)(2,1)} %late_grads.1), calls=%async_computation.2 | async-start | bytes 524288 | tf_op jit(solution)/shard_map/all_to_all | solution.py:332
  137.9 0.0 collective-permute-done.2
  137.9 0.6 slice_add_fusion.3
  138.5 6.6 %tail.1 = (bf16[2048,512]{1,0:T(8,128)(2,1)}, bf16[2048,512]{1,0:T(8,128)(2,1)}) custom-call(bf16[32,32,2048]{2,1,0:T(8,128)(2,1)} %all-to-all-done.1.got_ref.got_hbm, bf16[4,128,128]{2,1,0:T(8,128)(2,1)} %outer_hbm.6, bf16[4,128,128]{2,1,0:T(8,128)(2,1)} %inner_hbm.6), custom_call_target="tpu_custom_call" | custom-call | flops 2147483648 | bytes 4456448 | tf_op jit(solution)/shard_map/tail/pallas_call | solution.py:292
  145.2 3.6 %all-to-all-done.2 = bf16[8,128,128]{2,1,0:T(8,128)(2,1)S(1)} async-done(((bf16[8,128,128]{2,1,0:T(8,128)(2,1)}), bf16[8,128,128]{2,1,0:T(8,128)(2,1)S(1)}, u32[]{:S(2)}, u32[]{:S(2)}) %all-to-all-start.2) | async-done | bytes 262176 | tf_op jit(solution)/shard_map/all_to_all | solution.py:332
  148.8 0.7 convert_reduce_fusion
  (2 shorter events, 0.0 us)
Async XLA Ops:
  66.8 57.5 %all-to-all-start.1 = ((bf16[32,32,2048]{2,1,0:T(8,128)(2,1)}), bf16[32,32,2048]{2,1,0:T(8,128)(2,1)}, u32[]{:S(2)}, u32[]{:S(2)}) async-start(bf16[32,32,2048]{2,1,0:T(8,128)(2,1)} %get-tuple-element.14), calls=%async_computation.1 | async-start | bytes 8388608 | tf_op jit(solution)/shard_map/all_to_all | solution.py:332
  73.9 2.2 %copy-start = (bf16[32,32,2048]{2,1,0:T(8,128)(2,1)S(1)}, bf16[32,32,2048]{2,1,0:T(8,128)(2,1)}, u32[]{:S(2)}) copy-start(bf16[32,32,2048]{2,1,0:T(8,128)(2,1)} %get-tuple-element.17.got_ref) | copy-start | bytes 12582916
  83.4 15.1 %collective-permute-start = (f32[512,128]{1,0:T(8,128)S(1)}, f32[512,128]{1,0:T(8,128)S(1)}, u32[]{:S(2)}, u32[]{:S(2)}) collective-permute-start(f32[512,128]{1,0:T(8,128)S(1)} %get-tuple-element.19), channel_id=1, source_target_pairs={{0,128},{32,160},{64,192},{96,224},{128,0},{160,32},{192,64},{224,... | collective-permute-start | bytes 786440 | tf_op jit(solution)/shard_map/ppermute | solution.py:335
  98.5 12.3 %collective-permute-start.1 = (f32[256,128]{1,0:T(8,128)S(1)}, f32[256,128]{1,0:T(8,128)S(1)}, u32[]{:S(2)}, u32[]{:S(2)}) collective-permute-start(f32[256,128]{1,0:T(8,128)S(1)} %slice_add_fusion), channel_id=1, source_target_pairs={{0,64},{32,96},{64,0},{96,32},{128,192},{160,224},{192,128},{224,1... | collective-permute-start | bytes 393224 | tf_op jit(solution)/shard_map/ppermute | solution.py:335
  110.8 27.1 %collective-permute-start.2 = (f32[128,128]{1,0:T(8,128)S(1)}, f32[128,128]{1,0:T(8,128)S(1)}, u32[]{:S(2)}, u32[]{:S(2)}) collective-permute-start(f32[128,128]{1,0:T(8,128)S(1)} %slice_add_fusion.1), channel_id=1, source_target_pairs={{0,32},{32,0},{64,96},{96,64},{128,160},{160,128},{192,224},{224,1... | collective-permute-start | bytes 196616 | tf_op jit(solution)/shard_map/ppermute | solution.py:335
  129.4 19.4 %all-to-all-start.2 = ((bf16[8,128,128]{2,1,0:T(8,128)(2,1)}), bf16[8,128,128]{2,1,0:T(8,128)(2,1)S(1)}, u32[]{:S(2)}, u32[]{:S(2)}) async-start(bf16[8,128,128]{2,1,0:T(8,128)(2,1)} %late_grads.1), calls=%async_computation.2 | async-start | bytes 524288 | tf_op jit(solution)/shard_map/all_to_all | solution.py:332

commit v7 on v6

--- a/solution.py
+++ b/solution.py
@@ -238,30 +238,34 @@
     write_inner(inner_total, picked_ref, block_ref, slots, 64)
 
 
+def fetch_kernel(x_hbm, x_ref, sem):
+    copy = pltpu.make_async_copy(x_hbm, x_ref, sem)
+    copy.start()
+    copy.wait()
+
+
 def late_kernel(
-    got_hbm, x_hbm, g_hbm, out_ref,
-    got_buf, x_buf, g_buf, outer_total, inner_total, picked_ref, block_ref, second_sems, grad_sems, x_sems, g_sems,
+    got_hbm, x_ref, g_hbm, out_ref,
+    got_buf, g_buf, outer_total, inner_total, picked_ref, block_ref, second_sems, grad_sems, g_sems,
 ):
-    tile = x_buf.shape[0] // LATE_TILES
-    slots = [(rank, out_ref.at[rank]) for rank in range(8)]
+    tile = g_buf.shape[0] // LATE_TILES
+    slots = [(rank, out_ref.at[7 - rank]) for rank in range(8)]
     g_copies = copies(g_hbm, g_buf, g_sems, tile, 0)
-    x_copies = copies(x_hbm, x_buf, x_sems, tile, 0)
     second = copies(got_hbm.at[:, 0:16, :], got_buf.at[:, 0:16, :], second_sems, tile, 2)
     grad = copies(got_hbm.at[:, 16:32, :], got_buf.at[:, 16:32, :], grad_sems, tile, 2)
+    begin(grad)
     for i in range(LATE_TILES):
         begin([second[i], g_copies[i]])
     for i in range(LATE_TILES):
-        begin([grad[i], x_copies[i]])
+        lanes = slice(tile * i, tile * i + tile)
+        grad[i].wait()
+        add(inner_total, dot(rows(got_buf[:, 16:32, lanes]), x_ref[lanes, :], 1, 0), i == 0)
+    write_inner(inner_total, picked_ref, block_ref, slots, 64)
     for i in range(LATE_TILES):
         lanes = slice(tile * i, tile * i + tile)
         finish([second[i], g_copies[i]])
         add(outer_total, dot(rows(got_buf[:, 0:16, lanes]), g_buf[lanes, :], 1, 0), i == 0)
     write_outer(outer_total, picked_ref, block_ref, slots, 0)
-    for i in range(LATE_TILES):
-        lanes = slice(tile * i, tile * i + tile)
-        finish([grad[i], x_copies[i]])
-        add(inner_total, dot(rows(got_buf[:, 16:32, lanes]), x_buf[lanes, :], 1, 0), i == 0)
-    write_inner(inner_total, picked_ref, block_ref, slots, 64)
 
 
 def tail_kernel(
@@ -328,8 +332,10 @@
     head_sems = pltpu.SemaphoreType.DMA((HEAD_TILES,))
     late_sems = pltpu.SemaphoreType.DMA((LATE_TILES,))
 
-    def exchange(value, axis):
-        return lax.all_to_all(value, axis, split_axis=0, concat_axis=0, tiled=True)
+    def exchange(value, axis, order=None):
+        return lax.all_to_all(
+            value, axis, split_axis=0, concat_axis=0, tiled=True, axis_index_groups=order
+        )
 
     def across(value, flip):
         return lax.ppermute(value, "dp", [(rank, rank ^ flip) for rank in range(8)])
@@ -353,11 +359,14 @@
     quarters = across(middle + halves[256:], 2)
     eighth = across(near + halves[128:256] + quarters[128:], 1)
     got_two = pltpu.with_memory_space_constraint(got_two, pltpu.HBM)
+    tokens_here = call(
+        fetch_kernel, "fetch", (tokens,), [by_token], [hbm], [vmem], [pltpu.SemaphoreType.DMA], 0
+    )[0]
     late = call(
-        late_kernel, "late_grads", (got_two, tokens, cotangent), [shape((8, 128, 128), BF)], [hbm] * 3, [vmem],
-        [by_message, by_token, by_token, total, total, picked_part, block] + [late_sems] * 4, 2 * one,
+        late_kernel, "late_grads", (got_two, tokens_here, cotangent), [shape((8, 128, 128), BF)], [hbm, vmem, hbm], [vmem],
+        [by_message, by_token, total, total, picked_part, block] + [late_sems] * 3, 2 * one,
     )[0]
-    late = exchange(late, "dp")
+    late = exchange(late, "dp", [[7 - rank for rank in range(8)]])
     output, input_grad = call(
         tail_kernel, "tail", (got_two, outer_two, inner_one), [pltpu.HBM((tok, 512), BF)] * 2, [vmem, hbm, hbm], [hbm] * 2,
         [by_token, by_token, weight, weight, wide, wide, pair, sems, sems], 2 * one,

time: 152 us -> 149 us (0.980)
  waiting for transfers between devices: 30.7 us -> 25.9 us
    all_to_all x2, waiting for transfers between devices: 17.1 us -> 13.9 us  [exchange(): lax.all_to_all(value, axis, split_axis=0, concat_axis=0, tiled=True, axis...]
    ppermute x3, waiting for transfers between devices: 13.6 us -> 12 us  [across(): return lax.ppermute(value, 'dp', [(rank, rank ^ flip) for rank in range(8)])]
    pallas_call x5 -> x6, Pallas kernels: 29.1 us -> 30.5 us  [call(): pl.pallas_call(kernel, in_specs=specs, out_specs=out_specs, out_shape=out...]
  transfers between devices with their start and end apart: 5 -> 5, of which waited for: 4 -> 4; matrix products, arithmetic and copies ran while one was open for 0% -> 0% of each run, Pallas kernels for 13% -> 14%
where the time goes in v7:
time: 149 us; the launch traced here: 147 us
  blocking collectives  56 us (38%)
  Pallas kernels  30.5 us (20%)
  starting transfers between devices  30.2 us (20%)
  waiting for transfers between devices  25.9 us (17%)
  local copies, waits for them, and re-layouts  2.18 us (1%)
    all_to_all x1, blocking collectives, exchange(): lax.all_to_all(value, axis, split_axis=0, concat_axis=0, tiled=True, axis...  56 us
    pallas_call x6, Pallas kernels, call(): pl.pallas_call(kernel, in_specs=specs, out_specs=out_specs, out_shape=out...  30.5 us
    all_to_all x2, starting transfers between devices, exchange(): lax.all_to_all(value, axis, split_axis=0, concat_axis=0, tiled=True, axis...  16.3 us
    ppermute x3, starting transfers between devices, across(): return lax.ppermute(value, 'dp', [(rank, rank ^ flip) for rank in range(8)])  13.9 us
    all_to_all x2, waiting for transfers between devices, exchange(): lax.all_to_all(value, axis, split_axis=0, concat_axis=0, tiled=True, axis...  13.9 us
    ppermute x3, waiting for transfers between devices, across(): return lax.ppermute(value, 'dp', [(rank, rank ^ flip) for rank in range(8)])  12 us
  transfers between devices with their start and end apart: 5, of which 4 were waited for; matrix products, arithmetic and copies ran while one was open for 0% of the time, Pallas kernels for 14%

profile of v7, /device:TPU:8, one launch (start us, length us, event | category | flops | bytes accessed | tf_op | source)
XLA Modules:
  0.0 146.8 jit_solution(16816844567615417148)
XLA Ops:
  0.6 3.3 %head.1 = bf16[32,32,2048]{2,1,0:T(8,128)(2,1)S(1)} custom-call(bf16[2048,512]{1,0:T(8,128)(2,1)} %x_hbm.3, bf16[2048,512]{1,0:T(8,128)(2,1)} %g_hbm.3, bf16[4,128,128]{2,1,0:T(8,128)(2,1)} %inner_hbm.6, bf16[4,128,128]{2,1,0:T(8,128)(2,1)} %outer_hbm.6), custom_call_target="tpu_custom_call" | custom-call | flops 2147483648 | bytes 4456448 | tf_op jit(solution)/shard_map/head/pallas_call | solution.py:296
  3.9 56.0 %all_to_all.15.got_ref = bf16[32,32,2048]{2,1,0:T(8,128)(2,1)S(1)} all-to-all(bf16[32,32,2048]{2,1,0:T(8,128)(2,1)S(1)} %head.1), channel_id=1, replica_groups=mesh['dp'=8,'mp'=32] {'mp'}, dimensions={0} | all-to-all | bytes 8388608 | tf_op jit(solution)/shard_map/all_to_all | solution.py:336
  59.9 6.8 %middle.1 = (bf16[32,32,2048]{2,1,0:T(8,128)(2,1)}, bf16[32,32,2048]{2,1,0:T(8,128)(2,1)}) custom-call(bf16[32,32,2048]{2,1,0:T(8,128)(2,1)S(1)} %all_to_all.15.got_ref, bf16[4,128,128]{2,1,0:T(8,128)(2,1)} %outer_hbm.7, bf16[4,128,128]{2,1,0:T(8,128)(2,1)} %inner_hbm.7), custom_call_target="tpu_custom_call" | custom-call | flops 4294967296 | bytes 4456448 | tf_op jit(solution)/shard_map/middle/pallas_call | solution.py:296
  66.8 7.1 %all-to-all-start.1 = ((bf16[32,32,2048]{2,1,0:T(8,128)(2,1)}), bf16[32,32,2048]{2,1,0:T(8,128)(2,1)}, u32[]{:S(2)}, u32[]{:S(2)}) async-start(bf16[32,32,2048]{2,1,0:T(8,128)(2,1)} %get-tuple-element.14), calls=%async_computation.1 | async-start | bytes 8388608 | tf_op jit(solution)/shard_map/all_to_all | solution.py:336
  73.9 0.0 copy-start
  73.9 2.2 %copy-done = bf16[32,32,2048]{2,1,0:T(8,128)(2,1)S(1)} copy-done((bf16[32,32,2048]{2,1,0:T(8,128)(2,1)S(1)}, bf16[32,32,2048]{2,1,0:T(8,128)(2,1)}, u32[]{:S(2)}) %copy-start) | copy-done | bytes 4194328
  76.1 7.3 %early_grads.1 = (f32[128,128]{1,0:T(8,128)S(1)}, f32[128,128]{1,0:T(8,128)S(1)}, f32[256,128]{1,0:T(8,128)S(1)}, f32[512,128]{1,0:T(8,128)S(1)}) custom-call(bf16[32,32,2048]{2,1,0:T(8,128)(2,1)S(1)} %copy-done, bf16[4,128,128]{2,1,0:T(8,128)(2,1)} %outer_hbm.7, bf16[4,128,128]{2,1,0:T(8,128)(2,1)} %inner_hbm.7, s32[1]{0:T(128)} %bitcast.1.mine_ref), custom_call_target="tpu_custom_call" | custom-call | flops 4294967296 | bytes 4456450 | tf_op jit(solution)/shard_map/early_grads/pallas_call | solution.py:296
  83.4 7.3 %collective-permute-start = (f32[512,128]{1,0:T(8,128)S(1)}, f32[512,128]{1,0:T(8,128)S(1)}, u32[]{:S(2)}, u32[]{:S(2)}) collective-permute-start(f32[512,128]{1,0:T(8,128)S(1)} %get-tuple-element.19), channel_id=1, source_target_pairs={{0,128},{32,160},{64,192},{96,224},{128,0},{160,32},{192,64},{224,... | collective-permute-start | bytes 786440 | tf_op jit(solution)/shard_map/ppermute | solution.py:341
  90.7 7.8 %collective-permute-done = f32[512,128]{1,0:T(8,128)S(1)} collective-permute-done((f32[512,128]{1,0:T(8,128)S(1)}, f32[512,128]{1,0:T(8,128)S(1)}, u32[]{:S(2)}, u32[]{:S(2)}) %collective-permute-start) | collective-permute-done | bytes 262176 | tf_op jit(solution)/shard_map/ppermute | solution.py:341
  98.5 6.5 %collective-permute-start.1 = (f32[256,128]{1,0:T(8,128)S(1)}, f32[256,128]{1,0:T(8,128)S(1)}, u32[]{:S(2)}, u32[]{:S(2)}) collective-permute-start(f32[256,128]{1,0:T(8,128)S(1)} %slice_add_fusion), channel_id=1, source_target_pairs={{0,64},{32,96},{64,0},{96,32},{128,192},{160,224},{192,128},{224,1... | collective-permute-start | bytes 393224 | tf_op jit(solution)/shard_map/ppermute | solution.py:341
  104.9 1.6 %fetch.1.x_ref = bf16[2048,512]{1,0:T(8,128)(2,1)S(1)} custom-call(bf16[2048,512]{1,0:T(8,128)(2,1)} %x_hbm.3), custom_call_target="tpu_custom_call" | custom-call | bytes 2097152 | tf_op jit(solution)/shard_map/fetch/pallas_call | solution.py:296
  106.5 4.2 %collective-permute-done.1 = f32[256,128]{1,0:T(8,128)S(1)} collective-permute-done((f32[256,128]{1,0:T(8,128)S(1)}, f32[256,128]{1,0:T(8,128)S(1)}, u32[]{:S(2)}, u32[]{:S(2)}) %collective-permute-start.1) | collective-permute-done | bytes 131104 | tf_op jit(solution)/shard_map/ppermute | solution.py:341
  110.8 0.1 collective-permute-start.2
  110.9 13.4 %all-to-all-done.1.got_ref.got_hbm = bf16[32,32,2048]{2,1,0:T(8,128)(2,1)} async-done(((bf16[32,32,2048]{2,1,0:T(8,128)(2,1)}), bf16[32,32,2048]{2,1,0:T(8,128)(2,1)}, u32[]{:S(2)}, u32[]{:S(2)}) %all-to-all-start.1) | async-done | bytes 4194336 | tf_op jit(solution)/shard_map/all_to_all | solution.py:336
  124.3 4.9 %late_grads.1 = bf16[8,128,128]{2,1,0:T(8,128)(2,1)} custom-call(bf16[32,32,2048]{2,1,0:T(8,128)(2,1)} %all-to-all-done.1.got_ref.got_hbm, bf16[2048,512]{1,0:T(8,128)(2,1)S(1)} %fetch.1.x_ref, bf16[2048,512]{1,0:T(8,128)(2,1)} %g_hbm.3), custom_call_target="tpu_custom_call" | custom-call | flops 2147483648 | bytes 8388608 | tf_op jit(solution)/shard_map/late_grads/pallas_call | solution.py:296
  129.2 9.2 %all-to-all-start.2 = ((bf16[8,128,128]{2,1,0:T(8,128)(2,1)}), bf16[8,128,128]{2,1,0:T(8,128)(2,1)S(1)}, u32[]{:S(2)}, u32[]{:S(2)}) async-start(bf16[8,128,128]{2,1,0:T(8,128)(2,1)} %late_grads.1), calls=%async_computation.2 | async-start | bytes 524288 | tf_op jit(solution)/shard_map/all_to_all | solution.py:336
  138.4 0.0 collective-permute-done.2
  138.4 0.6 slice_add_fusion.3
  139.1 6.6 %tail.1 = (bf16[2048,512]{1,0:T(8,128)(2,1)}, bf16[2048,512]{1,0:T(8,128)(2,1)}) custom-call(bf16[32,32,2048]{2,1,0:T(8,128)(2,1)} %all-to-all-done.1.got_ref.got_hbm, bf16[4,128,128]{2,1,0:T(8,128)(2,1)} %outer_hbm.6, bf16[4,128,128]{2,1,0:T(8,128)(2,1)} %inner_hbm.6), custom_call_target="tpu_custom_call" | custom-call | flops 2147483648 | bytes 4456448 | tf_op jit(solution)/shard_map/tail/pallas_call | solution.py:296
  145.7 0.4 all-to-all-done.2
  146.1 0.7 convert_reduce_fusion
  (2 shorter events, 0.0 us)
Async XLA Ops:
  66.8 57.5 %all-to-all-start.1 = ((bf16[32,32,2048]{2,1,0:T(8,128)(2,1)}), bf16[32,32,2048]{2,1,0:T(8,128)(2,1)}, u32[]{:S(2)}, u32[]{:S(2)}) async-start(bf16[32,32,2048]{2,1,0:T(8,128)(2,1)} %get-tuple-element.14), calls=%async_computation.1 | async-start | bytes 8388608 | tf_op jit(solution)/shard_map/all_to_all | solution.py:336
  73.9 2.2 %copy-start = (bf16[32,32,2048]{2,1,0:T(8,128)(2,1)S(1)}, bf16[32,32,2048]{2,1,0:T(8,128)(2,1)}, u32[]{:S(2)}) copy-start(bf16[32,32,2048]{2,1,0:T(8,128)(2,1)} %get-tuple-element.17.got_ref) | copy-start | bytes 12582916
  83.4 15.1 %collective-permute-start = (f32[512,128]{1,0:T(8,128)S(1)}, f32[512,128]{1,0:T(8,128)S(1)}, u32[]{:S(2)}, u32[]{:S(2)}) collective-permute-start(f32[512,128]{1,0:T(8,128)S(1)} %get-tuple-element.19), channel_id=1, source_target_pairs={{0,128},{32,160},{64,192},{96,224},{128,0},{160,32},{192,64},{224,... | collective-permute-start | bytes 786440 | tf_op jit(solution)/shard_map/ppermute | solution.py:341
  98.5 12.3 %collective-permute-start.1 = (f32[256,128]{1,0:T(8,128)S(1)}, f32[256,128]{1,0:T(8,128)S(1)}, u32[]{:S(2)}, u32[]{:S(2)}) collective-permute-start(f32[256,128]{1,0:T(8,128)S(1)} %slice_add_fusion), channel_id=1, source_target_pairs={{0,64},{32,96},{64,0},{96,32},{128,192},{160,224},{192,128},{224,1... | collective-permute-start | bytes 393224 | tf_op jit(solution)/shard_map/ppermute | solution.py:341
  110.8 27.6 %collective-permute-start.2 = (f32[128,128]{1,0:T(8,128)S(1)}, f32[128,128]{1,0:T(8,128)S(1)}, u32[]{:S(2)}, u32[]{:S(2)}) collective-permute-start(f32[128,128]{1,0:T(8,128)S(1)} %slice_add_fusion.1), channel_id=1, source_target_pairs={{0,32},{32,0},{64,96},{96,64},{128,160},{160,128},{192,224},{224,1... | collective-permute-start | bytes 196616 | tf_op jit(solution)/shard_map/ppermute | solution.py:341
  129.2 17.0 %all-to-all-start.2 = ((bf16[8,128,128]{2,1,0:T(8,128)(2,1)}), bf16[8,128,128]{2,1,0:T(8,128)(2,1)S(1)}, u32[]{:S(2)}, u32[]{:S(2)}) async-start(bf16[8,128,128]{2,1,0:T(8,128)(2,1)} %late_grads.1), calls=%async_computation.2 | async-start | bytes 524288 | tf_op jit(solution)/shard_map/all_to_all | solution.py:336

commit v8 on v7

--- a/solution.py
+++ b/solution.py
@@ -12,6 +12,7 @@
 HEAD_TILES = 1
 TILES = 4
 LATE_TILES = 4
+TAIL_TILES = 2
 ROWS = 64
 
 
@@ -269,26 +270,28 @@
 
 
 def tail_kernel(
-    got_ref, outer_hbm, inner_hbm, output_hbm, input_grad_hbm,
-    output_buf, input_grad_buf, outer_buf, inner_buf, outer_wide, inner_wide, weight_sems, output_sems, input_grad_sems,
+    got_hbm, outer_hbm, inner_hbm, output_hbm, input_grad_hbm,
+    got_buf, output_buf, input_grad_buf, outer_buf, inner_buf, outer_wide, inner_wide,
+    weight_sems, got_sems, output_sems, input_grad_sems,
 ):
-    tile = output_buf.shape[0] // TILES
-    finish(load([(outer_hbm, outer_buf), (inner_hbm, inner_buf)], weight_sems))
+    tile = output_buf.shape[0] // TAIL_TILES
+    weights = load([(outer_hbm, outer_buf), (inner_hbm, inner_buf)], weight_sems)
+    loads = copies(got_hbm, got_buf, got_sems, tile, 2)
+    begin(loads)
+    finish(weights)
     fill_outer(outer_buf, outer_wide)
     fill_inner_t(inner_buf, inner_wide)
-    stores = []
-    for part, wide, buf, out, sems in (
-        (0, outer_wide, output_buf, output_hbm, output_sems),
-        (1, inner_wide, input_grad_buf, input_grad_hbm, input_grad_sems),
-    ):
-        leaving = copies(buf, out, sems, tile, 0)
-        stores += leaving
-        for i in range(TILES):
-            lanes = slice(tile * i, tile * i + tile)
-            message = rows(got_ref[:, 16 * part:16 * part + 16, lanes])
-            buf[lanes, :] = dot(message, wide[...], 0, 0).astype(BF)
-            leaving[i].start()
-    finish(stores)
+    output_stores = copies(output_buf, output_hbm, output_sems, tile, 0)
+    input_grad_stores = copies(input_grad_buf, input_grad_hbm, input_grad_sems, tile, 0)
+    for i in range(TAIL_TILES):
+        lanes = slice(tile * i, tile * i + tile)
+        loads[i].wait()
+        output_buf[lanes, :] = dot(rows(got_buf[:, 0:16, lanes]), outer_wide[...], 0, 0).astype(BF)
+        output_stores[i].start()
+        input_grad_buf[lanes, :] = dot(rows(got_buf[:, 16:32, lanes]), inner_wide[...], 0, 0).astype(BF)
+        input_grad_stores[i].start()
+    finish(output_stores)
+    finish(input_grad_stores)
 
 
 def call(kernel, name, args, outs, specs, out_specs, scratch, flops):
@@ -330,6 +333,7 @@
     pair = pltpu.SemaphoreType.DMA((2,))
     sems = pltpu.SemaphoreType.DMA((TILES,))
     head_sems = pltpu.SemaphoreType.DMA((HEAD_TILES,))
+    tail_sems = pltpu.SemaphoreType.DMA((TAIL_TILES,))
     late_sems = pltpu.SemaphoreType.DMA((LATE_TILES,))
 
     def exchange(value, axis, order=None):
@@ -362,21 +366,24 @@
     tokens_here = call(
         fetch_kernel, "fetch", (tokens,), [by_token], [hbm], [vmem], [pltpu.SemaphoreType.DMA], 0
     )[0]
+    outer_one_sum = own[:64] + halves[:64] + quarters[:64] + eighth[:64]
+    inner_two_sum = own[64:] + halves[64:128] + quarters[64:128] + eighth[64:]
+    tokens_here, outer_one_sum, inner_two_sum = lax.optimization_barrier((tokens_here, outer_one_sum, inner_two_sum))
     late = call(
         late_kernel, "late_grads", (got_two, tokens_here, cotangent), [shape((8, 128, 128), BF)], [hbm, vmem, hbm], [vmem],
         [by_message, by_token, total, total, picked_part, block] + [late_sems] * 3, 2 * one,
     )[0]
     late = exchange(late, "dp", [[7 - rank for rank in range(8)]])
     output, input_grad = call(
-        tail_kernel, "tail", (got_two, outer_two, inner_one), [pltpu.HBM((tok, 512), BF)] * 2, [vmem, hbm, hbm], [hbm] * 2,
-        [by_token, by_token, weight, weight, wide, wide, pair, sems, sems], 2 * one,
+        tail_kernel, "tail", (got_two, outer_two, inner_one), [pltpu.HBM((tok, 512), BF)] * 2, [hbm] * 3, [hbm] * 2,
+        [by_message, by_token, by_token, weight, weight, wide, wide, pair] + [tail_sems] * 3, 2 * one,
     )
     return (
         output,
         input_grad,
         jnp.sum(late[:, 64:], axis=0, dtype=F32).reshape(4, 16, 128),
-        (own[:64] + halves[:64] + quarters[:64] + eighth[:64]).reshape(4, 16, 128),
-        (own[64:] + halves[64:128] + quarters[64:128] + eighth[64:]).reshape(4, 16, 128),
+        outer_one_sum.reshape(4, 16, 128),
+        inner_two_sum.reshape(4, 16, 128),
         jnp.sum(late[:, :64], axis=0, dtype=F32).reshape(4, 16, 128),
     )
 

time: 149 us -> 149 us (level)
    ppermute x3, waiting for transfers between devices: 12 us -> 16.2 us  [across(): return lax.ppermute(value, 'dp', [(rank, rank ^ flip) for rank in range(8)])]
    all_to_all x2, waiting for transfers between devices: 13.9 us -> 10.6 us  [exchange(): lax.all_to_all(value, axis, split_axis=0, concat_axis=0, tiled=True, axis...]
  transfers between devices with their start and end apart: 5 -> 5, of which waited for: 4 -> 5; matrix products, arithmetic and copies ran while one was open for 0% -> 0% of each run, Pallas kernels for 14% -> 10%
where the time goes in v8:
time: 149 us; the launch traced here: 147 us
  blocking collectives  56 us (38%)
  starting transfers between devices  30.2 us (20%)
  Pallas kernels  29.5 us (20%)
  waiting for transfers between devices  26.9 us (18%)
  local copies, waits for them, and re-layouts  2.18 us (1%)
    all_to_all x1, blocking collectives, exchange(): lax.all_to_all(value, axis, split_axis=0, concat_axis=0, tiled=True, axis...  56 us
    pallas_call x6, Pallas kernels, call(): pl.pallas_call(kernel, in_specs=specs, out_specs=out_specs, out_shape=out...  29.5 us
    all_to_all x2, starting transfers between devices, exchange(): lax.all_to_all(value, axis, split_axis=0, concat_axis=0, tiled=True, axis...  16.3 us
    ppermute x3, waiting for transfers between devices, across(): return lax.ppermute(value, 'dp', [(rank, rank ^ flip) for rank in range(8)])  16.2 us
    ppermute x3, starting transfers between devices, across(): return lax.ppermute(value, 'dp', [(rank, rank ^ flip) for rank in range(8)])  13.9 us
    all_to_all x2, waiting for transfers between devices, exchange(): lax.all_to_all(value, axis, split_axis=0, concat_axis=0, tiled=True, axis...  10.6 us
  transfers between devices with their start and end apart: 5, of which 5 were waited for; matrix products, arithmetic and copies ran while one was open for 0% of the time, Pallas kernels for 10%

profile of v8, /device:TPU:8, one launch (start us, length us, event | category | flops | bytes accessed | tf_op | source)
XLA Modules:
  0.0 146.8 jit_solution(2871573623540121108)
XLA Ops:
  0.6 3.3 %head.1 = bf16[32,32,2048]{2,1,0:T(8,128)(2,1)S(1)} custom-call(bf16[2048,512]{1,0:T(8,128)(2,1)} %x_hbm.3, bf16[2048,512]{1,0:T(8,128)(2,1)} %g_hbm.3, bf16[4,128,128]{2,1,0:T(8,128)(2,1)} %inner_hbm.6, bf16[4,128,128]{2,1,0:T(8,128)(2,1)} %outer_hbm.6), custom_call_target="tpu_custom_call" | custom-call | flops 2147483648 | bytes 4456448 | tf_op jit(solution)/shard_map/head/pallas_call | solution.py:299
  3.9 56.0 %all_to_all.15.got_ref = bf16[32,32,2048]{2,1,0:T(8,128)(2,1)S(1)} all-to-all(bf16[32,32,2048]{2,1,0:T(8,128)(2,1)S(1)} %head.1), channel_id=1, replica_groups=mesh['dp'=8,'mp'=32] {'mp'}, dimensions={0} | all-to-all | bytes 8388608 | tf_op jit(solution)/shard_map/all_to_all | solution.py:340
  59.9 6.8 %middle.1 = (bf16[32,32,2048]{2,1,0:T(8,128)(2,1)}, bf16[32,32,2048]{2,1,0:T(8,128)(2,1)}) custom-call(bf16[32,32,2048]{2,1,0:T(8,128)(2,1)S(1)} %all_to_all.15.got_ref, bf16[4,128,128]{2,1,0:T(8,128)(2,1)} %outer_hbm.7, bf16[4,128,128]{2,1,0:T(8,128)(2,1)} %inner_hbm.7), custom_call_target="tpu_custom_call" | custom-call | flops 4294967296 | bytes 4456448 | tf_op jit(solution)/shard_map/middle/pallas_call | solution.py:299
  66.8 7.1 %all-to-all-start.1 = ((bf16[32,32,2048]{2,1,0:T(8,128)(2,1)}), bf16[32,32,2048]{2,1,0:T(8,128)(2,1)}, u32[]{:S(2)}, u32[]{:S(2)}) async-start(bf16[32,32,2048]{2,1,0:T(8,128)(2,1)} %get-tuple-element.17), calls=%async_computation.1 | async-start | bytes 8388608 | tf_op jit(solution)/shard_map/all_to_all | solution.py:340
  73.9 0.0 copy-start
  73.9 2.2 %copy-done = bf16[32,32,2048]{2,1,0:T(8,128)(2,1)S(1)} copy-done((bf16[32,32,2048]{2,1,0:T(8,128)(2,1)S(1)}, bf16[32,32,2048]{2,1,0:T(8,128)(2,1)}, u32[]{:S(2)}) %copy-start) | copy-done | bytes 4194328
  76.1 7.3 %early_grads.1 = (f32[128,128]{1,0:T(8,128)S(1)}, f32[128,128]{1,0:T(8,128)S(1)}, f32[256,128]{1,0:T(8,128)S(1)}, f32[512,128]{1,0:T(8,128)S(1)}) custom-call(bf16[32,32,2048]{2,1,0:T(8,128)(2,1)S(1)} %copy-done, bf16[4,128,128]{2,1,0:T(8,128)(2,1)} %outer_hbm.7, bf16[4,128,128]{2,1,0:T(8,128)(2,1)} %inner_hbm.7, s32[1]{0:T(128)} %bitcast.mine_ref), custom_call_target="tpu_custom_call" | custom-call | flops 4294967296 | bytes 4456450 | tf_op jit(solution)/shard_map/early_grads/pallas_call | solution.py:299
  83.4 7.3 %collective-permute-start = (f32[512,128]{1,0:T(8,128)S(1)}, f32[512,128]{1,0:T(8,128)S(1)}, u32[]{:S(2)}, u32[]{:S(2)}) collective-permute-start(f32[512,128]{1,0:T(8,128)S(1)} %get-tuple-element.22), channel_id=1, source_target_pairs={{0,128},{32,160},{64,192},{96,224},{128,0},{160,32},{192,64},{224,... | collective-permute-start | bytes 786440 | tf_op jit(solution)/shard_map/ppermute | solution.py:345
  90.7 7.8 %collective-permute-done = f32[512,128]{1,0:T(8,128)S(1)} collective-permute-done((f32[512,128]{1,0:T(8,128)S(1)}, f32[512,128]{1,0:T(8,128)S(1)}, u32[]{:S(2)}, u32[]{:S(2)}) %collective-permute-start) | collective-permute-done | bytes 262176 | tf_op jit(solution)/shard_map/ppermute | solution.py:345
  98.5 6.5 %collective-permute-start.1 = (f32[256,128]{1,0:T(8,128)S(1)}, f32[256,128]{1,0:T(8,128)S(1)}, u32[]{:S(2)}, u32[]{:S(2)}) collective-permute-start(f32[256,128]{1,0:T(8,128)S(1)} %slice_add_fusion), channel_id=1, source_target_pairs={{0,64},{32,96},{64,0},{96,32},{128,192},{160,224},{192,128},{224,1... | collective-permute-start | bytes 393224 | tf_op jit(solution)/shard_map/ppermute | solution.py:345
  104.9 5.8 %collective-permute-done.1 = f32[256,128]{1,0:T(8,128)S(1)} collective-permute-done((f32[256,128]{1,0:T(8,128)S(1)}, f32[256,128]{1,0:T(8,128)S(1)}, u32[]{:S(2)}, u32[]{:S(2)}) %collective-permute-start.1) | collective-permute-done | bytes 131104 | tf_op jit(solution)/shard_map/ppermute | solution.py:345
  110.8 0.1 collective-permute-start.2
  110.9 1.6 %fetch.1.x_ref = bf16[2048,512]{1,0:T(8,128)(2,1)S(1)} custom-call(bf16[2048,512]{1,0:T(8,128)(2,1)} %x_hbm.3), custom_call_target="tpu_custom_call" | custom-call | bytes 2097152 | tf_op jit(solution)/shard_map/fetch/pallas_call | solution.py:299
  112.5 2.6 %collective-permute-done.2 = f32[128,128]{1,0:T(8,128)S(1)} collective-permute-done((f32[128,128]{1,0:T(8,128)S(1)}, f32[128,128]{1,0:T(8,128)S(1)}, u32[]{:S(2)}, u32[]{:S(2)}) %collective-permute-start.2) | collective-permute-done | bytes 65568 | tf_op jit(solution)/shard_map/ppermute | solution.py:345
  115.2 0.6 slice_add_fusion.3
  115.8 8.5 %all-to-all-done.1.got_hbm = bf16[32,32,2048]{2,1,0:T(8,128)(2,1)} async-done(((bf16[32,32,2048]{2,1,0:T(8,128)(2,1)}), bf16[32,32,2048]{2,1,0:T(8,128)(2,1)}, u32[]{:S(2)}, u32[]{:S(2)}) %all-to-all-start.1) | async-done | bytes 4194336 | tf_op jit(solution)/shard_map/all_to_all | solution.py:340
  124.3 4.9 %late_grads.1 = bf16[8,128,128]{2,1,0:T(8,128)(2,1)} custom-call(bf16[32,32,2048]{2,1,0:T(8,128)(2,1)} %all-to-all-done.1.got_hbm, bf16[2048,512]{1,0:T(8,128)(2,1)S(1)} %fetch.1.x_ref, bf16[2048,512]{1,0:T(8,128)(2,1)} %g_hbm.3), custom_call_target="tpu_custom_call" | custom-call | flops 2147483648 | bytes 8388608 | tf_op jit(solution)/shard_map/late_grads/pallas_call | solution.py:299
  129.2 9.2 %all-to-all-start.2 = ((bf16[8,128,128]{2,1,0:T(8,128)(2,1)}), bf16[8,128,128]{2,1,0:T(8,128)(2,1)S(1)}, u32[]{:S(2)}, u32[]{:S(2)}) async-start(bf16[8,128,128]{2,1,0:T(8,128)(2,1)} %late_grads.1), calls=%async_computation.2 | async-start | bytes 524288 | tf_op jit(solution)/shard_map/all_to_all | solution.py:340
  138.4 5.6 %tail.1 = (bf16[2048,512]{1,0:T(8,128)(2,1)}, bf16[2048,512]{1,0:T(8,128)(2,1)}) custom-call(bf16[32,32,2048]{2,1,0:T(8,128)(2,1)} %all-to-all-done.1.got_hbm, bf16[4,128,128]{2,1,0:T(8,128)(2,1)} %outer_hbm.6, bf16[4,128,128]{2,1,0:T(8,128)(2,1)} %inner_hbm.6), custom_call_target="tpu_custom_call" | custom-call | flops 2147483648 | bytes 4456448 | tf_op jit(solution)/shard_map/tail/pallas_call | solution.py:299
  144.1 2.1 %all-to-all-done.2 = bf16[8,128,128]{2,1,0:T(8,128)(2,1)S(1)} async-done(((bf16[8,128,128]{2,1,0:T(8,128)(2,1)}), bf16[8,128,128]{2,1,0:T(8,128)(2,1)S(1)}, u32[]{:S(2)}, u32[]{:S(2)}) %all-to-all-start.2) | async-done | bytes 262176 | tf_op jit(solution)/shard_map/all_to_all | solution.py:340
  146.1 0.7 convert_reduce_fusion
  (2 shorter events, 0.0 us)
Async XLA Ops:
  66.8 57.5 %all-to-all-start.1 = ((bf16[32,32,2048]{2,1,0:T(8,128)(2,1)}), bf16[32,32,2048]{2,1,0:T(8,128)(2,1)}, u32[]{:S(2)}, u32[]{:S(2)}) async-start(bf16[32,32,2048]{2,1,0:T(8,128)(2,1)} %get-tuple-element.17), calls=%async_computation.1 | async-start | bytes 8388608 | tf_op jit(solution)/shard_map/all_to_all | solution.py:340
  73.9 2.2 %copy-start = (bf16[32,32,2048]{2,1,0:T(8,128)(2,1)S(1)}, bf16[32,32,2048]{2,1,0:T(8,128)(2,1)}, u32[]{:S(2)}) copy-start(bf16[32,32,2048]{2,1,0:T(8,128)(2,1)} %get-tuple-element.20.got_ref) | copy-start | bytes 12582916
  83.4 15.1 %collective-permute-start = (f32[512,128]{1,0:T(8,128)S(1)}, f32[512,128]{1,0:T(8,128)S(1)}, u32[]{:S(2)}, u32[]{:S(2)}) collective-permute-start(f32[512,128]{1,0:T(8,128)S(1)} %get-tuple-element.22), channel_id=1, source_target_pairs={{0,128},{32,160},{64,192},{96,224},{128,0},{160,32},{192,64},{224,... | collective-permute-start | bytes 786440 | tf_op jit(solution)/shard_map/ppermute | solution.py:345
  98.5 12.3 %collective-permute-start.1 = (f32[256,128]{1,0:T(8,128)S(1)}, f32[256,128]{1,0:T(8,128)S(1)}, u32[]{:S(2)}, u32[]{:S(2)}) collective-permute-start(f32[256,128]{1,0:T(8,128)S(1)} %slice_add_fusion), channel_id=1, source_target_pairs={{0,64},{32,96},{64,0},{96,32},{128,192},{160,224},{192,128},{224,1... | collective-permute-start | bytes 393224 | tf_op jit(solution)/shard_map/ppermute | solution.py:345
  110.8 4.4 %collective-permute-start.2 = (f32[128,128]{1,0:T(8,128)S(1)}, f32[128,128]{1,0:T(8,128)S(1)}, u32[]{:S(2)}, u32[]{:S(2)}) collective-permute-start(f32[128,128]{1,0:T(8,128)S(1)} %slice_add_fusion.1), channel_id=1, source_target_pairs={{0,32},{32,0},{64,96},{96,64},{128,160},{160,128},{192,224},{224,1... | collective-permute-start | bytes 196616 | tf_op jit(solution)/shard_map/ppermute | solution.py:345
  129.2 17.0 %all-to-all-start.2 = ((bf16[8,128,128]{2,1,0:T(8,128)(2,1)}), bf16[8,128,128]{2,1,0:T(8,128)(2,1)S(1)}, u32[]{:S(2)}, u32[]{:S(2)}) async-start(bf16[8,128,128]{2,1,0:T(8,128)(2,1)} %late_grads.1), calls=%async_computation.2 | async-start | bytes 524288 | tf_op jit(solution)/shard_map/all_to_all | solution.py:340

commit v9 on v8

--- a/solution.py
+++ b/solution.py
@@ -145,13 +145,16 @@
 def middle_kernel(
     got_ref, outer_hbm, inner_hbm, sent_hbm, kept_hbm,
     outer_buf, inner_buf, sent_buf, pre_ref, grad_hidden_ref, hidden_ref, grad_pre_ref,
-    outer_wide_t, inner_wide, inner_pair, outer_pair, weight_sems, sent_sems, kept_sem,
+    outer_wide_t, inner_wide, inner_pair, outer_pair, weight_sems, first_sems, second_sems, kept_sem,
 ):
     tile = got_ref.shape[2] // TILES
     outer_copy, inner_copy = load([(outer_hbm, outer_buf), (inner_hbm, inner_buf)], weight_sems)
     kept_copy = pltpu.make_async_copy(got_ref, kept_hbm, kept_sem)
     kept_copy.start()
-    sent_stores = copies(sent_buf, sent_hbm, sent_sems, tile, 2)
+    first_stores, second_stores = (
+        copies(sent_buf.at[:, band, :], sent_hbm.at[:, band, :], sems, tile, 2)
+        for band, sems in ((pl.ds(0, 16), first_sems), (pl.ds(16, 16), second_sems))
+    )
     outer_copy.wait()
     fill_outer_t(outer_buf, outer_wide_t)
     fill_second(outer_buf, outer_pair)
@@ -171,9 +174,11 @@
             pre_act(i + 1)
         activate(pre_ref.at[i % 2], hidden_ref, grad_hidden_ref, grad_pre_ref)
         sent_buf[:, 0:16, lanes(i)] = paired(inner_pair, lambda at: hidden_ref[at, :], 0)
+        first_stores[i].start()
         sent_buf[:, 16:32, lanes(i)] = paired(outer_pair, lambda at: grad_pre_ref[at, :], 0)
-        sent_stores[i].start()
-    finish(sent_stores)
+        second_stores[i].start()
+    finish(first_stores)
+    finish(second_stores)
     kept_copy.wait()
 
 
@@ -351,7 +356,7 @@
     got = exchange(sent, "mp")
     sent_two, kept = call(
         middle_kernel, "middle", (got, outer_one, inner_two), [pltpu.HBM((32, 32, tok), BF)] * 2, [vmem, hbm, hbm], [hbm] * 2,
-        [weight, weight, by_message, pltpu.VMEM((2, 512, tok // TILES), F32), tile_f32, tile_bf, tile_bf, wide, wide, halves_of, halves_of, pair, sems, pltpu.SemaphoreType.DMA], 4 * one,
+        [weight, weight, by_message, pltpu.VMEM((2, 512, tok // TILES), F32), tile_f32, tile_bf, tile_bf, wide, wide, halves_of, halves_of, pair, sems, sems, pltpu.SemaphoreType.DMA], 4 * one,
     )
     got_two = exchange(sent_two, "mp")
     own, near, middle, far = call(

time: 149 us -> 149 us (level)
  no operation moved by 1% of the time
where the time goes in v9:
time: 149 us; the launch traced here: 148 us
  blocking collectives  56 us (38%)
  Pallas kernels  30.2 us (20%)
  starting transfers between devices  30.2 us (20%)
  waiting for transfers between devices  26.9 us (18%)
  local copies, waits for them, and re-layouts  2.18 us (1%)
    all_to_all x1, blocking collectives, exchange(): lax.all_to_all(value, axis, split_axis=0, concat_axis=0, tiled=True, axis...  56 us
    pallas_call x6, Pallas kernels, call(): pl.pallas_call(kernel, in_specs=specs, out_specs=out_specs, out_shape=out...  30.2 us
    all_to_all x2, starting transfers between devices, exchange(): lax.all_to_all(value, axis, split_axis=0, concat_axis=0, tiled=True, axis...  16.3 us
    ppermute x3, waiting for transfers between devices, across(): return lax.ppermute(value, 'dp', [(rank, rank ^ flip) for rank in range(8)])  16.2 us
    ppermute x3, starting transfers between devices, across(): return lax.ppermute(value, 'dp', [(rank, rank ^ flip) for rank in range(8)])  13.9 us
    all_to_all x2, waiting for transfers between devices, exchange(): lax.all_to_all(value, axis, split_axis=0, concat_axis=0, tiled=True, axis...  10.6 us
  transfers between devices with their start and end apart: 5, of which 5 were waited for; matrix products, arithmetic and copies ran while one was open for 0% of the time, Pallas kernels for 10%

profile of v9, /device:TPU:8, one launch (start us, length us, event | category | flops | bytes accessed | tf_op | source)
XLA Modules:
  0.0 147.5 jit_solution(13816708725662745156)
XLA Ops:
  0.6 3.3 %head.1 = bf16[32,32,2048]{2,1,0:T(8,128)(2,1)S(1)} custom-call(bf16[2048,512]{1,0:T(8,128)(2,1)} %x_hbm.3, bf16[2048,512]{1,0:T(8,128)(2,1)} %g_hbm.3, bf16[4,128,128]{2,1,0:T(8,128)(2,1)} %inner_hbm.6, bf16[4,128,128]{2,1,0:T(8,128)(2,1)} %outer_hbm.6), custom_call_target="tpu_custom_call" | custom-call | flops 2147483648 | bytes 4456448 | tf_op jit(solution)/shard_map/head/pallas_call | solution.py:304
  3.9 56.0 %all_to_all.15.got_ref = bf16[32,32,2048]{2,1,0:T(8,128)(2,1)S(1)} all-to-all(bf16[32,32,2048]{2,1,0:T(8,128)(2,1)S(1)} %head.1), channel_id=1, replica_groups=mesh['dp'=8,'mp'=32] {'mp'}, dimensions={0} | all-to-all | bytes 8388608 | tf_op jit(solution)/shard_map/all_to_all | solution.py:345
  59.9 7.6 %middle.1 = (bf16[32,32,2048]{2,1,0:T(8,128)(2,1)}, bf16[32,32,2048]{2,1,0:T(8,128)(2,1)}) custom-call(bf16[32,32,2048]{2,1,0:T(8,128)(2,1)S(1)} %all_to_all.15.got_ref, bf16[4,128,128]{2,1,0:T(8,128)(2,1)} %outer_hbm.7, bf16[4,128,128]{2,1,0:T(8,128)(2,1)} %inner_hbm.7), custom_call_target="tpu_custom_call" | custom-call | flops 4294967296 | bytes 4456448 | tf_op jit(solution)/shard_map/middle/pallas_call | solution.py:304
  67.5 7.1 %all-to-all-start.1 = ((bf16[32,32,2048]{2,1,0:T(8,128)(2,1)}), bf16[32,32,2048]{2,1,0:T(8,128)(2,1)}, u32[]{:S(2)}, u32[]{:S(2)}) async-start(bf16[32,32,2048]{2,1,0:T(8,128)(2,1)} %get-tuple-element.17), calls=%async_computation.1 | async-start | bytes 8388608 | tf_op jit(solution)/shard_map/all_to_all | solution.py:345
  74.6 0.0 copy-start
  74.6 2.2 %copy-done = bf16[32,32,2048]{2,1,0:T(8,128)(2,1)S(1)} copy-done((bf16[32,32,2048]{2,1,0:T(8,128)(2,1)S(1)}, bf16[32,32,2048]{2,1,0:T(8,128)(2,1)}, u32[]{:S(2)}) %copy-start) | copy-done | bytes 4194328
  76.8 7.3 %early_grads.1 = (f32[128,128]{1,0:T(8,128)S(1)}, f32[128,128]{1,0:T(8,128)S(1)}, f32[256,128]{1,0:T(8,128)S(1)}, f32[512,128]{1,0:T(8,128)S(1)}) custom-call(bf16[32,32,2048]{2,1,0:T(8,128)(2,1)S(1)} %copy-done, bf16[4,128,128]{2,1,0:T(8,128)(2,1)} %outer_hbm.7, bf16[4,128,128]{2,1,0:T(8,128)(2,1)} %inner_hbm.7, s32[1]{0:T(128)} %bitcast.mine_ref), custom_call_target="tpu_custom_call" | custom-call | flops 4294967296 | bytes 4456450 | tf_op jit(solution)/shard_map/early_grads/pallas_call | solution.py:304
  84.1 7.3 %collective-permute-start = (f32[512,128]{1,0:T(8,128)S(1)}, f32[512,128]{1,0:T(8,128)S(1)}, u32[]{:S(2)}, u32[]{:S(2)}) collective-permute-start(f32[512,128]{1,0:T(8,128)S(1)} %get-tuple-element.22), channel_id=1, source_target_pairs={{0,128},{32,160},{64,192},{96,224},{128,0},{160,32},{192,64},{224,... | collective-permute-start | bytes 786440 | tf_op jit(solution)/shard_map/ppermute | solution.py:350
  91.4 7.8 %collective-permute-done = f32[512,128]{1,0:T(8,128)S(1)} collective-permute-done((f32[512,128]{1,0:T(8,128)S(1)}, f32[512,128]{1,0:T(8,128)S(1)}, u32[]{:S(2)}, u32[]{:S(2)}) %collective-permute-start) | collective-permute-done | bytes 262176 | tf_op jit(solution)/shard_map/ppermute | solution.py:350
  99.1 6.5 %collective-permute-start.1 = (f32[256,128]{1,0:T(8,128)S(1)}, f32[256,128]{1,0:T(8,128)S(1)}, u32[]{:S(2)}, u32[]{:S(2)}) collective-permute-start(f32[256,128]{1,0:T(8,128)S(1)} %slice_add_fusion), channel_id=1, source_target_pairs={{0,64},{32,96},{64,0},{96,32},{128,192},{160,224},{192,128},{224,1... | collective-permute-start | bytes 393224 | tf_op jit(solution)/shard_map/ppermute | solution.py:350
  105.7 5.8 %collective-permute-done.1 = f32[256,128]{1,0:T(8,128)S(1)} collective-permute-done((f32[256,128]{1,0:T(8,128)S(1)}, f32[256,128]{1,0:T(8,128)S(1)}, u32[]{:S(2)}, u32[]{:S(2)}) %collective-permute-start.1) | collective-permute-done | bytes 131104 | tf_op jit(solution)/shard_map/ppermute | solution.py:350
  111.5 0.1 collective-permute-start.2
  111.6 1.6 %fetch.1.x_ref = bf16[2048,512]{1,0:T(8,128)(2,1)S(1)} custom-call(bf16[2048,512]{1,0:T(8,128)(2,1)} %x_hbm.3), custom_call_target="tpu_custom_call" | custom-call | bytes 2097152 | tf_op jit(solution)/shard_map/fetch/pallas_call | solution.py:304
  113.2 2.6 %collective-permute-done.2 = f32[128,128]{1,0:T(8,128)S(1)} collective-permute-done((f32[128,128]{1,0:T(8,128)S(1)}, f32[128,128]{1,0:T(8,128)S(1)}, u32[]{:S(2)}, u32[]{:S(2)}) %collective-permute-start.2) | collective-permute-done | bytes 65568 | tf_op jit(solution)/shard_map/ppermute | solution.py:350
  115.9 0.6 slice_add_fusion.3
  116.5 8.5 %all-to-all-done.1.got_hbm = bf16[32,32,2048]{2,1,0:T(8,128)(2,1)} async-done(((bf16[32,32,2048]{2,1,0:T(8,128)(2,1)}), bf16[32,32,2048]{2,1,0:T(8,128)(2,1)}, u32[]{:S(2)}, u32[]{:S(2)}) %all-to-all-start.1) | async-done | bytes 4194336 | tf_op jit(solution)/shard_map/all_to_all | solution.py:345
  125.0 4.9 %late_grads.1 = bf16[8,128,128]{2,1,0:T(8,128)(2,1)} custom-call(bf16[32,32,2048]{2,1,0:T(8,128)(2,1)} %all-to-all-done.1.got_hbm, bf16[2048,512]{1,0:T(8,128)(2,1)S(1)} %fetch.1.x_ref, bf16[2048,512]{1,0:T(8,128)(2,1)} %g_hbm.3), custom_call_target="tpu_custom_call" | custom-call | flops 2147483648 | bytes 8388608 | tf_op jit(solution)/shard_map/late_grads/pallas_call | solution.py:304
  129.9 9.2 %all-to-all-start.2 = ((bf16[8,128,128]{2,1,0:T(8,128)(2,1)}), bf16[8,128,128]{2,1,0:T(8,128)(2,1)S(1)}, u32[]{:S(2)}, u32[]{:S(2)}) async-start(bf16[8,128,128]{2,1,0:T(8,128)(2,1)} %late_grads.1), calls=%async_computation.2 | async-start | bytes 524288 | tf_op jit(solution)/shard_map/all_to_all | solution.py:345
  139.1 5.6 %tail.1 = (bf16[2048,512]{1,0:T(8,128)(2,1)}, bf16[2048,512]{1,0:T(8,128)(2,1)}) custom-call(bf16[32,32,2048]{2,1,0:T(8,128)(2,1)} %all-to-all-done.1.got_hbm, bf16[4,128,128]{2,1,0:T(8,128)(2,1)} %outer_hbm.6, bf16[4,128,128]{2,1,0:T(8,128)(2,1)} %inner_hbm.6), custom_call_target="tpu_custom_call" | custom-call | flops 2147483648 | bytes 4456448 | tf_op jit(solution)/shard_map/tail/pallas_call | solution.py:304
  144.8 2.1 %all-to-all-done.2 = bf16[8,128,128]{2,1,0:T(8,128)(2,1)S(1)} async-done(((bf16[8,128,128]{2,1,0:T(8,128)(2,1)}), bf16[8,128,128]{2,1,0:T(8,128)(2,1)S(1)}, u32[]{:S(2)}, u32[]{:S(2)}) %all-to-all-start.2) | async-done | bytes 262176 | tf_op jit(solution)/shard_map/all_to_all | solution.py:345
  146.9 0.7 convert_reduce_fusion
  (2 shorter events, 0.0 us)
Async XLA Ops:
  67.5 57.5 %all-to-all-start.1 = ((bf16[32,32,2048]{2,1,0:T(8,128)(2,1)}), bf16[32,32,2048]{2,1,0:T(8,128)(2,1)}, u32[]{:S(2)}, u32[]{:S(2)}) async-start(bf16[32,32,2048]{2,1,0:T(8,128)(2,1)} %get-tuple-element.17), calls=%async_computation.1 | async-start | bytes 8388608 | tf_op jit(solution)/shard_map/all_to_all | solution.py:345
  74.6 2.2 %copy-start = (bf16[32,32,2048]{2,1,0:T(8,128)(2,1)S(1)}, bf16[32,32,2048]{2,1,0:T(8,128)(2,1)}, u32[]{:S(2)}) copy-start(bf16[32,32,2048]{2,1,0:T(8,128)(2,1)} %get-tuple-element.20.got_ref) | copy-start | bytes 12582916
  84.1 15.0 %collective-permute-start = (f32[512,128]{1,0:T(8,128)S(1)}, f32[512,128]{1,0:T(8,128)S(1)}, u32[]{:S(2)}, u32[]{:S(2)}) collective-permute-start(f32[512,128]{1,0:T(8,128)S(1)} %get-tuple-element.22), channel_id=1, source_target_pairs={{0,128},{32,160},{64,192},{96,224},{128,0},{160,32},{192,64},{224,... | collective-permute-start | bytes 786440 | tf_op jit(solution)/shard_map/ppermute | solution.py:350
  99.1 12.4 %collective-permute-start.1 = (f32[256,128]{1,0:T(8,128)S(1)}, f32[256,128]{1,0:T(8,128)S(1)}, u32[]{:S(2)}, u32[]{:S(2)}) collective-permute-start(f32[256,128]{1,0:T(8,128)S(1)} %slice_add_fusion), channel_id=1, source_target_pairs={{0,64},{32,96},{64,0},{96,32},{128,192},{160,224},{192,128},{224,1... | collective-permute-start | bytes 393224 | tf_op jit(solution)/shard_map/ppermute | solution.py:350
  111.5 4.4 %collective-permute-start.2 = (f32[128,128]{1,0:T(8,128)S(1)}, f32[128,128]{1,0:T(8,128)S(1)}, u32[]{:S(2)}, u32[]{:S(2)}) collective-permute-start(f32[128,128]{1,0:T(8,128)S(1)} %slice_add_fusion.1), channel_id=1, source_target_pairs={{0,32},{32,0},{64,96},{96,64},{128,160},{160,128},{192,224},{224,1... | collective-permute-start | bytes 196616 | tf_op jit(solution)/shard_map/ppermute | solution.py:350
  129.9 17.0 %all-to-all-start.2 = ((bf16[8,128,128]{2,1,0:T(8,128)(2,1)}), bf16[8,128,128]{2,1,0:T(8,128)(2,1)S(1)}, u32[]{:S(2)}, u32[]{:S(2)}) async-start(bf16[8,128,128]{2,1,0:T(8,128)(2,1)} %late_grads.1), calls=%async_computation.2 | async-start | bytes 524288 | tf_op jit(solution)/shard_map/all_to_all | solution.py:345

commit v10 on v8

--- a/solution.py
+++ b/solution.py
@@ -11,7 +11,7 @@
 GELU_CUBE = 0.044715
 HEAD_TILES = 1
 TILES = 4
-LATE_TILES = 4
+LATE_TILES = 2
 TAIL_TILES = 2
 ROWS = 64
 

time: 149 us -> 148 us (level)
  no operation moved by 1% of the time
where the time goes in v10:
time: 148 us; the launch traced here: 147 us
  blocking collectives  56 us (38%)
  starting transfers between devices  30.2 us (20%)
  Pallas kernels  29.4 us (20%)
  waiting for transfers between devices  26.9 us (18%)
  local copies, waits for them, and re-layouts  2.18 us (1%)
    all_to_all x1, blocking collectives, exchange(): lax.all_to_all(value, axis, split_axis=0, concat_axis=0, tiled=True, axis...  56 us
    pallas_call x6, Pallas kernels, call(): pl.pallas_call(kernel, in_specs=specs, out_specs=out_specs, out_shape=out...  29.4 us
    all_to_all x2, starting transfers between devices, exchange(): lax.all_to_all(value, axis, split_axis=0, concat_axis=0, tiled=True, axis...  16.3 us
    ppermute x3, waiting for transfers between devices, across(): return lax.ppermute(value, 'dp', [(rank, rank ^ flip) for rank in range(8)])  16.2 us
    ppermute x3, starting transfers between devices, across(): return lax.ppermute(value, 'dp', [(rank, rank ^ flip) for rank in range(8)])  13.9 us
    all_to_all x2, waiting for transfers between devices, exchange(): lax.all_to_all(value, axis, split_axis=0, concat_axis=0, tiled=True, axis...  10.6 us
  transfers between devices with their start and end apart: 5, of which 5 were waited for; matrix products, arithmetic and copies ran while one was open for 0% of the time, Pallas kernels for 10%

profile of v10, /device:TPU:8, one launch (start us, length us, event | category | flops | bytes accessed | tf_op | source)
XLA Modules:
  0.0 146.7 jit_solution(4796532245719019508)
XLA Ops:
  0.6 3.3 %head.1 = bf16[32,32,2048]{2,1,0:T(8,128)(2,1)S(1)} custom-call(bf16[2048,512]{1,0:T(8,128)(2,1)} %x_hbm.3, bf16[2048,512]{1,0:T(8,128)(2,1)} %g_hbm.3, bf16[4,128,128]{2,1,0:T(8,128)(2,1)} %inner_hbm.6, bf16[4,128,128]{2,1,0:T(8,128)(2,1)} %outer_hbm.6), custom_call_target="tpu_custom_call" | custom-call | flops 2147483648 | bytes 4456448 | tf_op jit(solution)/shard_map/head/pallas_call | solution.py:299
  3.9 56.0 %all_to_all.15.got_ref = bf16[32,32,2048]{2,1,0:T(8,128)(2,1)S(1)} all-to-all(bf16[32,32,2048]{2,1,0:T(8,128)(2,1)S(1)} %head.1), channel_id=1, replica_groups=mesh['dp'=8,'mp'=32] {'mp'}, dimensions={0} | all-to-all | bytes 8388608 | tf_op jit(solution)/shard_map/all_to_all | solution.py:340
  59.9 6.8 %middle.1 = (bf16[32,32,2048]{2,1,0:T(8,128)(2,1)}, bf16[32,32,2048]{2,1,0:T(8,128)(2,1)}) custom-call(bf16[32,32,2048]{2,1,0:T(8,128)(2,1)S(1)} %all_to_all.15.got_ref, bf16[4,128,128]{2,1,0:T(8,128)(2,1)} %outer_hbm.7, bf16[4,128,128]{2,1,0:T(8,128)(2,1)} %inner_hbm.7), custom_call_target="tpu_custom_call" | custom-call | flops 4294967296 | bytes 4456448 | tf_op jit(solution)/shard_map/middle/pallas_call | solution.py:299
  66.8 7.1 %all-to-all-start.1 = ((bf16[32,32,2048]{2,1,0:T(8,128)(2,1)}), bf16[32,32,2048]{2,1,0:T(8,128)(2,1)}, u32[]{:S(2)}, u32[]{:S(2)}) async-start(bf16[32,32,2048]{2,1,0:T(8,128)(2,1)} %get-tuple-element.17), calls=%async_computation.1 | async-start | bytes 8388608 | tf_op jit(solution)/shard_map/all_to_all | solution.py:340
  73.9 0.0 copy-start
  73.9 2.2 %copy-done = bf16[32,32,2048]{2,1,0:T(8,128)(2,1)S(1)} copy-done((bf16[32,32,2048]{2,1,0:T(8,128)(2,1)S(1)}, bf16[32,32,2048]{2,1,0:T(8,128)(2,1)}, u32[]{:S(2)}) %copy-start) | copy-done | bytes 4194328
  76.1 7.3 %early_grads.1 = (f32[128,128]{1,0:T(8,128)S(1)}, f32[128,128]{1,0:T(8,128)S(1)}, f32[256,128]{1,0:T(8,128)S(1)}, f32[512,128]{1,0:T(8,128)S(1)}) custom-call(bf16[32,32,2048]{2,1,0:T(8,128)(2,1)S(1)} %copy-done, bf16[4,128,128]{2,1,0:T(8,128)(2,1)} %outer_hbm.7, bf16[4,128,128]{2,1,0:T(8,128)(2,1)} %inner_hbm.7, s32[1]{0:T(128)} %bitcast.mine_ref), custom_call_target="tpu_custom_call" | custom-call | flops 4294967296 | bytes 4456450 | tf_op jit(solution)/shard_map/early_grads/pallas_call | solution.py:299
  83.4 7.3 %collective-permute-start = (f32[512,128]{1,0:T(8,128)S(1)}, f32[512,128]{1,0:T(8,128)S(1)}, u32[]{:S(2)}, u32[]{:S(2)}) collective-permute-start(f32[512,128]{1,0:T(8,128)S(1)} %get-tuple-element.22), channel_id=1, source_target_pairs={{0,128},{32,160},{64,192},{96,224},{128,0},{160,32},{192,64},{224,... | collective-permute-start | bytes 786440 | tf_op jit(solution)/shard_map/ppermute | solution.py:345
  90.7 7.8 %collective-permute-done = f32[512,128]{1,0:T(8,128)S(1)} collective-permute-done((f32[512,128]{1,0:T(8,128)S(1)}, f32[512,128]{1,0:T(8,128)S(1)}, u32[]{:S(2)}, u32[]{:S(2)}) %collective-permute-start) | collective-permute-done | bytes 262176 | tf_op jit(solution)/shard_map/ppermute | solution.py:345
  98.5 6.5 %collective-permute-start.1 = (f32[256,128]{1,0:T(8,128)S(1)}, f32[256,128]{1,0:T(8,128)S(1)}, u32[]{:S(2)}, u32[]{:S(2)}) collective-permute-start(f32[256,128]{1,0:T(8,128)S(1)} %slice_add_fusion), channel_id=1, source_target_pairs={{0,64},{32,96},{64,0},{96,32},{128,192},{160,224},{192,128},{224,1... | collective-permute-start | bytes 393224 | tf_op jit(solution)/shard_map/ppermute | solution.py:345
  104.9 5.8 %collective-permute-done.1 = f32[256,128]{1,0:T(8,128)S(1)} collective-permute-done((f32[256,128]{1,0:T(8,128)S(1)}, f32[256,128]{1,0:T(8,128)S(1)}, u32[]{:S(2)}, u32[]{:S(2)}) %collective-permute-start.1) | collective-permute-done | bytes 131104 | tf_op jit(solution)/shard_map/ppermute | solution.py:345
  110.8 0.1 collective-permute-start.2
  110.9 1.6 %fetch.1.x_ref = bf16[2048,512]{1,0:T(8,128)(2,1)S(1)} custom-call(bf16[2048,512]{1,0:T(8,128)(2,1)} %x_hbm.3), custom_call_target="tpu_custom_call" | custom-call | bytes 2097152 | tf_op jit(solution)/shard_map/fetch/pallas_call | solution.py:299
  112.5 2.6 %collective-permute-done.2 = f32[128,128]{1,0:T(8,128)S(1)} collective-permute-done((f32[128,128]{1,0:T(8,128)S(1)}, f32[128,128]{1,0:T(8,128)S(1)}, u32[]{:S(2)}, u32[]{:S(2)}) %collective-permute-start.2) | collective-permute-done | bytes 65568 | tf_op jit(solution)/shard_map/ppermute | solution.py:345
  115.2 0.6 slice_add_fusion.3
  115.8 8.5 %all-to-all-done.1.got_hbm = bf16[32,32,2048]{2,1,0:T(8,128)(2,1)} async-done(((bf16[32,32,2048]{2,1,0:T(8,128)(2,1)}), bf16[32,32,2048]{2,1,0:T(8,128)(2,1)}, u32[]{:S(2)}, u32[]{:S(2)}) %all-to-all-start.1) | async-done | bytes 4194336 | tf_op jit(solution)/shard_map/all_to_all | solution.py:340
  124.3 4.8 %late_grads.1 = bf16[8,128,128]{2,1,0:T(8,128)(2,1)} custom-call(bf16[32,32,2048]{2,1,0:T(8,128)(2,1)} %all-to-all-done.1.got_hbm, bf16[2048,512]{1,0:T(8,128)(2,1)S(1)} %fetch.1.x_ref, bf16[2048,512]{1,0:T(8,128)(2,1)} %g_hbm.3), custom_call_target="tpu_custom_call" | custom-call | flops 2147483648 | bytes 8388608 | tf_op jit(solution)/shard_map/late_grads/pallas_call | solution.py:299
  129.1 9.2 %all-to-all-start.2 = ((bf16[8,128,128]{2,1,0:T(8,128)(2,1)}), bf16[8,128,128]{2,1,0:T(8,128)(2,1)S(1)}, u32[]{:S(2)}, u32[]{:S(2)}) async-start(bf16[8,128,128]{2,1,0:T(8,128)(2,1)} %late_grads.1), calls=%async_computation.2 | async-start | bytes 524288 | tf_op jit(solution)/shard_map/all_to_all | solution.py:340
  138.3 5.6 %tail.1 = (bf16[2048,512]{1,0:T(8,128)(2,1)}, bf16[2048,512]{1,0:T(8,128)(2,1)}) custom-call(bf16[32,32,2048]{2,1,0:T(8,128)(2,1)} %all-to-all-done.1.got_hbm, bf16[4,128,128]{2,1,0:T(8,128)(2,1)} %outer_hbm.6, bf16[4,128,128]{2,1,0:T(8,128)(2,1)} %inner_hbm.6), custom_call_target="tpu_custom_call" | custom-call | flops 2147483648 | bytes 4456448 | tf_op jit(solution)/shard_map/tail/pallas_call | solution.py:299
  144.0 2.1 %all-to-all-done.2 = bf16[8,128,128]{2,1,0:T(8,128)(2,1)S(1)} async-done(((bf16[8,128,128]{2,1,0:T(8,128)(2,1)}), bf16[8,128,128]{2,1,0:T(8,128)(2,1)S(1)}, u32[]{:S(2)}, u32[]{:S(2)}) %all-to-all-start.2) | async-done | bytes 262176 | tf_op jit(solution)/shard_map/all_to_all | solution.py:340
  146.1 0.7 convert_reduce_fusion
  (2 shorter events, 0.0 us)
Async XLA Ops:
  66.8 57.5 %all-to-all-start.1 = ((bf16[32,32,2048]{2,1,0:T(8,128)(2,1)}), bf16[32,32,2048]{2,1,0:T(8,128)(2,1)}, u32[]{:S(2)}, u32[]{:S(2)}) async-start(bf16[32,32,2048]{2,1,0:T(8,128)(2,1)} %get-tuple-element.17), calls=%async_computation.1 | async-start | bytes 8388608 | tf_op jit(solution)/shard_map/all_to_all | solution.py:340
  73.9 2.2 %copy-start = (bf16[32,32,2048]{2,1,0:T(8,128)(2,1)S(1)}, bf16[32,32,2048]{2,1,0:T(8,128)(2,1)}, u32[]{:S(2)}) copy-start(bf16[32,32,2048]{2,1,0:T(8,128)(2,1)} %get-tuple-element.20.got_ref) | copy-start | bytes 12582916
  83.4 15.1 %collective-permute-start = (f32[512,128]{1,0:T(8,128)S(1)}, f32[512,128]{1,0:T(8,128)S(1)}, u32[]{:S(2)}, u32[]{:S(2)}) collective-permute-start(f32[512,128]{1,0:T(8,128)S(1)} %get-tuple-element.22), channel_id=1, source_target_pairs={{0,128},{32,160},{64,192},{96,224},{128,0},{160,32},{192,64},{224,... | collective-permute-start | bytes 786440 | tf_op jit(solution)/shard_map/ppermute | solution.py:345
  98.5 12.3 %collective-permute-start.1 = (f32[256,128]{1,0:T(8,128)S(1)}, f32[256,128]{1,0:T(8,128)S(1)}, u32[]{:S(2)}, u32[]{:S(2)}) collective-permute-start(f32[256,128]{1,0:T(8,128)S(1)} %slice_add_fusion), channel_id=1, source_target_pairs={{0,64},{32,96},{64,0},{96,32},{128,192},{160,224},{192,128},{224,1... | collective-permute-start | bytes 393224 | tf_op jit(solution)/shard_map/ppermute | solution.py:345
  110.8 4.4 %collective-permute-start.2 = (f32[128,128]{1,0:T(8,128)S(1)}, f32[128,128]{1,0:T(8,128)S(1)}, u32[]{:S(2)}, u32[]{:S(2)}) collective-permute-start(f32[128,128]{1,0:T(8,128)S(1)} %slice_add_fusion.1), channel_id=1, source_target_pairs={{0,32},{32,0},{64,96},{96,64},{128,160},{160,128},{192,224},{224,1... | collective-permute-start | bytes 196616 | tf_op jit(solution)/shard_map/ppermute | solution.py:345
  129.1 17.0 %all-to-all-start.2 = ((bf16[8,128,128]{2,1,0:T(8,128)(2,1)}), bf16[8,128,128]{2,1,0:T(8,128)(2,1)S(1)}, u32[]{:S(2)}, u32[]{:S(2)}) async-start(bf16[8,128,128]{2,1,0:T(8,128)(2,1)} %late_grads.1), calls=%async_computation.2 | async-start | bytes 524288 | tf_op jit(solution)/shard_map/all_to_all | solution.py:340
